TPU v7x, 512 devices: a whole 4x8x8 slice. The times are simulated.
512 devices in a mesh: dp: 8 (over z), context: 16 (over y, core), tensor: 4 (over x).
Axes of the slice: x: 4, y: 8, z: 8, core: 2. Of those that a mesh axis runs over, the one named last changes fastest.
Arguments:
- layer_input: bfloat16 [8, 8192, 4096], P('dp', 'context', 'tensor'), may hold values from -6 to 6
- queries: bfloat16 [8, 16, 8192, 128], P('dp', 'tensor', 'context'), may hold values from -6 to 6
- key_states: bfloat16 [8, 4, 8192, 128], P('dp', 'tensor', 'context'), may hold values from -6 to 6
- value_states: bfloat16 [8, 4, 8192, 128], P('dp', 'tensor', 'context'), may hold values from -6 to 6
- out_grad: bfloat16 [8, 16, 8192, 128], P('dp', 'tensor', 'context'), may hold values from -0.0234375 to 0.0234375
- log_sums: bfloat16 [8, 16, 8192], P('dp', 'tensor', 'context'), may hold values from 2 to 5
- grad_dots: bfloat16 [8, 16, 8192], P('dp', 'tensor', 'context'), may hold values from -0.1875 to 0.1875
- doc_stretches: int32 [8, 10], P('dp'), may hold values from 1 to 8, as said below
- stretch_order: int32 [8, 256], P('dp'), may hold values from 0 to 255, as said below
- sign_vector: int32 [32, 128], P('context'), may hold values from -1 to 1, as said below
- exponents: int32 [8, 32], P('dp', 'context'), may hold values from 0 to 3
Outputs:
- rotated_grad: float32 [32, 128, 1024], P('context', 'dp', 'tensor')
Inputs may be any that keep to these rules, and one draw needn't show every extreme that they name: `doc_stretches`: each row gives the lengths in units of 128 tokens of 10 documents; they sum to 64. The second document is one of the longest, exactly 8 units, and begins 512 - 128 tokens after a multiple of 512 tokens. `stretch_order`: each row is a permutation of the 256 sequence blocks. Sequence blocks d * 16 to d * 16 + 15 belong to index d of context; the 16 stored blocks of one index of context hold at most 1 block belonging to any one index. `sign_vector`: every entry is 1 or -1.
All inputs are finite; a program needn't handle non-finite values.
Results may differ from a plain program's by a relative error of at most 0.0075.
Values may be sent and summed in bfloat16 or wider, within the bound.
No kernel may reach another device: no remote copies, remote signals or barrier semaphores. Data moves between devices by JAX's collectives and lax.ppermute only.
A program may use at most 64 MiB of HBM per device.

v0:
```python
import math

import jax
import jax.numpy as jnp
from jax import lax
from jax.sharding import PartitionSpec as P

HD = 128
GROUP = 4
BLK = 32
PAD = 128
HB = 128


def passed_along(block, axis, distance):
    devices = range(lax.axis_size(axis))
    route = [(i - distance, i) for i in devices if i - distance in devices]
    return lax.ppermute(block, axis, route)


def hadamard_table(table_size):
    index_row = jnp.arange(table_size, dtype=jnp.int32)
    common = jnp.bitwise_and(index_row[:, None], index_row[None, :])
    parity = jnp.zeros((table_size, table_size), jnp.int32)
    for bit_pos in range(table_size.bit_length() - 1):
        parity = parity + jnp.bitwise_and(jnp.right_shift(common, bit_pos), 1)
    signed = 1 - 2 * jnp.bitwise_and(parity, 1)
    return signed.astype(jnp.float32) * float(table_size) ** (-0.5)


def doc_of(position, ends_row):
    return jnp.sum(((position // PAD)[:, None] >= ends_row[None, :]).astype(jnp.int32), axis=1)


def live_pairs(query_pos, query_doc, key_pos, key_doc):
    return (query_doc[:, None] == key_doc[None, :]) & (key_pos[None, :] <= query_pos[:, None])


def block_grads(query_blk, grad_blk, lse_blk, dots_blk, key_blk, value_blk, live):
    scale = HD ** (-0.5)
    scores = (
        jnp.einsum("ghqd,gkd->ghqk", query_blk, key_blk, preferred_element_type=jnp.float32) * scale
    )
    probs = jnp.where(
        live[None, None], jnp.exp(scores - lse_blk.astype(jnp.float32)[..., None]), 0.0
    )
    value_part = jnp.einsum(
        "ghqk,ghqd->gkd", probs.astype(jnp.bfloat16), grad_blk, preferred_element_type=jnp.float32
    )
    dprobs = jnp.einsum("ghqd,gkd->ghqk", grad_blk, value_blk, preferred_element_type=jnp.float32)
    dscores = (probs * (dprobs - dots_blk.astype(jnp.float32)[..., None])).astype(jnp.bfloat16)
    key_part = (
        jnp.einsum("ghqk,ghqd->gkd", dscores, query_blk, preferred_element_type=jnp.float32) * scale
    )
    return (key_part, value_part)


def per_device(
    layer_input,
    queries,
    key_states,
    value_states,
    out_grad,
    log_sums,
    grad_dots,
    doc_stretches,
    stretch_order,
    sign_vector,
    exponents,
):
    local_tokens = queries.shape[2]
    local_kv = key_states.shape[1]
    local_cols = 2 * local_kv * HD
    order_row = stretch_order[0]
    ends_row = jnp.cumsum(doc_stretches[0])
    groups = lax.axis_size("context")
    slot_count = local_tokens // BLK
    capacity = max(1, slot_count // groups)
    device_id = lax.axis_index("context")
    order_grid = order_row.reshape(groups, slot_count)
    own_order = lax.dynamic_slice_in_dim(order_row, device_id * slot_count, slot_count, 0)
    own_target = own_order // slot_count
    slot_ids = jnp.arange(slot_count, dtype=jnp.int32)
    earlier = slot_ids[None, :] < slot_ids[:, None]
    send_rank = jnp.sum(
        jnp.where(earlier & (own_target[None, :] == own_target[:, None]), 1, 0), axis=1
    )
    send_row = own_target * capacity + send_rank
    buffer_ids = jnp.arange(groups * capacity, dtype=jnp.int32)
    send_table = (buffer_ids[:, None] == send_row[None, :]).astype(jnp.bfloat16)
    wanted = device_id * slot_count + slot_ids
    stretch_ids = jnp.arange(order_row.shape[0], dtype=jnp.int32)
    stored_at = jnp.sum(
        jnp.where(order_row[None, :] == wanted[:, None], stretch_ids[None, :], 0), axis=1
    )
    source = stored_at // slot_count
    source_slot = stored_at % slot_count
    source_orders = jnp.take(order_grid, source, axis=0)
    same_target = source_orders // slot_count == device_id
    recv_rank = jnp.sum(
        jnp.where(same_target & (slot_ids[None, :] < source_slot[:, None]), 1, 0), axis=1
    )
    recv_row = source * capacity + recv_rank
    recv_table = (recv_row[:, None] == buffer_ids[None, :]).astype(jnp.bfloat16)

    def pack(array):
        blocks = array[0].reshape(array.shape[1], slot_count, -1)
        return jnp.einsum(
            "rt,htx->rhx", send_table, blocks, preferred_element_type=jnp.float32
        ).astype(jnp.bfloat16)

    def unpack(packed):
        placed = jnp.einsum(
            "sr,rhx->hsx", recv_table, packed, preferred_element_type=jnp.float32
        ).astype(jnp.bfloat16)
        return placed.reshape(packed.shape[1], local_tokens, -1)

    moved = (
        lax.all_to_all(pack(queries), "context", split_axis=0, concat_axis=0, tiled=True),
        lax.all_to_all(pack(out_grad), "context", split_axis=0, concat_axis=0, tiled=True),
        lax.all_to_all(pack(key_states), "context", split_axis=0, concat_axis=0, tiled=True),
        lax.all_to_all(pack(value_states), "context", split_axis=0, concat_axis=0, tiled=True),
        lax.all_to_all(pack(log_sums), "context", split_axis=0, concat_axis=0, tiled=True),
        lax.all_to_all(pack(grad_dots), "context", split_axis=0, concat_axis=0, tiled=True),
    )
    query_sorted = unpack(moved[0])
    grad_sorted = unpack(moved[1])
    key_sorted = unpack(moved[2])
    value_sorted = unpack(moved[3])
    lse_sorted = unpack(moved[4])[:, :, 0]
    dots_sorted = unpack(moved[5])[:, :, 0]
    total_len = local_tokens * groups
    longest_tokens = max(total_len // PAD // 8, local_tokens // PAD) * PAD
    reach = (local_tokens - PAD + longest_tokens - 1) // local_tokens
    query_list = [query_sorted]
    grad_list = [grad_sorted]
    lse_list = [lse_sorted]
    dots_list = [dots_sorted]
    for ahead in range(1, reach + 1):
        later = passed_along(
            (query_sorted, grad_sorted, lse_sorted, dots_sorted), "context", -ahead
        )
        query_list.append(later[0])
        grad_list.append(later[1])
        lse_list.append(later[2])
        dots_list.append(later[3])
    all_query = jnp.concatenate(query_list, axis=1)
    all_grad = jnp.concatenate(grad_list, axis=1)
    all_lse = jnp.concatenate(lse_list, axis=1)
    all_dots = jnp.concatenate(dots_list, axis=1)
    total_rows = all_query.shape[1]
    query_pos_all = device_id * local_tokens + jnp.arange(total_rows, dtype=jnp.int32)
    query_doc_all = doc_of(query_pos_all, ends_row)
    key_pos_own = device_id * local_tokens + jnp.arange(local_tokens, dtype=jnp.int32)
    key_doc_own = doc_of(key_pos_own, ends_row)
    step_len = math.gcd(total_rows, 640)

    def ahead_block(index_val, running):
        offset = index_val * step_len
        query_blk = lax.dynamic_slice_in_dim(all_query, offset, step_len, 1).reshape(
            local_kv, GROUP, step_len, HD
        )
        grad_blk = lax.dynamic_slice_in_dim(all_grad, offset, step_len, 1).reshape(
            local_kv, GROUP, step_len, HD
        )
        lse_blk = lax.dynamic_slice_in_dim(all_lse, offset, step_len, 1).reshape(
            local_kv, GROUP, step_len
        )
        dots_blk = lax.dynamic_slice_in_dim(all_dots, offset, step_len, 1).reshape(
            local_kv, GROUP, step_len
        )
        query_pos = lax.dynamic_slice_in_dim(query_pos_all, offset, step_len, 0)
        query_doc = lax.dynamic_slice_in_dim(query_doc_all, offset, step_len, 0)
        live = live_pairs(query_pos, query_doc, key_pos_own, key_doc_own)
        key_part, value_part = block_grads(
            query_blk, grad_blk, lse_blk, dots_blk, key_sorted, value_sorted, live
        )
        return (running[0] + key_part, running[1] + value_part)

    empty = jnp.zeros((local_kv, local_tokens, HD), jnp.float32)
    key_total, value_total = lax.fori_loop(0, total_rows // step_len, ahead_block, (empty, empty))
    stacked = jnp.stack([key_total, value_total], axis=1)
    sorted_rows = (
        jnp.transpose(stacked, (2, 0, 1, 3))
        .reshape(slot_count, BLK * local_cols)
        .astype(jnp.bfloat16)
    )
    outgoing = jnp.einsum(
        "sr,sx->rx", recv_table, sorted_rows, preferred_element_type=jnp.float32
    ).astype(jnp.bfloat16)
    returned = lax.all_to_all(outgoing, "context", split_axis=0, concat_axis=0, tiled=True)
    stored_rows = jnp.einsum(
        "rt,rx->tx", send_table, returned, preferred_element_type=jnp.float32
    ).astype(jnp.bfloat16)
    kv_local = stored_rows.reshape(local_tokens, local_cols)[None]
    full_input = lax.all_gather(layer_input, "tensor", axis=2, tiled=True)
    row_input = lax.all_to_all(full_input, "context", split_axis=2, concat_axis=1, tiled=True)
    span = row_input[0]
    member_grad = jnp.einsum(
        "td,tc->dc",
        span,
        lax.all_gather(kv_local, "context", axis=1, tiled=True)[0],
        preferred_element_type=jnp.float32,
    )
    local_blocks = sign_vector.shape[0]
    had = hadamard_table(HB)
    shaped = (
        member_grad.reshape(local_blocks, HB, local_cols)
        * sign_vector.astype(jnp.float32)[:, :, None]
    )
    rotated = jnp.einsum("ij,bjc->bic", had, shaped, precision=lax.Precision.HIGHEST)
    factor = 1.0 / jnp.left_shift(jnp.int32(1), exponents[0]).astype(jnp.float32)
    quantized = (rotated * factor[:, None, None]).astype(jnp.bfloat16)
    spread = lax.all_to_all(quantized[None], "dp", split_axis=2, concat_axis=0, tiled=True)
    return jnp.sum(spread.astype(jnp.float32), axis=0)


def solution(mesh):
    return jax.shard_map(
        per_device,
        mesh=mesh,
        in_specs=(
            P("dp", "context", "tensor"),
            P("dp", "tensor", "context", None),
            P("dp", "tensor", "context", None),
            P("dp", "tensor", "context", None),
            P("dp", "tensor", "context", None),
            P("dp", "tensor", "context"),
            P("dp", "tensor", "context"),
            P("dp", None),
            P("dp", None),
            P("context", None),
            P("dp", "context"),
        ),
        out_specs=P("context", "dp", "tensor"),
        check_vma=False,
    )
```

profile of v0, /device:TPU:6, one launch (start us, length us, event | category | flops | bytes accessed | tf_op | source)
XLA Modules:
  0.0 429.9 jit_solution(6349806971333252527)
XLA Ops:
  12.0 7.2 %all-to-all-start.2 = ((bf16[16,4,32]{2,1,0:T(4,128)(2,1)}), bf16[16,4,32]{2,1,0:T(4,128)(2,1)S(1)}, u32[]{:S(2)}, u32[]{:S(2)}) async-start(bf16[16,4,32]{2,1,0:T(4,128)(2,1)} %copy.89), calls=%async_computation.2 | async-start | bytes 32768 | tf_op jit(solution)/shard_map/all_to_all | solution.py:123
  22.9 4.0 all-to-all-done.2
  26.9 3.5 all-to-all-start.5
  38.2 7.1 %all-to-all-start = ((bf16[16,4,4096]{2,1,0:T(4,128)(2,1)}), bf16[16,4,4096]{2,1,0:T(4,128)(2,1)S(1)}, u32[]{:S(2)}, u32[]{:S(2)}) async-start(bf16[16,4,4096]{2,1,0:T(4,128)(2,1)} %copy.86), calls=%async_computation | async-start | bytes 1048576 | tf_op jit(solution)/shard_map/all_to_all | solution.py:119
  45.8 15.6 %all-to-all-done = bf16[16,4,4096]{2,1,0:T(4,128)(2,1)S(1)} async-done(((bf16[16,4,4096]{2,1,0:T(4,128)(2,1)}), bf16[16,4,4096]{2,1,0:T(4,128)(2,1)S(1)}, u32[]{:S(2)}, u32[]{:S(2)}) %all-to-all-start) | async-done | bytes 524320 | tf_op jit(solution)/shard_map/all_to_all | solution.py:119
  61.3 4.2 all-to-all-start.3
  71.3 8.8 %collective-permute-done.3 = bf16[4,512]{1,0:T(4,128)(2,1)S(1)} collective-permute-done((bf16[4,512]{1,0:T(4,128)(2,1)S(1)}, bf16[4,512]{1,0:T(4,128)(2,1)S(1)}, u32[]{:S(2)}, u32[]{:S(2)}) %collective-permute-start.3) | collective-permute-done | bytes 4128 | tf_op jit(solution)/shard_map/ppermute | solution.py:18
  83.4 9.8 %all-to-all-start.1 = ((bf16[16,2,2048]{2,1,0:T(2,128)(2,1)}), bf16[16,2,2048]{2,1,0:T(2,128)(2,1)S(1)}, u32[]{:S(2)}, u32[]{:S(2)}) async-start(bf16[16,2,2048]{2,1,0:T(2,128)(2,1)} %reshape.396), calls=%async_computation.1 | async-start | bytes 262144 | tf_op jit(solution)/shard_map/all_to_all | solution.py:121
  95.2 16.5 %all-to-all-done.1 = bf16[16,2,2048]{2,1,0:T(2,128)(2,1)S(1)} async-done(((bf16[16,2,2048]{2,1,0:T(2,128)(2,1)}), bf16[16,2,2048]{2,1,0:T(2,128)(2,1)S(1)}, u32[]{:S(2)}, u32[]{:S(2)}) %all-to-all-start.1) | async-done | bytes 131104 | tf_op jit(solution)/shard_map/all_to_all | solution.py:121
  111.8 5.7 %all-to-all-start.4 = ((bf16[16,2,2048]{2,1,0:T(2,128)(2,1)}), bf16[16,2,2048]{2,1,0:T(2,128)(2,1)S(1)}, u32[]{:S(2)}, u32[]{:S(2)}) async-start(bf16[16,2,2048]{2,1,0:T(2,128)(2,1)} %reshape.398), calls=%async_computation.4 | async-start | bytes 262144 | tf_op jit(solution)/shard_map/all_to_all | solution.py:122
  119.3 6.9 %all-to-all-done.4 = bf16[16,2,2048]{2,1,0:T(2,128)(2,1)S(1)} async-done(((bf16[16,2,2048]{2,1,0:T(2,128)(2,1)}), bf16[16,2,2048]{2,1,0:T(2,128)(2,1)S(1)}, u32[]{:S(2)}, u32[]{:S(2)}) %all-to-all-start.4) | async-done | bytes 131104 | tf_op jit(solution)/shard_map/all_to_all | solution.py:122
  126.7 2.3 pad_maximum_fusion
  130.3 44.5 %while.16 = (s32[]{:T(128)}, f32[1,512,128]{2,1,0:T(8,128)S(1)}, f32[1,512,128]{2,1,0:T(8,128)S(1)}, s32[1536]{0:T(1024)S(1)}, s32[512]{0:T(512)S(1)}, /*index=5...) while((s32[]{:T(128)}, f32[1,512,128]{2,1,0:T(8,128)S(1)}, ...), condition=%wide.region_7.8_spmd.clone, body=%wide.region_6.7_spmd.clone.sunk | while | flops 270796288 | bytes 5133045 | solution.py:181
  176.7 17.0 %all_to_all.66 = bf16[16,2,4096]{2,1,0:T(2,128)(2,1)S(1)} all-to-all(bf16[16,2,4096]{2,1,0:T(2,128)(2,1)S(1)} %reshape.400), channel_id=1, replica_groups=mesh['dp'=8,'context'=16,'tensor'=4] {'context'}, dimensions={0} | all-to-all | bytes 524288 | tf_op jit(solution)/shard_map/all_to_all | solution.py:191
  194.0 18.9 %copy.98 = bf16[1,512,4096]{1,0,2:T(2,128)(2,1)} copy(bf16[1,512,4096]{2,1,0:T(8,128)(2,1)} %all-gather.5.cloned.1.call-done) | data formatting | bytes 8388608 | tf_op jit(solution)/shard_map/all_gather | solution.py:196
  212.9 28.5 %reduce.7 = bf16[4096,512]{1,0:T(8,128)(2,1)} reduce(bf16[4096,1,512]{2,1,0:T(2,128)(2,1)} %bitcast.157, bf16[]{:T(256)} %broadcast.474), dimensions={1}, to_apply=%bitcast.136.reduce_sub_computation | reduce | bytes 8388610
  241.4 11.4 %reshape.394 = bf16[16,2,65536]{2,1,0:T(2,128)(2,1)} reshape(bf16[4096,512]{1,0:T(8,128)(2,1)} %reduce.7) | data formatting | bytes 8388608
  252.8 4.7 %all-to-all-start.7 = ((bf16[16,2,65536]{2,1,0:T(2,128)(2,1)}), bf16[16,2,65536]{2,1,0:T(2,128)(2,1)}, u32[]{:S(2)}, u32[]{:S(2)}) async-start(bf16[16,2,65536]{2,1,0:T(2,128)(2,1)} %reshape.394), calls=%async_computation.7 | async-start | bytes 8388608 | tf_op jit(solution)/shard_map/all_to_all | solution.py:197
  258.9 112.6 %all-to-all-done.7 = bf16[16,2,65536]{2,1,0:T(2,128)(2,1)} async-done(((bf16[16,2,65536]{2,1,0:T(2,128)(2,1)}), bf16[16,2,65536]{2,1,0:T(2,128)(2,1)}, u32[]{:S(2)}, u32[]{:S(2)}) %all-to-all-start.7) | async-done | bytes 4194336 | tf_op jit(solution)/shard_map/all_to_all | solution.py:197
  371.4 12.3 %reshape.395 = bf16[4096,1,512]{2,1,0:T(2,128)(2,1)} reshape(bf16[16,2,65536]{2,1,0:T(2,128)(2,1)} %all-to-all-done.7) | data formatting | bytes 8388608
  383.8 6.5 %copy.108 = bf16[1,512,4096]{1,2,0:T(8,128)(2,1)} copy(bf16[1,512,4096]{1,0,2:T(2,128)(2,1)} %bitcast.158) | data formatting | bytes 8388608
  390.3 6.4 %copy.99 = bf16[1,16,512,256]{3,2,1,0:T(8,128)(2,1)} copy(bf16[1,16,512,256]{2,3,1,0:T(8,128)(2,1)} %bitcast.159) | data formatting | bytes 8388608 | tf_op jit(solution)/shard_map/all_to_all | solution.py:197
  396.7 5.2 %fusion.34 = f32[256,256]{0,1:T(8,128)S(1)} fusion(bf16[8192,256]{1,0:T(8,128)(2,1)} %bitcast.160, bf16[1,8192,256]{2,1,0:T(8,128)(2,1)} %all-gather.3.cloned.1.call-done), kind=kOutput, calls=%fused_computation.48 | convolution fusion | flops 1073741824 | bytes 8650752 | tf_op jit(solution)/shard_map/td,tc->dc/dot_general | solution.py:199
  402.6 19.2 %all_to_all.67 = bf16[1,2,128,256]{3,1,0,2:T(2,128)(2,1)S(1)} all-to-all(bf16[1,2,128,256]{3,1,0,2:T(2,128)(2,1)S(1)} %copy.101), channel_id=1, replica_groups=mesh['dp'=8,'context'=16,'tensor'=4] {'dp'}, dimensions={2} | all-to-all | bytes 262144 | tf_op jit(solution)/shard_map/all_to_all | solution.py:214
  (214 shorter events, 79.2 us)
Async XLA Ops:
  7.4 13.5 %copy-start.3 = (s32[1,256]{1,0:T(1,128)S(1)}, s32[1,256]{1,0:T(1,128)}, u32[]{:S(2)}) copy-start(s32[1,256]{1,0:T(1,128)} %param.21) | copy-start | bytes 3076
  7.4 13.7 %copy-start.1 = (bf16[1,1,512,128]{3,2,1,0:T(8,128)(2,1)S(1)}, bf16[1,1,512,128]{3,2,1,0:T(8,128)(2,1)}, u32[]{:S(2)}) copy-start(bf16[1,1,512,128]{3,2,1,0:T(8,128)(2,1)} %param.15) | copy-start | bytes 393220
  7.4 13.9 %copy-start = (bf16[1,4,512,128]{3,2,1,0:T(8,128)(2,1)S(1)}, bf16[1,4,512,128]{3,2,1,0:T(8,128)(2,1)}, u32[]{:S(2)}) copy-start(bf16[1,4,512,128]{3,2,1,0:T(8,128)(2,1)} %param.17) | copy-start | bytes 1572868
  7.4 14.4 %copy-start.2 = (bf16[1,1,512,128]{3,2,1,0:T(8,128)(2,1)S(1)}, bf16[1,1,512,128]{3,2,1,0:T(8,128)(2,1)}, u32[]{:S(2)}) copy-start(bf16[1,1,512,128]{3,2,1,0:T(8,128)(2,1)} %param.16) | copy-start | bytes 393220
  7.4 14.5 %copy-start.4 = (bf16[1,4,512]{2,1,0:T(4,128)(2,1)S(1)}, bf16[1,4,512]{2,1,0:T(4,128)(2,1)}, u32[]{:S(2)}) copy-start(bf16[1,4,512]{2,1,0:T(4,128)(2,1)} %param.19) | copy-start | bytes 12292
  7.4 23.0 %copy-start.6 = (s32[1,10]{1,0:T(1,128)S(1)}, s32[1,10]{1,0:T(1,128)}, u32[]{:S(2)}) copy-start(s32[1,10]{1,0:T(1,128)} %param.20) | copy-start | bytes 124
  7.4 186.6 %all-gather.5.cloned.1.call-start = ((), (), s32[]{:S(2)}) async-start(), calls=%async_computation.10 | async-start | bytes 5242880 | tf_op jit(solution)/shard_map/all_gather | solution.py:196
  12.0 14.8 %all-to-all-start.2 = ((bf16[16,4,32]{2,1,0:T(4,128)(2,1)}), bf16[16,4,32]{2,1,0:T(4,128)(2,1)S(1)}, u32[]{:S(2)}, u32[]{:S(2)}) async-start(bf16[16,4,32]{2,1,0:T(4,128)(2,1)} %copy.89), calls=%async_computation.2 | async-start | bytes 32768 | tf_op jit(solution)/shard_map/all_to_all | solution.py:123
  26.9 11.3 %all-to-all-start.5 = ((bf16[16,4,32]{2,1,0:T(4,128)(2,1)}), bf16[16,4,32]{2,1,0:T(4,128)(2,1)S(1)}, u32[]{:S(2)}, u32[]{:S(2)}) async-start(bf16[16,4,32]{2,1,0:T(4,128)(2,1)} %copy.94), calls=%async_computation.5 | async-start | bytes 32768 | tf_op jit(solution)/shard_map/all_to_all | solution.py:124
  38.2 23.2 %all-to-all-start = ((bf16[16,4,4096]{2,1,0:T(4,128)(2,1)}), bf16[16,4,4096]{2,1,0:T(4,128)(2,1)S(1)}, u32[]{:S(2)}, u32[]{:S(2)}) async-start(bf16[16,4,4096]{2,1,0:T(4,128)(2,1)} %copy.86), calls=%async_computation | async-start | bytes 1048576 | tf_op jit(solution)/shard_map/all_to_all | solution.py:119
  61.3 22.0 %all-to-all-start.3 = ((bf16[16,4,4096]{2,1,0:T(4,128)(2,1)}), bf16[16,4,4096]{2,1,0:T(4,128)(2,1)S(1)}, u32[]{:S(2)}, u32[]{:S(2)}) async-start(bf16[16,4,4096]{2,1,0:T(4,128)(2,1)} %copy.91), calls=%async_computation.3 | async-start | bytes 1048576 | tf_op jit(solution)/shard_map/all_to_all | solution.py:120
  65.8 14.2 %collective-permute-start.3 = (bf16[4,512]{1,0:T(4,128)(2,1)S(1)}, bf16[4,512]{1,0:T(4,128)(2,1)S(1)}, u32[]{:S(2)}, u32[]{:S(2)}) collective-permute-start(bf16[4,512]{1,0:T(4,128)(2,1)S(1)} %squeeze_reshape.6), channel_id=1, source_target_pairs={{8,0},{12,4},{16,8},{20,12},{24,16},{28,20},{32,24},{36,28},{40,32... | collective-permute-start | bytes 12296 | tf_op jit(solution)/shard_map/ppermute | solution.py:18
  67.1 13.0 %collective-permute-start.2 = (bf16[4,512]{1,0:T(4,128)(2,1)S(1)}, bf16[4,512]{1,0:T(4,128)(2,1)S(1)}, u32[]{:S(2)}, u32[]{:S(2)}) collective-permute-start(bf16[4,512]{1,0:T(4,128)(2,1)S(1)} %squeeze_reshape.6), channel_id=1, source_target_pairs={{4,0},{8,4},{12,8},{16,12},{20,16},{24,20},{28,24},{32,28},{36,32}... | collective-permute-start | bytes 12296 | tf_op jit(solution)/shard_map/ppermute | solution.py:18
  68.7 48.7 %collective-permute-start.7 = (bf16[4,512]{1,0:T(4,128)(2,1)S(1)}, bf16[4,512]{1,0:T(4,128)(2,1)S(1)}, u32[]{:S(2)}, u32[]{:S(2)}) collective-permute-start(bf16[4,512]{1,0:T(4,128)(2,1)S(1)} %squeeze_reshape.7), channel_id=1, source_target_pairs={{8,0},{12,4},{16,8},{20,12},{24,16},{28,20},{32,24},{36,28},{40,32... | collective-permute-start | bytes 12296 | tf_op jit(solution)/shard_map/ppermute | solution.py:18
  70.0 48.8 %collective-permute-start.6 = (bf16[4,512]{1,0:T(4,128)(2,1)S(1)}, bf16[4,512]{1,0:T(4,128)(2,1)S(1)}, u32[]{:S(2)}, u32[]{:S(2)}) collective-permute-start(bf16[4,512]{1,0:T(4,128)(2,1)S(1)} %squeeze_reshape.7), channel_id=1, source_target_pairs={{4,0},{8,4},{12,8},{16,12},{20,16},{24,20},{28,24},{32,28},{36,32}... | collective-permute-start | bytes 12296 | tf_op jit(solution)/shard_map/ppermute | solution.py:18
  80.8 45.9 %collective-permute-start.1 = (bf16[4,512,128]{2,1,0:T(8,128)(2,1)S(1)}, bf16[4,512,128]{2,1,0:T(8,128)(2,1)S(1)}, u32[]{:S(2)}, u32[]{:S(2)}) collective-permute-start(bf16[4,512,128]{2,1,0:T(8,128)(2,1)S(1)} %reshape.358), channel_id=1, source_target_pairs={{8,0},{12,4},{16,8},{20,12},{24,16},{28,20},{32,24},{36,28},{40,32... | collective-permute-start | bytes 1572872 | tf_op jit(solution)/shard_map/ppermute | solution.py:18
  82.1 44.6 %collective-permute-start = (bf16[4,512,128]{2,1,0:T(8,128)(2,1)S(1)}, bf16[4,512,128]{2,1,0:T(8,128)(2,1)}, u32[]{:S(2)}, u32[]{:S(2)}) collective-permute-start(bf16[4,512,128]{2,1,0:T(8,128)(2,1)S(1)} %reshape.358), channel_id=1, source_target_pairs={{4,0},{8,4},{12,8},{16,12},{20,16},{24,20},{28,24},{32,28},{36,32}... | collective-permute-start | bytes 1572872 | tf_op jit(solution)/shard_map/ppermute | solution.py:18
  83.4 28.4 %all-to-all-start.1 = ((bf16[16,2,2048]{2,1,0:T(2,128)(2,1)}), bf16[16,2,2048]{2,1,0:T(2,128)(2,1)S(1)}, u32[]{:S(2)}, u32[]{:S(2)}) async-start(bf16[16,2,2048]{2,1,0:T(2,128)(2,1)} %reshape.396), calls=%async_computation.1 | async-start | bytes 262144 | tf_op jit(solution)/shard_map/all_to_all | solution.py:121
  93.9 35.1 %collective-permute-start.5 = (bf16[4,512,128]{2,1,0:T(8,128)(2,1)S(1)}, bf16[4,512,128]{2,1,0:T(8,128)(2,1)}, u32[]{:S(2)}, u32[]{:S(2)}) collective-permute-start(bf16[4,512,128]{2,1,0:T(8,128)(2,1)S(1)} %reshape.362), channel_id=1, source_target_pairs={{8,0},{12,4},{16,8},{20,12},{24,16},{28,20},{32,24},{36,28},{40,32... | collective-permute-start | bytes 1572872 | tf_op jit(solution)/shard_map/ppermute | solution.py:18
  111.8 14.4 %all-to-all-start.4 = ((bf16[16,2,2048]{2,1,0:T(2,128)(2,1)}), bf16[16,2,2048]{2,1,0:T(2,128)(2,1)S(1)}, u32[]{:S(2)}, u32[]{:S(2)}) async-start(bf16[16,2,2048]{2,1,0:T(2,128)(2,1)} %reshape.398), calls=%async_computation.4 | async-start | bytes 262144 | tf_op jit(solution)/shard_map/all_to_all | solution.py:122
  117.5 11.6 %collective-permute-start.4 = (bf16[4,512,128]{2,1,0:T(8,128)(2,1)S(1)}, bf16[4,512,128]{2,1,0:T(8,128)(2,1)}, u32[]{:S(2)}, u32[]{:S(2)}) collective-permute-start(bf16[4,512,128]{2,1,0:T(8,128)(2,1)S(1)} %reshape.362), channel_id=1, source_target_pairs={{4,0},{8,4},{12,8},{16,12},{20,16},{24,20},{28,24},{32,28},{36,32}... | collective-permute-start | bytes 1572872 | tf_op jit(solution)/shard_map/ppermute | solution.py:18
  252.8 6.0 %copy-start.7 = (s32[1,2]{1,0:T(1,128)S(1)}, s32[1,2]{1,0:T(1,128)}, u32[]{:S(2)}) copy-start(s32[1,2]{1,0:T(1,128)} %param.23) | copy-start | bytes 28
  252.8 118.6 %all-to-all-start.7 = ((bf16[16,2,65536]{2,1,0:T(2,128)(2,1)}), bf16[16,2,65536]{2,1,0:T(2,128)(2,1)}, u32[]{:S(2)}, u32[]{:S(2)}) async-start(bf16[16,2,65536]{2,1,0:T(2,128)(2,1)} %reshape.394), calls=%async_computation.7 | async-start | bytes 8388608 | tf_op jit(solution)/shard_map/all_to_all | solution.py:197
  257.5 139.2 %all-gather.3.cloned.1.call-start = ((), (), s32[]{:S(2)}) async-start(), calls=%async_computation.9 | async-start | bytes 4456448 | tf_op jit(solution)/shard_map/all_gather | solution.py:202
  (1 other events, 6.0 us)
Sparse Core Ops, SparseCore 0:
  10.3 56.3 all-gather.4
Sparse Core Ops, SparseCore 1:
  260.1 110.8 all-gather.2
where the time goes:
time: 433 us; the launch traced here: 430 us
  waiting for transfers between devices  165 us (38%)
  local copies, waits for them, and re-layouts  69.7 us (16%)
  starting transfers between devices  52.6 us (12%)
  matrix products  49.4 us (11%)
  other arithmetic  40.5 us (9%)
  blocking collectives  36.2 us (8%)
  between operations  15.5 us (4%)
    all_to_all x1, waiting for transfers between devices, per_device(): lax.all_to_all(full_input, 'context', split_axis=2, concat_axis=1, tiled=...  113 us
    unnamed x27, local copies, waits for them, and re-layouts  33.5 us
    unnamed x4, other arithmetic  29.1 us
    dot_general x12, matrix products, block_grads(): jnp.einsum('ghqk,ghqd->gkd', dscores, query_blk, preferred_element_type=j...  19.9 us
    all_to_all x1, blocking collectives, per_device(): lax.all_to_all(quantized[None], 'dp', split_axis=2, concat_axis=0, tiled=...  19.2 us
    all_gather x1, local copies, waits for them, and re-layouts, per_device(): full_input = lax.all_gather(layer_input, 'tensor', axis=2, tiled=True)  18.9 us
    all_to_all x1, blocking collectives, per_device(): lax.all_to_all(outgoing, 'context', split_axis=0, concat_axis=0, tiled=True)  17 us
    all_to_all x1, waiting for transfers between devices, per_device(): lax.all_to_all(pack(key_states), 'context', split_axis=0, concat_axis=0,...  16.5 us
  transfers between devices with their start and end apart: 17, of which 6 were waited for; matrix products, arithmetic and copies ran while one was open for 22% of the time, Pallas kernels for 0%

commit v1 on v0

v1 whole, which is shorter than its diff:
```python
import jax
import jax.numpy as jnp
from jax import lax
from jax.experimental import pallas as pl
from jax.experimental.pallas import tpu as pltpu
from jax.sharding import Mesh
from jax.sharding import PartitionSpec as P

HD = 128
GROUP = 4
BLK = 32
PAD = 128
HB = 128
CORES = 2
SPAN = 3
LOG2E = 1.4426950408889634

QROWS = GROUP * BLK
KV_AT = 2 * QROWS
AUX_AT = KV_AT + SPAN * 2 * BLK
AUX_ROWS = 16
ROWS = AUX_AT + AUX_ROWS
UNIT_BLKS = PAD // BLK


def hadamard_signs(table_size):
    index_row = jnp.arange(table_size, dtype=jnp.int32)
    common = jnp.bitwise_and(index_row[:, None], index_row[None, :])
    parity = jnp.zeros((table_size, table_size), jnp.int32)
    for bit_pos in range(table_size.bit_length() - 1):
        parity = parity + jnp.bitwise_and(jnp.right_shift(common, bit_pos), 1)
    return (1 - 2 * jnp.bitwise_and(parity, 1)).astype(jnp.bfloat16)


def pack_kernel(order_ref, where_ref, query_ref, grad_ref, key_ref, value_ref, aux_ref, out_ref):
    slots = key_ref.shape[0] // BLK
    groups = out_ref.shape[0]
    first = where_ref[0] * slots
    for span in range(1, SPAN):
        for dest in range(span):
            at = KV_AT + span * 2 * BLK
            out_ref[dest, at : at + 2 * BLK, :] = jnp.zeros((2 * BLK, HD), out_ref.dtype)
    for slot in range(slots):
        dest = order_ref[first + slot] // slots
        rows = slice(slot * BLK, (slot + 1) * BLK)
        for head in range(GROUP):
            out_ref[dest, head * BLK : (head + 1) * BLK, :] = query_ref[head, rows, :]
            at = QROWS + head * BLK
            out_ref[dest, at : at + BLK, :] = grad_ref[head, rows, :]
        out_ref[dest, AUX_AT:ROWS, :] = aux_ref[slot]
        key_blk = key_ref[rows, :]
        value_blk = value_ref[rows, :]
        for span in range(SPAN):

            @pl.when(dest + span < groups)
            def _():
                at = KV_AT + span * 2 * BLK
                out_ref[dest + span, at : at + BLK, :] = key_blk
                out_ref[dest + span, at + BLK : at + 2 * BLK, :] = value_blk


def attend_kernel(
    slot_ref, start_ref, recv_ref, out_ref,
    query_scr, grad_scr, stat_scr, key_scr, value_scr, dkey_scr, dvalue_scr,
):
    groups = recv_ref.shape[0]
    chunk = key_scr.shape[0] // SPAN
    units = chunk // PAD
    width = UNIT_BLKS * QROWS
    dkey_scr[...] = jnp.zeros_like(dkey_scr)
    dvalue_scr[...] = jnp.zeros_like(dvalue_scr)
    for src in range(groups):
        slot = slot_ref[0, src]
        at = pl.multiple_of(slot * QROWS, QROWS)
        query_scr[pl.ds(at, QROWS), :] = recv_ref[src, 0:QROWS, :]
        grad_scr[pl.ds(at, QROWS), :] = recv_ref[src, QROWS : 2 * QROWS, :]
        stat_scr[slot] = recv_ref[src, AUX_AT:ROWS, :].astype(jnp.float32)
        for span in range(SPAN):
            row = (SPAN - 1 - span) * chunk + slot_ref[span, src] * BLK
            row = pl.multiple_of(row, BLK)
            at = KV_AT + span * 2 * BLK
            key_scr[pl.ds(row, BLK), :] = recv_ref[src, at : at + BLK, :]
            value_scr[pl.ds(row, BLK), :] = recv_ref[src, at + BLK : at + 2 * BLK, :]

    scale = HD ** (-0.5)
    key_at = lax.broadcasted_iota(jnp.int32, (PAD, width), 0)
    column = lax.broadcasted_iota(jnp.int32, (PAD, width), 1)
    query_at = (column // QROWS) * BLK + column % BLK
    causal = key_at <= query_at

    for unit in range(units):
        cols = slice(unit * width, (unit + 1) * width)
        blocks = range(unit * UNIT_BLKS, (unit + 1) * UNIT_BLKS)
        lse = jnp.concatenate([stat_scr[b, 0:1, :] for b in blocks], axis=1) * LOG2E
        dots = jnp.concatenate([stat_scr[b, 1:2, :] for b in blocks], axis=1)

        def visit(tile, diagonal):
            row = pl.multiple_of(tile * PAD, PAD)
            query_blk = query_scr[cols, :]
            grad_blk = grad_scr[cols, :]
            key_blk = key_scr[pl.ds(row, PAD), :]
            value_blk = value_scr[pl.ds(row, PAD), :]
            contract_last = (((1,), (1,)), ((), ()))
            scores = lax.dot_general(
                key_blk, query_blk, contract_last, preferred_element_type=jnp.float32
            )
            probs = jnp.exp2(scores * (scale * LOG2E) - lse)
            if diagonal:
                probs = jnp.where(causal, probs, 0.0)
            dprobs = lax.dot_general(
                value_blk, grad_blk, contract_last, preferred_element_type=jnp.float32
            )
            dscores = (probs * (dprobs - dots)).astype(jnp.bfloat16)
            dvalue_scr[pl.ds(row, PAD), :] += jnp.dot(
                probs.astype(jnp.bfloat16), grad_blk, preferred_element_type=jnp.float32
            )
            dkey_scr[pl.ds(row, PAD), :] += jnp.dot(
                dscores, query_blk, preferred_element_type=jnp.float32
            )

        last = (SPAN - 1) * units + unit

        @pl.loop(start_ref[unit], last)
        def _(tile):
            visit(tile, False)

        visit(jnp.int32(last), True)

    for src in range(groups):
        for span in range(SPAN):
            row = (SPAN - 1 - span) * chunk + slot_ref[span, src] * BLK
            row = pl.multiple_of(row, BLK)
            dkey = dkey_scr[pl.ds(row, BLK), :] * scale
            out_ref[src, span, 0:BLK, :] = dkey.astype(out_ref.dtype)
            out_ref[src, span, BLK : 2 * BLK, :] = dvalue_scr[pl.ds(row, BLK), :].astype(
                out_ref.dtype
            )


def collect_kernel(target_ref, recv_ref, out_ref):
    groups = recv_ref.shape[0]
    for slot in range(out_ref.shape[0] // BLK):
        owner = target_ref[slot]
        total = recv_ref[owner, 0].astype(jnp.float32)
        for span in range(1, SPAN):
            extra = recv_ref[jnp.minimum(owner + span, groups - 1), span].astype(jnp.float32)
            total = total + jnp.where(owner + span < groups, extra, 0.0)
        rows = slice(slot * BLK, (slot + 1) * BLK)
        total = total.astype(out_ref.dtype)
        out_ref[rows, 0:HD] = total[0:BLK]
        out_ref[rows, HD : 2 * HD] = total[BLK : 2 * BLK]


def turn_kernel(core_ref, input_ref, own_ref, other_ref):
    span = 2 * HB
    core = core_ref[0]
    for part in range(own_ref.shape[0] // span):
        rows = slice(part * span, (part + 1) * span)
        at = pl.multiple_of((CORES * part + core) * span, span)
        own_ref[rows, :] = input_ref[:, pl.ds(at, span)].T
        at = pl.multiple_of((CORES * part + 1 - core) * span, span)
        other_ref[rows, :] = input_ref[:, pl.ds(at, span)].T


def product_kernel(
    core_ref, own_ref, other_ref, own_kv_ref, other_kv_ref, had_ref, aux_ref, out_ref
):
    grad = jnp.dot(own_ref[...], own_kv_ref[...], preferred_element_type=jnp.float32)
    grad = grad + jnp.dot(other_ref[...], other_kv_ref[...], preferred_element_type=jnp.float32)
    aux = aux_ref[0].astype(jnp.float32)
    replicas = out_ref.shape[0]
    had = had_ref[...].astype(jnp.float32)
    for blk in range(grad.shape[0] // HB):
        rows = grad[blk * HB : (blk + 1) * HB]
        table = (had * aux[2 + blk : 3 + blk, :]).astype(jnp.bfloat16)
        high = rows.astype(jnp.bfloat16)
        low = (rows - high.astype(jnp.float32)).astype(jnp.bfloat16)
        rotated = jnp.dot(table, high, preferred_element_type=jnp.float32)
        rotated = rotated + jnp.dot(table, low, preferred_element_type=jnp.float32)
        factor = aux[4 + blk : 5 + blk, :] * (HB ** (-0.5))
        rotated = rotated * jnp.concatenate([factor] * (rows.shape[1] // HB), axis=1)
        out_ref[:, 0, blk] = rotated.astype(out_ref.dtype).reshape(
            replicas, HB // replicas, rows.shape[1]
        )


def prefetched(kernel, scalars, out_shape, scratch=(), grid=(), in_specs=None, out_specs=None):
    vmem = pl.BlockSpec(memory_space=pltpu.VMEM)
    many = isinstance(out_shape, tuple)

    def call(*operands):
        specs = in_specs or [vmem] * (len(operands) - scalars)
        outs = out_specs or (tuple(vmem for _ in out_shape) if many else vmem)
        return pl.pallas_call(
            kernel,
            out_shape=out_shape,
            grid_spec=pltpu.PrefetchScalarGridSpec(
                num_scalar_prefetch=scalars,
                grid=grid,
                in_specs=specs,
                out_specs=outs,
                scratch_shapes=list(scratch),
            ),
            compiler_params=pltpu.CompilerParams(vmem_limit_bytes=48 << 20),
        )(*operands)

    return call


def per_device(
    layer_input,
    queries,
    key_states,
    value_states,
    out_grad,
    log_sums,
    grad_dots,
    doc_stretches,
    stretch_order,
    sign_vector,
    exponents,
):
    context = ("y", "core")
    low = jnp.bfloat16
    tokens = queries.shape[2]
    slots = tokens // BLK
    groups = lax.axis_size(context)
    lines = lax.axis_size("y")
    replicas = lax.axis_size("dp")
    widths = lax.axis_size("tensor")
    order_row = stretch_order[0]
    where = lax.axis_index(context)
    core = lax.axis_index("core").reshape(1)

    def by_block(array):
        return jnp.transpose(array[0].reshape(GROUP, slots, BLK), (1, 0, 2)).reshape(slots, 1, HD)

    signs = jnp.broadcast_to(sign_vector.astype(low)[None], (slots, 2, HB))
    factor = 1.0 / jnp.left_shift(jnp.int32(1), exponents[0]).astype(jnp.float32)
    factors = jnp.broadcast_to(factor.astype(low)[None, :, None], (slots, 2, HB))
    aux = jnp.concatenate(
        [
            by_block(log_sums),
            by_block(grad_dots),
            signs,
            factors,
            jnp.zeros((slots, AUX_ROWS - 6, HD), low),
        ],
        axis=1,
    )
    packed = prefetched(pack_kernel, 2, jax.ShapeDtypeStruct((groups, ROWS, HD), low))(
        order_row,
        where.reshape(1),
        queries[0],
        out_grad[0],
        key_states[0, 0],
        value_states[0, 0],
        aux,
    )
    recv = lax.all_to_all(packed, context, split_axis=0, concat_axis=0, tiled=True)

    half = layer_input.shape[2] // CORES
    turned = jax.ShapeDtypeStruct((half, tokens), low)
    own_input, other_input = prefetched(turn_kernel, 1, (turned, turned))(core, layer_input[0])
    other_input = lax.ppermute(other_input, "core", [(0, 1), (1, 0)])
    own_input = lax.all_gather(own_input, "tensor", axis=0, tiled=True)
    other_input = lax.all_gather(other_input, "tensor", axis=0, tiled=True)

    order_grid = order_row.reshape(groups, slots)
    chunk_ids = (where - jnp.arange(SPAN, dtype=jnp.int32))[:, None, None]
    slot_map = jnp.sum(
        jnp.where(order_grid[None] // slots == chunk_ids, order_grid[None] % slots, 0), axis=2
    )
    ends = jnp.cumsum(doc_stretches[0])
    chunk_units = tokens // PAD
    unit_ids = where * chunk_units + jnp.arange(chunk_units, dtype=jnp.int32)
    doc_start = jnp.max(jnp.where(ends[None, :] <= unit_ids[:, None], ends[None, :], 0), axis=1)
    starts = doc_start - (where - (SPAN - 1)) * chunk_units

    window = SPAN * tokens
    partial_grads = prefetched(
        attend_kernel,
        2,
        jax.ShapeDtypeStruct((groups, SPAN, 2 * BLK, HD), low),
        scratch=(
            pltpu.VMEM((slots * QROWS, HD), low),
            pltpu.VMEM((slots * QROWS, HD), low),
            pltpu.VMEM((slots, AUX_ROWS, HD), jnp.float32),
            pltpu.VMEM((window, HD), low),
            pltpu.VMEM((window, HD), low),
            pltpu.VMEM((window, HD), jnp.float32),
            pltpu.VMEM((window, HD), jnp.float32),
        ),
    )(slot_map, starts, recv)
    returned = lax.all_to_all(partial_grads, context, split_axis=0, concat_axis=0, tiled=True)
    targets = lax.dynamic_slice_in_dim(order_row, where * slots, slots, 0) // slots
    own_kv = prefetched(collect_kernel, 1, jax.ShapeDtypeStruct((tokens, 2 * HD), low))(
        targets, returned
    )
    other_kv = lax.ppermute(own_kv, "core", [(0, 1), (1, 0)])

    rows = 2 * HB
    spread = prefetched(
        product_kernel,
        1,
        jax.ShapeDtypeStruct((replicas, lines, 2, HB // replicas, 2 * HD), low),
        grid=(lines,),
        in_specs=[
            pl.BlockSpec((rows, tokens), lambda i, core: (i, 0)),
            pl.BlockSpec((rows, tokens), lambda i, core: (i, 0)),
            pl.BlockSpec((tokens, 2 * HD), lambda i, core: (0, 0)),
            pl.BlockSpec((tokens, 2 * HD), lambda i, core: (0, 0)),
            pl.BlockSpec((HB, HB), lambda i, core: (0, 0)),
            pl.BlockSpec(
                (1, AUX_ROWS, HD), lambda i, core: (CORES * i + core[0], AUX_AT // AUX_ROWS, 0)
            ),
        ],
        out_specs=pl.BlockSpec(
            (replicas, 1, 2, HB // replicas, 2 * HD), lambda i, core: (0, i, 0, 0, 0)
        ),
    )(core, own_input, other_input, own_kv, other_kv, hadamard_signs(HB), recv)
    spread = spread.reshape(replicas * lines, 2, HB // replicas, 2 * HD)
    shares = lax.all_to_all(spread, ("dp", "y"), split_axis=0, concat_axis=0, tiled=True)
    return jnp.sum(shares.astype(jnp.float32), axis=0)


def solution(mesh):
    replicas, groups, widths = mesh.devices.shape
    split = Mesh(
        mesh.devices.reshape(replicas, groups // CORES, CORES, widths),
        ("dp", "y", "core", "tensor"),
    )
    context = ("y", "core")
    return jax.shard_map(
        per_device,
        mesh=split,
        in_specs=(
            P("dp", context, "tensor"),
            P("dp", "tensor", context, None),
            P("dp", "tensor", context, None),
            P("dp", "tensor", context, None),
            P("dp", "tensor", context, None),
            P("dp", "tensor", context),
            P("dp", "tensor", context),
            P("dp", None),
            P("dp", None),
            P(context, None),
            P("dp", context),
        ),
        out_specs=P(context, "dp", "tensor"),
        check_vma=False,
    )
```

time: 433 us -> 170 us (0.39)
  waiting for transfers between devices: 165 us -> 61.5 us
  local copies, waits for them, and re-layouts: 69.7 us -> 9.14 us
  matrix products: 49.4 us -> 0 us
  other arithmetic: 40.5 us -> 3.51 us
  starting transfers between devices: 52.6 us -> 22.9 us
  Pallas kernels: 0 us -> 15.2 us
  blocking collectives: 36.2 us -> 43.9 us
    all_to_all x7 -> x2, waiting for transfers between devices: 156 us -> 58.9 us  [the longest x1 38.3 us: per_device(): lax.all_to_all(packed, context, split_axis=0, concat_axis=0, tiled=True)]
    dot_general x52 -> x0, matrix products: 49.4 us -> none  [the longest x12 19.9 us: block_grads(): jnp.einsum('ghqk,ghqd->gkd', dscores, query_blk, preferred_element_type=j...]
    unnamed x4 -> x1, other arithmetic: 29.1 us -> 0.63 us
    unnamed x27, local copies, waits for them, and re-layouts: 33.5 us -> 6.95 us
    all_to_all x7 -> x2, starting transfers between devices: 42.2 us -> 16.3 us  [the longest x1 8.95 us: per_device(): lax.all_to_all(partial_grads, context, split_axis=0, concat_axis=0, tiled...]
    all_gather x1 -> x0, local copies, waits for them, and re-layouts: 18.9 us -> none  [per_device(): full_input = lax.all_gather(layer_input, 'tensor', axis=2, tiled=True)]
    pallas_call x0 -> x5, Pallas kernels: none -> 15.2 us  [call(): pl.pallas_call(kernel, out_shape=out_shape, grid_spec=pltpu.PrefetchScala...]
    all_to_all x2 -> x1, blocking collectives: 36.2 us -> 43.9 us  [per_device(): lax.all_to_all(spread, ('dp', 'y'), split_axis=0, concat_axis=0, tiled=True)]
  transfers between devices with their start and end apart: 17 -> 6, of which waited for: 6 -> 4; matrix products, arithmetic and copies ran while one was open for 22% -> 3% of each run, Pallas kernels for 0% -> 4%
where the time goes in v1:
time: 170 us
  waiting for transfers between devices  61.5 us (36%)
  blocking collectives  43.9 us (26%)
  starting transfers between devices  22.9 us (13%)
  Pallas kernels  15.2 us (9%)
  between operations  13.6 us (8%)
  local copies, waits for them, and re-layouts  9.14 us (5%)
  other arithmetic  3.51 us (2%)
    all_to_all x1, blocking collectives, per_device(): lax.all_to_all(spread, ('dp', 'y'), split_axis=0, concat_axis=0, tiled=True)  43.9 us
    all_to_all x1, waiting for transfers between devices, per_device(): lax.all_to_all(packed, context, split_axis=0, concat_axis=0, tiled=True)  38.3 us
    all_to_all x1, waiting for transfers between devices, per_device(): lax.all_to_all(partial_grads, context, split_axis=0, concat_axis=0, tiled...  20.6 us
    pallas_call x5, Pallas kernels, call(): pl.pallas_call(kernel, out_shape=out_shape, grid_spec=pltpu.PrefetchScala...  15.2 us
    all_to_all x1, starting transfers between devices, per_device(): lax.all_to_all(partial_grads, context, split_axis=0, concat_axis=0, tiled...  8.95 us
    all_to_all x1, starting transfers between devices, per_device(): lax.all_to_all(packed, context, split_axis=0, concat_axis=0, tiled=True)  7.34 us
    unnamed x27, local copies, waits for them, and re-layouts  6.95 us
    ppermute x1, starting transfers between devices, per_device(): other_kv = lax.ppermute(own_kv, 'core', [(0, 1), (1, 0)])  4.29 us
  transfers between devices with their start and end apart: 6, of which 4 were waited for; matrix products, arithmetic and copies ran while one was open for 3% of the time, Pallas kernels for 4%

profile of v1, /device:TPU:6, one launch (start us, length us, event | category | flops | bytes accessed | tf_op | source)
XLA Modules:
  0.0 169.8 jit_solution(1178008766198297714)
XLA Ops:
  6.5 1.2 copy-done.2
  7.8 1.1 shard_map.109
  8.8 0.8 copy-done.9
  9.7 0.8 reshape_squeeze.6
  10.6 0.8 reshape_squeeze.7
  11.4 0.7 convert_element_type.27
  13.2 0.7 copy-done.7
  13.9 1.0 shard_map.110
  14.9 1.3 copy-done
  16.1 7.3 %all-to-all-start = ((bf16[16,464,128]{2,1,0:T(8,128)(2,1)}), bf16[16,464,128]{2,1,0:T(8,128)(2,1)S(1)}, u32[]{:S(2)}, u32[]{:S(2)}) async-start(bf16[16,464,128]{2,1,0:T(8,128)(2,1)} %copy-done), calls=%async_computation | async-start | bytes 3801088 | tf_op jit(solution)/shard_map/all_to_all | solution.py:260
  23.5 2.3 %collective-permute-start = (bf16[512,512]{1,0:T(8,128)(2,1)S(1)}, bf16[512,512]{1,0:T(8,128)(2,1)S(1)}, u32[]{:S(2)}, u32[]{:S(2)}) collective-permute-start(bf16[512,512]{1,0:T(8,128)(2,1)S(1)} %copy-done.10), channel_id=1, source_target_pairs={{0,4},{4,0},{1,5},{5,1},{2,6},{6,2},{3,7},{7,3},{8,12},{12,8},{9,1... | collective-permute-start | bytes 1572872 | tf_op jit(solution)/shard_map/ppermute | solution.py:265
  25.9 1.5 collective-permute-done
  27.4 0.8 copy-done.11
  30.1 38.3 %all-to-all-done.recv_ref.aux_ref = bf16[16,464,128]{2,1,0:T(8,128)(2,1)S(1)} async-done(((bf16[16,464,128]{2,1,0:T(8,128)(2,1)}), bf16[16,464,128]{2,1,0:T(8,128)(2,1)S(1)}, u32[]{:S(2)}, u32[]{:S(2)}) %all-to-all-start) | async-done | bytes 1900576 | tf_op jit(solution)/shard_map/all_to_all | solution.py:260
  68.4 5.6 %shard_map.111 = bf16[16,3,64,128]{3,2,1,0:T(8,128)(2,1)} custom-call(s32[3,16]{1,0:T(4,128)S(1)} %select_reduce_fusion.slot_ref, s32[4]{0:T(128)S(1)} %broadcast_subtract_fusion.start_ref, bf16[16,464,128]{2,1,0:T(8,128)(2,1)S(1)} %all-to-all-done.recv_ref.aux_ref), custom_call_target="tpu_custom_call" | custom-call | tf_op jit(solution)/shard_map/pallas_call | solution.py:194
  74.0 9.0 %all-to-all-start.1 = ((bf16[16,3,64,128]{3,2,1,0:T(8,128)(2,1)}), bf16[16,3,64,128]{3,2,1,0:T(8,128)(2,1)S(1)}, u32[]{:S(2)}, u32[]{:S(2)}) async-start(bf16[16,3,64,128]{3,2,1,0:T(8,128)(2,1)} %shard_map.111), calls=%async_computation.1 | async-start | bytes 1572864 | tf_op jit(solution)/shard_map/all_to_all | solution.py:295
  83.0 20.6 %all-to-all-done.1.recv_ref = bf16[16,3,64,128]{3,2,1,0:T(8,128)(2,1)S(1)} async-done(((bf16[16,3,64,128]{3,2,1,0:T(8,128)(2,1)}), bf16[16,3,64,128]{3,2,1,0:T(8,128)(2,1)S(1)}, u32[]{:S(2)}, u32[]{:S(2)}) %all-to-all-start.1) | async-done | bytes 786464 | tf_op jit(solution)/shard_map/all_to_all | solution.py:295
  103.6 0.7 shard_map.112.own_kv_ref
  104.3 4.3 %collective-permute-start.1 = (bf16[512,256]{1,0:T(8,128)(2,1)S(1)}, bf16[512,256]{1,0:T(8,128)(2,1)S(1)}, u32[]{:S(2)}, u32[]{:S(2)}) collective-permute-start(bf16[512,256]{1,0:T(8,128)(2,1)S(1)} %shard_map.112.own_kv_ref), channel_id=1, source_target_pairs={{0,4},{4,0},{1,5},{5,1},{2,6},{6,2},{3,7},{7,3},{8,12},{12,8},{9,1... | collective-permute-start | bytes 786440 | tf_op jit(solution)/shard_map/ppermute | solution.py:300
  108.8 1.0 collective-permute-done.1.other_kv_ref
  109.8 1.6 copy-done.1
  111.4 6.9 %shard_map.113 = bf16[8,8,2,16,256]{4,3,2,1,0:T(8,128)(2,1)S(1)} custom-call(s32[1]{0:T(128)} %bitcast.core_ref, bf16[2048,512]{1,0:T(8,128)(2,1)S(1)} %copy-done.1, bf16[2048,512]{1,0:T(8,128)(2,1)} %all-gather.5.cloned.1.call-done.other_ref, bf16[512,256]{1,0:T(8,128)(2,1)S(1)} %shard_map.112.own_kv_ref, ...), custom_call_target="tpu_custom_call" | custom-call | tf_op jit(solution)/shard_map/pallas_call | solution.py:194
  118.3 43.9 %all_to_all.15 = bf16[64,2,16,256]{3,2,1,0:T(8,128)(2,1)S(1)} all-to-all(bf16[64,2,16,256]{3,2,1,0:T(8,128)(2,1)S(1)} %bitcast.27), channel_id=1, replica_groups=mesh['dp'=8,'y'=8,'core'=2,'tensor'=4] {'dp','y'}, dimensions={0} | all-to-all | bytes 2097152 | tf_op jit(solution)/shard_map/all_to_all | solution.py:323
  162.2 0.8 convert_reduce_fusion
  (47 shorter events, 3.4 us)
Async XLA Ops:
  6.5 102.2 %all-gather.3.cloned.1.call-start = ((), (), s32[]{:S(2)}) async-start(), calls=%async_computation.3 | async-start | bytes 2621440 | tf_op jit(solution)/shard_map/all_gather | solution.py:266
  6.5 1.2 copy-start.2
  7.8 5.4 %copy-start.3 = (bf16[1,4,512,128]{3,2,1,0:T(8,128)(2,1)S(1)}, bf16[1,4,512,128]{3,2,1,0:T(8,128)(2,1)}, u32[]{:S(2)}) copy-start(bf16[1,4,512,128]{3,2,1,0:T(8,128)(2,1)} %param.12) | copy-start | bytes 1572868
  7.8 5.4 %copy-start.4 = (bf16[1,4,512,128]{3,2,1,0:T(8,128)(2,1)S(1)}, bf16[1,4,512,128]{3,2,1,0:T(8,128)(2,1)}, u32[]{:S(2)}) copy-start(bf16[1,4,512,128]{3,2,1,0:T(8,128)(2,1)} %param.15) | copy-start | bytes 1572868
  7.8 5.4 %copy-start.5 = (bf16[1,1,512,128]{3,2,1,0:T(8,128)(2,1)S(1)}, bf16[1,1,512,128]{3,2,1,0:T(8,128)(2,1)}, u32[]{:S(2)}) copy-start(bf16[1,1,512,128]{3,2,1,0:T(8,128)(2,1)} %param.13) | copy-start | bytes 393220
  7.8 5.4 %copy-start.6 = (bf16[1,1,512,128]{3,2,1,0:T(8,128)(2,1)S(1)}, bf16[1,1,512,128]{3,2,1,0:T(8,128)(2,1)}, u32[]{:S(2)}) copy-start(bf16[1,1,512,128]{3,2,1,0:T(8,128)(2,1)} %param.14) | copy-start | bytes 393220
  8.8 0.8 copy-start.9
  13.2 0.7 copy-start.7
  14.9 1.3 copy-start
  16.1 7.4 %copy-start.10 = (bf16[512,512]{1,0:T(8,128)(2,1)S(1)}, bf16[512,512]{1,0:T(8,128)(2,1)}, u32[]{:S(2)}) copy-start(bf16[512,512]{1,0:T(8,128)(2,1)} %copy-done.9) | copy-start | bytes 1572868
  16.1 12.1 %copy-start.12 = (s32[1,10]{1,0:T(1,128)S(1)}, s32[1,10]{1,0:T(1,128)}, u32[]{:S(2)}) copy-start(s32[1,10]{1,0:T(1,128)} %param.18) | copy-start | bytes 124
  16.1 12.8 %copy-start.8 = (s32[1,256]{1,0:T(1,128)S(1)}, s32[1,256]{1,0:T(1,128)}, u32[]{:S(2)}) copy-start(s32[1,256]{1,0:T(1,128)} %param.19) | copy-start | bytes 3076
  16.1 52.3 %all-to-all-start = ((bf16[16,464,128]{2,1,0:T(8,128)(2,1)}), bf16[16,464,128]{2,1,0:T(8,128)(2,1)S(1)}, u32[]{:S(2)}, u32[]{:S(2)}) async-start(bf16[16,464,128]{2,1,0:T(8,128)(2,1)} %copy-done), calls=%async_computation | async-start | bytes 3801088 | tf_op jit(solution)/shard_map/all_to_all | solution.py:260
  23.5 85.3 %all-gather.5.cloned.1.call-start = ((), (), s32[]{:S(2)}) async-start(), calls=%async_computation.4 | async-start | bytes 2621440 | tf_op jit(solution)/shard_map/all_gather | solution.py:267
  23.5 3.8 %collective-permute-start = (bf16[512,512]{1,0:T(8,128)(2,1)S(1)}, bf16[512,512]{1,0:T(8,128)(2,1)S(1)}, u32[]{:S(2)}, u32[]{:S(2)}) collective-permute-start(bf16[512,512]{1,0:T(8,128)(2,1)S(1)} %copy-done.10), channel_id=1, source_target_pairs={{0,4},{4,0},{1,5},{5,1},{2,6},{6,2},{3,7},{7,3},{8,12},{12,8},{9,1... | collective-permute-start | bytes 1572872 | tf_op jit(solution)/shard_map/ppermute | solution.py:265
  27.4 0.8 copy-start.11
  74.0 29.6 %all-to-all-start.1 = ((bf16[16,3,64,128]{3,2,1,0:T(8,128)(2,1)}), bf16[16,3,64,128]{3,2,1,0:T(8,128)(2,1)S(1)}, u32[]{:S(2)}, u32[]{:S(2)}) async-start(bf16[16,3,64,128]{3,2,1,0:T(8,128)(2,1)} %shard_map.111), calls=%async_computation.1 | async-start | bytes 1572864 | tf_op jit(solution)/shard_map/all_to_all | solution.py:295
  104.3 5.4 %collective-permute-start.1 = (bf16[512,256]{1,0:T(8,128)(2,1)S(1)}, bf16[512,256]{1,0:T(8,128)(2,1)S(1)}, u32[]{:S(2)}, u32[]{:S(2)}) collective-permute-start(bf16[512,256]{1,0:T(8,128)(2,1)S(1)} %shard_map.112.own_kv_ref), channel_id=1, source_target_pairs={{0,4},{4,0},{1,5},{5,1},{2,6},{6,2},{3,7},{7,3},{8,12},{12,8},{9,1... | collective-permute-start | bytes 786440 | tf_op jit(solution)/shard_map/ppermute | solution.py:300
  109.8 1.6 copy-start.1
Sparse Core Ops, SparseCore 0:
  9.8 38.9 all-gather.2
  50.9 36.2 all-gather.4

commit v2 on v1

v2 whole, which is shorter than its diff:
```python
import jax
import jax.numpy as jnp
from jax import lax
from jax.experimental import pallas as pl
from jax.experimental.pallas import tpu as pltpu
from jax.sharding import Mesh
from jax.sharding import PartitionSpec as P

HD = 128
GROUP = 4
BLK = 32
PAD = 128
HB = 128
CORES = 2
SPAN = 3
LOG2E = 1.4426950408889634

QROWS = GROUP * BLK
KV_AT = 2 * QROWS
AUX_AT = KV_AT + SPAN * 2 * BLK
AUX_ROWS = 16
ROWS = AUX_AT + AUX_ROWS
UNIT_BLKS = PAD // BLK


def hadamard_signs(table_size):
    index_row = jnp.arange(table_size, dtype=jnp.int32)
    common = jnp.bitwise_and(index_row[:, None], index_row[None, :])
    parity = jnp.zeros((table_size, table_size), jnp.int32)
    for bit_pos in range(table_size.bit_length() - 1):
        parity = parity + jnp.bitwise_and(jnp.right_shift(common, bit_pos), 1)
    return (1 - 2 * jnp.bitwise_and(parity, 1)).astype(jnp.bfloat16)


def pack_kernel(
    order_ref, where_ref, exponent_ref,
    query_ref, grad_ref, key_ref, value_ref, lse_ref, dots_ref, sign_ref, out_ref,
):
    slots = key_ref.shape[0] // BLK
    groups = out_ref.shape[0]
    first = where_ref[0] * slots
    for span in range(1, SPAN):
        for dest in range(span):
            at = KV_AT + span * 2 * BLK
            out_ref[dest, at : at + 2 * BLK, :] = jnp.zeros((2 * BLK, HD), out_ref.dtype)
    signs = sign_ref[...].astype(jnp.float32)
    fixed = [signs]
    for blk in range(sign_ref.shape[0]):
        power = jnp.full((1, HD), jnp.left_shift(jnp.int32(1), exponent_ref[blk]), jnp.int32)
        fixed.append(1.0 / power.astype(jnp.float32))
    fixed.append(jnp.zeros((AUX_ROWS - 6, HD), jnp.float32))
    head_of = lax.broadcasted_iota(jnp.int32, (1, HD), 1) // BLK
    stats = (lse_ref[...].astype(jnp.float32), dots_ref[...].astype(jnp.float32))

    def by_head(array, slot):
        part = slot * BLK // HD * HD
        inner = slot % (HD // BLK)
        row = jnp.zeros((1, HD), jnp.float32)
        for head in range(GROUP):
            line = array[head : head + 1, part : part + HD]
            turn = (head - inner) * BLK % HD
            line = pltpu.roll(line, turn, 1) if turn else line
            row = jnp.where(head_of == head, line, row)
        return row

    for slot in range(slots):
        dest = order_ref[first + slot] // slots
        rows = slice(slot * BLK, (slot + 1) * BLK)
        for head in range(GROUP):
            out_ref[dest, head * BLK : (head + 1) * BLK, :] = query_ref[head, rows, :]
            at = QROWS + head * BLK
            out_ref[dest, at : at + BLK, :] = grad_ref[head, rows, :]
        aux = jnp.concatenate([by_head(array, slot) for array in stats] + fixed, axis=0)
        out_ref[dest, AUX_AT:ROWS, :] = aux.astype(out_ref.dtype)
        key_blk = key_ref[rows, :]
        value_blk = value_ref[rows, :]
        for span in range(SPAN):

            @pl.when(dest + span < groups)
            def _():
                at = KV_AT + span * 2 * BLK
                out_ref[dest + span, at : at + BLK, :] = key_blk
                out_ref[dest + span, at + BLK : at + 2 * BLK, :] = value_blk


def attend_kernel(
    slot_ref, start_ref, recv_ref, out_ref,
    query_scr, grad_scr, query_turned, grad_turned, stat_scr,
    key_scr, value_scr, dkey_scr, dvalue_scr,
):
    groups = recv_ref.shape[0]
    chunk = key_scr.shape[0] // SPAN
    units = chunk // PAD
    width = UNIT_BLKS * QROWS
    pair = 2 * PAD
    dkey_scr[...] = jnp.zeros_like(dkey_scr)
    dvalue_scr[...] = jnp.zeros_like(dvalue_scr)
    for src in range(groups):
        slot = slot_ref[0, src]
        at = pl.multiple_of(slot * QROWS, QROWS)
        query_blk = recv_ref[src, 0:QROWS, :]
        grad_blk = recv_ref[src, QROWS : 2 * QROWS, :]
        query_scr[pl.ds(at, QROWS), :] = query_blk
        grad_scr[pl.ds(at, QROWS), :] = grad_blk
        query_turned[:, pl.ds(at, QROWS)] = query_blk.T
        grad_turned[:, pl.ds(at, QROWS)] = grad_blk.T
        stat_scr[slot] = recv_ref[src, AUX_AT:ROWS, :].astype(jnp.float32)
        for span in range(SPAN):
            row = (SPAN - 1 - span) * chunk + slot_ref[span, src] * BLK
            row = pl.multiple_of(row, BLK)
            at = KV_AT + span * 2 * BLK
            key_scr[pl.ds(row, BLK), :] = recv_ref[src, at : at + BLK, :]
            value_scr[pl.ds(row, BLK), :] = recv_ref[src, at + BLK : at + 2 * BLK, :]

    scale = HD ** (-0.5)
    key_at = lax.broadcasted_iota(jnp.int32, (pair, width), 0)
    column = lax.broadcasted_iota(jnp.int32, (pair, width), 1)
    query_at = (column // QROWS) * BLK + column % BLK
    causal = key_at - PAD <= query_at

    for unit in range(units):
        cols = slice(unit * width, (unit + 1) * width)
        blocks = range(unit * UNIT_BLKS, (unit + 1) * UNIT_BLKS)
        lse = jnp.concatenate([stat_scr[b, 0:1, :] for b in blocks], axis=1) * LOG2E
        dots = jnp.concatenate([stat_scr[b, 1:2, :] for b in blocks], axis=1)

        def visit(row, live):
            rows = pl.ds(row, pair)
            scores = jnp.dot(
                key_scr[rows, :], query_turned[:, cols], preferred_element_type=jnp.float32
            )
            dprobs = jnp.dot(
                value_scr[rows, :], grad_turned[:, cols], preferred_element_type=jnp.float32
            )
            probs = jnp.where(live, jnp.exp2(scores * (scale * LOG2E) - lse), 0.0)
            dscores = (probs * (dprobs - dots)).astype(jnp.bfloat16)
            dvalue_scr[rows, :] += jnp.dot(
                probs.astype(jnp.bfloat16), grad_scr[cols, :], preferred_element_type=jnp.float32
            )
            dkey_scr[rows, :] += jnp.dot(
                dscores, query_scr[cols, :], preferred_element_type=jnp.float32
            )

        first = start_ref[unit]
        last = (SPAN - 1) * units + unit
        visit((last - 1) * PAD, causal & (key_at >= (first - (last - 1)) * PAD))

        @pl.loop(1, (last - first + 2) // 2)
        def _(step):
            base = last - 1 - 2 * step
            visit(pl.multiple_of(base * PAD, PAD), key_at >= (first - base) * PAD)

    for src in range(groups):
        for span in range(SPAN):
            row = (SPAN - 1 - span) * chunk + slot_ref[span, src] * BLK
            row = pl.multiple_of(row, BLK)
            dkey = dkey_scr[pl.ds(row, BLK), :] * scale
            out_ref[src, span, 0:BLK, :] = dkey.astype(out_ref.dtype)
            out_ref[src, span, BLK : 2 * BLK, :] = dvalue_scr[pl.ds(row, BLK), :].astype(
                out_ref.dtype
            )


def collect_kernel(target_ref, recv_ref, out_ref):
    groups = recv_ref.shape[0]
    for slot in range(out_ref.shape[0] // BLK):
        owner = target_ref[slot]
        total = recv_ref[owner, 0].astype(jnp.float32)
        for span in range(1, SPAN):
            extra = recv_ref[jnp.minimum(owner + span, groups - 1), span].astype(jnp.float32)
            total = total + jnp.where(owner + span < groups, extra, 0.0)
        rows = slice(slot * BLK, (slot + 1) * BLK)
        total = total.astype(out_ref.dtype)
        out_ref[rows, 0:HD] = total[0:BLK]
        out_ref[rows, HD : 2 * HD] = total[BLK : 2 * BLK]


def turn_kernel(core_ref, input_ref, own_ref, other_ref):
    span = 2 * HB
    core = core_ref[0]
    for part in range(own_ref.shape[0] // span):
        rows = slice(part * span, (part + 1) * span)
        at = pl.multiple_of((CORES * part + core) * span, span)
        own_ref[rows, :] = input_ref[:, pl.ds(at, span)].T
        at = pl.multiple_of((CORES * part + 1 - core) * span, span)
        other_ref[rows, :] = input_ref[:, pl.ds(at, span)].T


def product_kernel(where_ref, *refs):
    own_refs = refs[: len(refs) // 2 - 2]
    other_refs = refs[len(own_refs) : 2 * len(own_refs)]
    own_kv_ref, other_kv_ref, had_ref, aux_ref, out_ref = refs[2 * len(own_refs) :]
    core, width = where_ref[0], where_ref[1]
    replicas = out_ref.shape[0]
    span = 2 * HB
    parts = own_refs[0].shape[0] // span
    had = had_ref[...].astype(jnp.float32)
    for step, (own_ref, other_ref) in enumerate(zip(own_refs, other_refs)):
        source = (width + len(own_refs) - step) % len(own_refs)
        grad = jnp.dot(own_ref[...], own_kv_ref[...], preferred_element_type=jnp.float32)
        grad += jnp.dot(other_ref[...], other_kv_ref[...], preferred_element_type=jnp.float32)
        for part in range(parts):
            line = source * parts + part
            aux = aux_ref[CORES * line + core].astype(jnp.float32)
            for blk in range(2):
                at = part * span + blk * HB
                rows = grad[at : at + HB]
                table = (had * aux[2 + blk : 3 + blk, :]).astype(jnp.bfloat16)
                high = rows.astype(jnp.bfloat16)
                low = (rows - high.astype(jnp.float32)).astype(jnp.bfloat16)
                rotated = jnp.dot(table, high, preferred_element_type=jnp.float32)
                rotated += jnp.dot(table, low, preferred_element_type=jnp.float32)
                factor = aux[4 + blk : 5 + blk, :] * (HB ** (-0.5))
                rotated *= jnp.concatenate([factor] * (rows.shape[1] // HB), axis=1)
                out_ref[:, line, blk] = rotated.astype(out_ref.dtype).reshape(
                    replicas, HB // replicas, rows.shape[1]
                )


def prefetched(kernel, scalars, out_shape, scratch=()):
    vmem = pl.BlockSpec(memory_space=pltpu.VMEM)

    def call(*operands):
        return pl.pallas_call(
            kernel,
            out_shape=out_shape,
            grid_spec=pltpu.PrefetchScalarGridSpec(
                num_scalar_prefetch=scalars,
                in_specs=[vmem] * (len(operands) - scalars),
                out_specs=jax.tree.map(lambda _: vmem, out_shape),
                scratch_shapes=list(scratch),
            ),
            compiler_params=pltpu.CompilerParams(vmem_limit_bytes=48 << 20),
        )(*operands)

    return call


def gather_ring(own, other):
    count = lax.axis_size("tensor")
    up = [(i, (i + 1) % count) for i in range(count)]
    down = [(i, (i - 1) % count) for i in range(count)]
    own_list = [own, lax.ppermute(own, "tensor", up)]
    own_last = lax.ppermute(own, "tensor", down)
    other_list = [other, lax.ppermute(other, "tensor", up)]
    other_last = lax.ppermute(other, "tensor", down)
    own_list += [lax.ppermute(own_list[1], "tensor", up), own_last]
    other_list += [lax.ppermute(other_last, "tensor", down), other_last]
    return own_list, other_list


def per_device(
    layer_input,
    queries,
    key_states,
    value_states,
    out_grad,
    log_sums,
    grad_dots,
    doc_stretches,
    stretch_order,
    sign_vector,
    exponents,
):
    context = ("y", "core")
    low = jnp.bfloat16
    tokens = queries.shape[2]
    slots = tokens // BLK
    groups = lax.axis_size(context)
    lines = lax.axis_size("y")
    replicas = lax.axis_size("dp")
    order_row = stretch_order[0]
    where = lax.axis_index(context)
    core = lax.axis_index("core")

    packed = prefetched(pack_kernel, 3, jax.ShapeDtypeStruct((groups, ROWS, HD), low))(
        order_row,
        where.reshape(1),
        exponents[0],
        queries[0],
        out_grad[0],
        key_states[0, 0],
        value_states[0, 0],
        log_sums[0],
        grad_dots[0],
        sign_vector,
    )
    packed, layer_input = lax.optimization_barrier((packed, layer_input))
    recv = lax.all_to_all(packed, context, split_axis=0, concat_axis=0, tiled=True)

    half = layer_input.shape[2] // CORES
    turned = jax.ShapeDtypeStruct((half, tokens), low)
    own_input, other_input = prefetched(turn_kernel, 1, (turned, turned))(
        core.reshape(1), layer_input[0]
    )
    swap = [(0, 1), (1, 0)]
    other_input = lax.ppermute(other_input, "core", swap)
    own_list, other_list = gather_ring(own_input, other_input)

    order_grid = order_row.reshape(groups, slots)
    chunk_ids = (where - jnp.arange(SPAN, dtype=jnp.int32))[:, None, None]
    slot_map = jnp.sum(
        jnp.where(order_grid[None] // slots == chunk_ids, order_grid[None] % slots, 0), axis=2
    )
    ends = jnp.cumsum(doc_stretches[0])
    chunk_units = tokens // PAD
    unit_ids = where * chunk_units + jnp.arange(chunk_units, dtype=jnp.int32)
    doc_start = jnp.max(jnp.where(ends[None, :] <= unit_ids[:, None], ends[None, :], 0), axis=1)
    starts = doc_start - (where - (SPAN - 1)) * chunk_units

    window = SPAN * tokens
    partial_grads = prefetched(
        attend_kernel,
        2,
        jax.ShapeDtypeStruct((groups, SPAN, 2 * BLK, HD), low),
        scratch=(
            pltpu.VMEM((slots * QROWS, HD), low),
            pltpu.VMEM((slots * QROWS, HD), low),
            pltpu.VMEM((HD, slots * QROWS), low),
            pltpu.VMEM((HD, slots * QROWS), low),
            pltpu.VMEM((slots, AUX_ROWS, HD), jnp.float32),
            pltpu.VMEM((window, HD), low),
            pltpu.VMEM((window, HD), low),
            pltpu.VMEM((window, HD), jnp.float32),
            pltpu.VMEM((window, HD), jnp.float32),
        ),
    )(slot_map, starts, recv)
    returned = lax.all_to_all(partial_grads, context, split_axis=0, concat_axis=0, tiled=True)
    targets = lax.dynamic_slice_in_dim(order_row, where * slots, slots, 0) // slots
    own_kv = prefetched(collect_kernel, 1, jax.ShapeDtypeStruct((tokens, 2 * HD), low))(
        targets, returned
    )
    other_kv = lax.ppermute(own_kv, "core", swap)

    spread = prefetched(
        product_kernel,
        1,
        jax.ShapeDtypeStruct((replicas, lines, 2, HB // replicas, 2 * HD), low),
    )(
        jnp.stack([core, lax.axis_index("tensor")]),
        *own_list,
        *other_list,
        own_kv,
        other_kv,
        hadamard_signs(HB),
        recv[:, AUX_AT:ROWS],
    )
    spread = spread.reshape(replicas * lines, 2, HB // replicas, 2 * HD)
    shares = lax.all_to_all(spread, ("dp", "y"), split_axis=0, concat_axis=0, tiled=True)
    return jnp.sum(shares.astype(jnp.float32), axis=0)


def solution(mesh):
    replicas, groups, widths = mesh.devices.shape
    split = Mesh(
        mesh.devices.reshape(replicas, groups // CORES, CORES, widths),
        ("dp", "y", "core", "tensor"),
    )
    context = ("y", "core")
    return jax.shard_map(
        per_device,
        mesh=split,
        in_specs=(
            P("dp", context, "tensor"),
            P("dp", "tensor", context, None),
            P("dp", "tensor", context, None),
            P("dp", "tensor", context, None),
            P("dp", "tensor", context, None),
            P("dp", "tensor", context),
            P("dp", "tensor", context),
            P("dp", None),
            P("dp", None),
            P(context, None),
            P("dp", context),
        ),
        out_specs=P(context, "dp", "tensor"),
        check_vma=False,
    )
```

time: 170 us -> 174 us (1.024)
  starting transfers between devices: 22.9 us -> 39.8 us
  between operations: 13.6 us -> 0.21 us
  Pallas kernels: 15.2 us -> 13.1 us
  waiting for transfers between devices: 61.5 us -> 63.4 us
    all_to_all x1, waiting for transfers between devices: 20.6 us -> 0.01 us  [per_device(): lax.all_to_all(partial_grads, context, split_axis=0, concat_axis=0, tiled...]
    ppermute x2 -> x8, starting transfers between devices: 6.61 us -> 24.7 us  [the longest x1 5.39 us: gather_ring(): own_list += [lax.ppermute(own_list[1], 'tensor', up), own_last]]
    ppermute x2 -> x8, waiting for transfers between devices: 2.53 us -> 20.4 us  [the longest x1 6.44 us: gather_ring(): own_last = lax.ppermute(own, 'tensor', down)]
    all_to_all x1, waiting for transfers between devices: 38.3 us -> 43.1 us  [per_device(): lax.all_to_all(packed, context, split_axis=0, concat_axis=0, tiled=True)]
    unnamed x27, local copies, waits for them, and re-layouts: 6.95 us -> 10.3 us
    pallas_call x5, Pallas kernels: 15.2 us -> 13.1 us  [call(): pl.pallas_call(kernel, out_shape=out_shape, grid_spec=pltpu.PrefetchScala...]
  transfers between devices with their start and end apart: 6 -> 10, of which waited for: 4 -> 6; matrix products, arithmetic and copies ran while one was open for 3% -> 1% of each run, Pallas kernels for 4% -> 1%
where the time goes in v2:
time: 174 us; the launch traced here: 173 us
  waiting for transfers between devices  63.4 us (36%)
  blocking collectives  43.5 us (25%)
  starting transfers between devices  39.8 us (23%)
  Pallas kernels  13.1 us (8%)
  local copies, waits for them, and re-layouts  10.4 us (6%)
  other arithmetic  2.24 us (1%)
    all_to_all x1, blocking collectives, per_device(): lax.all_to_all(spread, ('dp', 'y'), split_axis=0, concat_axis=0, tiled=True)  43.5 us
    all_to_all x1, waiting for transfers between devices, per_device(): lax.all_to_all(packed, context, split_axis=0, concat_axis=0, tiled=True)  43.1 us
    pallas_call x5, Pallas kernels, call(): pl.pallas_call(kernel, out_shape=out_shape, grid_spec=pltpu.PrefetchScala...  13.1 us
    unnamed x27, local copies, waits for them, and re-layouts  10.3 us
    all_to_all x1, starting transfers between devices, per_device(): lax.all_to_all(partial_grads, context, split_axis=0, concat_axis=0, tiled...  7.75 us
    all_to_all x1, starting transfers between devices, per_device(): lax.all_to_all(packed, context, split_axis=0, concat_axis=0, tiled=True)  7.34 us
    ppermute x1, waiting for transfers between devices, gather_ring(): own_last = lax.ppermute(own, 'tensor', down)  6.44 us
    ppermute x1, starting transfers between devices, gather_ring(): own_list += [lax.ppermute(own_list[1], 'tensor', up), own_last]  5.39 us
  transfers between devices with their start and end apart: 10, of which 6 were waited for; matrix products, arithmetic and copies ran while one was open for 1% of the time, Pallas kernels for 1%

profile of v2, /device:TPU:6, one launch (start us, length us, event | category | flops | bytes accessed | tf_op | source)
XLA Modules:
  0.0 172.8 jit_solution(204782343505832323)
XLA Ops:
  0.0 1.0 copy-done.2
  1.0 1.0 copy-done.3
  2.1 0.9 copy-done.4
  7.3 1.9 %shard_map.109 = bf16[16,464,128]{2,1,0:T(8,128)(2,1)S(1)} custom-call(s32[256]{0:T(256)S(1)} %bitcast.31, s32[1]{0:T(128)} %bitcast.3.where_ref, s32[2]{0:T(128)S(1)} %bitcast.32, bf16[4,512,128]{2,1,0:T(8,128)(2,1)S(1)} %bitcast.25, bf16[4,512,128]{2,1,0:T(8,128)(2,1)S(1)} %bitcast.26, bf16[512,128]{1,0:T(8,128)(2,1)S(1)} %bitcast.27, ...), custom_call_target="tpu_custom_call" | custom-call | tf_op jit(solution)/shard_map/pallas_call | solution.py:224
  9.2 1.3 copy-done
  10.4 7.3 %all-to-all-start = ((bf16[16,464,128]{2,1,0:T(8,128)(2,1)}), bf16[16,464,128]{2,1,0:T(8,128)(2,1)S(1)}, u32[]{:S(2)}, u32[]{:S(2)}) async-start(bf16[16,464,128]{2,1,0:T(8,128)(2,1)} %copy-done), calls=%async_computation | async-start | bytes 3801088 | tf_op jit(solution)/shard_map/all_to_all | solution.py:289
  19.7 43.1 %all-to-all-done.recv_ref = bf16[16,464,128]{2,1,0:T(8,128)(2,1)S(1)} async-done(((bf16[16,464,128]{2,1,0:T(8,128)(2,1)}), bf16[16,464,128]{2,1,0:T(8,128)(2,1)S(1)}, u32[]{:S(2)}, u32[]{:S(2)}) %all-to-all-start) | async-done | bytes 1900576 | tf_op jit(solution)/shard_map/all_to_all | solution.py:289
  62.8 4.6 %shard_map.111 = bf16[16,3,64,128]{3,2,1,0:T(8,128)(2,1)} custom-call(s32[3,16]{1,0:T(4,128)S(1)} %select_reduce_fusion.slot_ref, s32[4]{0:T(128)S(1)} %broadcast_subtract_fusion.start_ref, bf16[16,464,128]{2,1,0:T(8,128)(2,1)S(1)} %all-to-all-done.recv_ref), custom_call_target="tpu_custom_call" | custom-call | tf_op jit(solution)/shard_map/pallas_call | solution.py:224
  67.3 7.8 %all-to-all-start.1 = ((bf16[16,3,64,128]{3,2,1,0:T(8,128)(2,1)}), bf16[16,3,64,128]{3,2,1,0:T(8,128)(2,1)S(1)}, u32[]{:S(2)}, u32[]{:S(2)}) async-start(bf16[16,3,64,128]{3,2,1,0:T(8,128)(2,1)} %shard_map.111), calls=%async_computation.1 | async-start | bytes 1572864 | tf_op jit(solution)/shard_map/all_to_all | solution.py:328
  75.1 1.2 copy-done.1
  76.6 2.3 %collective-permute-start.3 = (bf16[512,512]{1,0:T(8,128)(2,1)S(1)}, bf16[512,512]{1,0:T(8,128)(2,1)}, u32[]{:S(2)}, u32[]{:S(2)}) collective-permute-start(bf16[512,512]{1,0:T(8,128)(2,1)S(1)} %get-tuple-element.11), channel_id=1, source_target_pairs={{0,4},{4,0},{1,5},{5,1},{2,6},{6,2},{3,7},{7,3},{8,12},{12,8},{9,1... | collective-permute-start | bytes 1572872 | tf_op jit(solution)/shard_map/ppermute | solution.py:297
  79.0 4.2 %collective-permute-start = (bf16[512,512]{1,0:T(8,128)(2,1)S(1)}, bf16[512,512]{1,0:T(8,128)(2,1)}, u32[]{:S(2)}, u32[]{:S(2)}) collective-permute-start(bf16[512,512]{1,0:T(8,128)(2,1)S(1)} %get-tuple-element.10.refs_0_), channel_id=1, source_target_pairs={{0,1},{1,2},{2,3},{3,0},{4,5},{5,6},{6,7},{7,4},{8,9},{9,10},{10,1... | collective-permute-start | bytes 1572872 | tf_op jit(solution)/shard_map/ppermute | solution.py:243
  83.2 1.9 %collective-permute-start.5 = (bf16[512,512]{1,0:T(8,128)(2,1)}, bf16[512,512]{1,0:T(8,128)(2,1)}, u32[]{:S(2)}, u32[]{:S(2)}) collective-permute-start(bf16[512,512]{1,0:T(8,128)(2,1)} %collective-permute-done.3.refs_4_), channel_id=1, source_target_pairs={{0,3},{1,0},{2,1},{3,2},{4,7},{5,4},{6,5},{7,6},{8,11},{9,8},{10,9... | collective-permute-start | bytes 1572872 | tf_op jit(solution)/shard_map/ppermute | solution.py:246
  85.1 2.5 %collective-permute-start.2 = (bf16[512,512]{1,0:T(8,128)(2,1)S(1)}, bf16[512,512]{1,0:T(8,128)(2,1)}, u32[]{:S(2)}, u32[]{:S(2)}) collective-permute-start(bf16[512,512]{1,0:T(8,128)(2,1)S(1)} %get-tuple-element.10.refs_0_), channel_id=1, source_target_pairs={{0,3},{1,0},{2,1},{3,2},{4,7},{5,4},{6,5},{7,6},{8,11},{9,8},{10,9... | collective-permute-start | bytes 1572872 | tf_op jit(solution)/shard_map/ppermute | solution.py:244
  87.6 4.6 %collective-permute-start.4 = (bf16[512,512]{1,0:T(8,128)(2,1)}, bf16[512,512]{1,0:T(8,128)(2,1)}, u32[]{:S(2)}, u32[]{:S(2)}) collective-permute-start(bf16[512,512]{1,0:T(8,128)(2,1)} %collective-permute-done.3.refs_4_), channel_id=1, source_target_pairs={{0,1},{1,2},{2,3},{3,0},{4,5},{5,6},{6,7},{7,4},{8,9},{9,10},{10,1... | collective-permute-start | bytes 1572872 | tf_op jit(solution)/shard_map/ppermute | solution.py:245
  92.2 3.6 %collective-permute-done.refs_1_ = bf16[512,512]{1,0:T(8,128)(2,1)} collective-permute-done((bf16[512,512]{1,0:T(8,128)(2,1)S(1)}, bf16[512,512]{1,0:T(8,128)(2,1)}, u32[]{:S(2)}, u32[]{:S(2)}) %collective-permute-start) | collective-permute-done | bytes 524320 | tf_op jit(solution)/shard_map/ppermute | solution.py:243
  95.7 5.4 %collective-permute-start.1 = (bf16[512,512]{1,0:T(8,128)(2,1)}, bf16[512,512]{1,0:T(8,128)(2,1)}, u32[]{:S(2)}, u32[]{:S(2)}) collective-permute-start(bf16[512,512]{1,0:T(8,128)(2,1)} %collective-permute-done.refs_1_), channel_id=1, source_target_pairs={{0,1},{1,2},{2,3},{3,0},{4,5},{5,6},{6,7},{7,4},{8,9},{9,10},{10,1... | collective-permute-start | bytes 1572872 | tf_op jit(solution)/shard_map/ppermute | solution.py:247
  101.4 1.9 %collective-permute-start.6 = (bf16[512,512]{1,0:T(8,128)(2,1)}, bf16[512,512]{1,0:T(8,128)(2,1)}, u32[]{:S(2)}, u32[]{:S(2)}) collective-permute-start(bf16[512,512]{1,0:T(8,128)(2,1)} %collective-permute-done.5.refs_7_), channel_id=1, source_target_pairs={{0,3},{1,0},{2,1},{3,2},{4,7},{5,4},{6,5},{7,6},{8,11},{9,8},{10,9... | collective-permute-start | bytes 1572872 | tf_op jit(solution)/shard_map/ppermute | solution.py:248
  104.1 1.9 %collective-permute-start.7 = (bf16[512,256]{1,0:T(8,128)(2,1)S(1)}, bf16[512,256]{1,0:T(8,128)(2,1)S(1)}, u32[]{:S(2)}, u32[]{:S(2)}) collective-permute-start(bf16[512,256]{1,0:T(8,128)(2,1)S(1)} %shard_map.112.refs_8_), channel_id=1, source_target_pairs={{0,4},{4,0},{1,5},{5,1},{2,6},{6,2},{3,7},{7,3},{8,12},{12,8},{9,1... | collective-permute-start | bytes 786440 | tf_op jit(solution)/shard_map/ppermute | solution.py:333
  106.2 6.4 %collective-permute-done.2.refs_3_ = bf16[512,512]{1,0:T(8,128)(2,1)} collective-permute-done((bf16[512,512]{1,0:T(8,128)(2,1)S(1)}, bf16[512,512]{1,0:T(8,128)(2,1)}, u32[]{:S(2)}, u32[]{:S(2)}) %collective-permute-start.2) | collective-permute-done | bytes 524320 | tf_op jit(solution)/shard_map/ppermute | solution.py:244
  112.6 4.7 %collective-permute-done.1.refs_2_ = bf16[512,512]{1,0:T(8,128)(2,1)} collective-permute-done((bf16[512,512]{1,0:T(8,128)(2,1)}, bf16[512,512]{1,0:T(8,128)(2,1)}, u32[]{:S(2)}, u32[]{:S(2)}) %collective-permute-start.1) | collective-permute-done | bytes 524320 | tf_op jit(solution)/shard_map/ppermute | solution.py:247
  117.4 5.3 %collective-permute-done.6.refs_6_ = bf16[512,512]{1,0:T(8,128)(2,1)} collective-permute-done((bf16[512,512]{1,0:T(8,128)(2,1)}, bf16[512,512]{1,0:T(8,128)(2,1)}, u32[]{:S(2)}, u32[]{:S(2)}) %collective-permute-start.6) | collective-permute-done | bytes 524320 | tf_op jit(solution)/shard_map/ppermute | solution.py:248
  122.7 5.7 %shard_map.113 = bf16[8,8,2,16,256]{4,3,2,1,0:T(8,128)(2,1)S(1)} custom-call(s32[2]{0:T(128)S(1)} %pad_add_fusion.where_ref, bf16[512,512]{1,0:T(8,128)(2,1)S(1)} %get-tuple-element.10.refs_0_, bf16[512,512]{1,0:T(8,128)(2,1)} %collective-permute-done.refs_1_, bf16[512,512]{1,0:T(8,128)(2,1)} %collective-permute-done.1.refs_2_, ...), custom_call_target="tpu_custom_call" | custom-call | tf_op jit(solution)/shard_map/pallas_call | solution.py:224
  128.4 43.5 %all_to_all.15 = bf16[64,2,16,256]{3,2,1,0:T(8,128)(2,1)S(1)} all-to-all(bf16[64,2,16,256]{3,2,1,0:T(8,128)(2,1)S(1)} %bitcast.23), channel_id=1, replica_groups=mesh['dp'=8,'y'=8,'core'=2,'tensor'=4] {'dp','y'}, dimensions={0} | all-to-all | bytes 2097152 | tf_op jit(solution)/shard_map/all_to_all | solution.py:349
  (43 shorter events, 8.5 us)
Async XLA Ops:
  0.0 1.0 copy-start.2
  1.0 1.0 copy-start.3
  2.1 0.9 copy-start.4
  3.0 0.9 copy-start.5
  3.9 0.7 copy-start.6
  4.6 0.7 copy-start.7
  5.3 0.7 copy-start.8
  5.9 0.7 copy-start.10
  6.6 0.7 copy-start.11
  9.1 1.3 copy-start
  10.4 7.4 %copy-start.12 = (s32[1,10]{1,0:T(1,128)S(1)}, s32[1,10]{1,0:T(1,128)}, u32[]{:S(2)}) copy-start(s32[1,10]{1,0:T(1,128)} %param.18) | copy-start | bytes 124
  10.4 8.1 %copy-start.9 = (s32[1,256]{1,0:T(1,128)S(1)}, s32[1,256]{1,0:T(1,128)}, u32[]{:S(2)}) copy-start(s32[1,256]{1,0:T(1,128)} %param.19) | copy-start | bytes 3076
  10.4 52.3 %all-to-all-start = ((bf16[16,464,128]{2,1,0:T(8,128)(2,1)}), bf16[16,464,128]{2,1,0:T(8,128)(2,1)S(1)}, u32[]{:S(2)}, u32[]{:S(2)}) async-start(bf16[16,464,128]{2,1,0:T(8,128)(2,1)} %copy-done), calls=%async_computation | async-start | bytes 3801088 | tf_op jit(solution)/shard_map/all_to_all | solution.py:289
  67.3 36.1 %all-to-all-start.1 = ((bf16[16,3,64,128]{3,2,1,0:T(8,128)(2,1)}), bf16[16,3,64,128]{3,2,1,0:T(8,128)(2,1)S(1)}, u32[]{:S(2)}, u32[]{:S(2)}) async-start(bf16[16,3,64,128]{3,2,1,0:T(8,128)(2,1)} %shard_map.111), calls=%async_computation.1 | async-start | bytes 1572864 | tf_op jit(solution)/shard_map/all_to_all | solution.py:328
  75.1 1.2 copy-start.1
  76.6 6.5 %collective-permute-start.3 = (bf16[512,512]{1,0:T(8,128)(2,1)S(1)}, bf16[512,512]{1,0:T(8,128)(2,1)}, u32[]{:S(2)}, u32[]{:S(2)}) collective-permute-start(bf16[512,512]{1,0:T(8,128)(2,1)S(1)} %get-tuple-element.11), channel_id=1, source_target_pairs={{0,4},{4,0},{1,5},{5,1},{2,6},{6,2},{3,7},{7,3},{8,12},{12,8},{9,1... | collective-permute-start | bytes 1572872 | tf_op jit(solution)/shard_map/ppermute | solution.py:297
  79.0 16.8 %collective-permute-start = (bf16[512,512]{1,0:T(8,128)(2,1)S(1)}, bf16[512,512]{1,0:T(8,128)(2,1)}, u32[]{:S(2)}, u32[]{:S(2)}) collective-permute-start(bf16[512,512]{1,0:T(8,128)(2,1)S(1)} %get-tuple-element.10.refs_0_), channel_id=1, source_target_pairs={{0,1},{1,2},{2,3},{3,0},{4,5},{5,6},{6,7},{7,4},{8,9},{9,10},{10,1... | collective-permute-start | bytes 1572872 | tf_op jit(solution)/shard_map/ppermute | solution.py:243
  83.2 18.2 %collective-permute-start.5 = (bf16[512,512]{1,0:T(8,128)(2,1)}, bf16[512,512]{1,0:T(8,128)(2,1)}, u32[]{:S(2)}, u32[]{:S(2)}) collective-permute-start(bf16[512,512]{1,0:T(8,128)(2,1)} %collective-permute-done.3.refs_4_), channel_id=1, source_target_pairs={{0,3},{1,0},{2,1},{3,2},{4,7},{5,4},{6,5},{7,6},{8,11},{9,8},{10,9... | collective-permute-start | bytes 1572872 | tf_op jit(solution)/shard_map/ppermute | solution.py:246
  85.1 27.5 %collective-permute-start.2 = (bf16[512,512]{1,0:T(8,128)(2,1)S(1)}, bf16[512,512]{1,0:T(8,128)(2,1)}, u32[]{:S(2)}, u32[]{:S(2)}) collective-permute-start(bf16[512,512]{1,0:T(8,128)(2,1)S(1)} %get-tuple-element.10.refs_0_), channel_id=1, source_target_pairs={{0,3},{1,0},{2,1},{3,2},{4,7},{5,4},{6,5},{7,6},{8,11},{9,8},{10,9... | collective-permute-start | bytes 1572872 | tf_op jit(solution)/shard_map/ppermute | solution.py:244
  87.6 25.1 %collective-permute-start.4 = (bf16[512,512]{1,0:T(8,128)(2,1)}, bf16[512,512]{1,0:T(8,128)(2,1)}, u32[]{:S(2)}, u32[]{:S(2)}) collective-permute-start(bf16[512,512]{1,0:T(8,128)(2,1)} %collective-permute-done.3.refs_4_), channel_id=1, source_target_pairs={{0,1},{1,2},{2,3},{3,0},{4,5},{5,6},{6,7},{7,4},{8,9},{9,10},{10,1... | collective-permute-start | bytes 1572872 | tf_op jit(solution)/shard_map/ppermute | solution.py:245
  95.7 21.6 %collective-permute-start.1 = (bf16[512,512]{1,0:T(8,128)(2,1)}, bf16[512,512]{1,0:T(8,128)(2,1)}, u32[]{:S(2)}, u32[]{:S(2)}) collective-permute-start(bf16[512,512]{1,0:T(8,128)(2,1)} %collective-permute-done.refs_1_), channel_id=1, source_target_pairs={{0,1},{1,2},{2,3},{3,0},{4,5},{5,6},{6,7},{7,4},{8,9},{9,10},{10,1... | collective-permute-start | bytes 1572872 | tf_op jit(solution)/shard_map/ppermute | solution.py:247
  101.4 21.3 %collective-permute-start.6 = (bf16[512,512]{1,0:T(8,128)(2,1)}, bf16[512,512]{1,0:T(8,128)(2,1)}, u32[]{:S(2)}, u32[]{:S(2)}) collective-permute-start(bf16[512,512]{1,0:T(8,128)(2,1)} %collective-permute-done.5.refs_7_), channel_id=1, source_target_pairs={{0,3},{1,0},{2,1},{3,2},{4,7},{5,4},{6,5},{7,6},{8,11},{9,8},{10,9... | collective-permute-start | bytes 1572872 | tf_op jit(solution)/shard_map/ppermute | solution.py:248
  104.1 18.6 %collective-permute-start.7 = (bf16[512,256]{1,0:T(8,128)(2,1)S(1)}, bf16[512,256]{1,0:T(8,128)(2,1)S(1)}, u32[]{:S(2)}, u32[]{:S(2)}) collective-permute-start(bf16[512,256]{1,0:T(8,128)(2,1)S(1)} %shard_map.112.refs_8_), channel_id=1, source_target_pairs={{0,4},{4,0},{1,5},{5,1},{2,6},{6,2},{3,7},{7,3},{8,12},{12,8},{9,1... | collective-permute-start | bytes 786440 | tf_op jit(solution)/shard_map/ppermute | solution.py:333

commit v3 on v2

--- a/solution.py
+++ b/solution.py
@@ -32,25 +32,36 @@
     return (1 - 2 * jnp.bitwise_and(parity, 1)).astype(jnp.bfloat16)
 
 
-def pack_kernel(
-    order_ref, where_ref, exponent_ref,
-    query_ref, grad_ref, key_ref, value_ref, lse_ref, dots_ref, sign_ref, out_ref,
-):
-    slots = key_ref.shape[0] // BLK
+def pack_kernel(where_ref, *refs):
+    (query_ref, grad_ref, key_ref, value_ref, lse_ref, dots_ref, sign_ref), refs = refs[:7], refs[7:]
+    order_ref, exponent_ref, out_ref = refs[:3]
+    query_scr, grad_scr, key_scr, value_scr, lse_scr, dots_scr, sign_scr = refs[3:10]
+    order_scr, exponent_scr, held_scr, aux_scr, packed_scr, in_sem, out_sem = refs[10:]
+    sources = (order_ref, exponent_ref, lse_ref, dots_ref, sign_ref)
+    sources += (key_ref, value_ref, query_ref, grad_ref)
+    places = (order_scr, exponent_scr, lse_scr, dots_scr, sign_scr)
+    places += (key_scr, value_scr, query_scr, grad_scr)
+    loads = [
+        pltpu.make_async_copy(source, place, in_sem.at[i])
+        for i, (source, place) in enumerate(zip(sources, places))
+    ]
+    for load in loads:
+        load.start()
     groups = out_ref.shape[0]
+    slots = key_ref.shape[2] // BLK
+    for load in loads[:5]:
+        load.wait()
     first = where_ref[0] * slots
-    for span in range(1, SPAN):
-        for dest in range(span):
-            at = KV_AT + span * 2 * BLK
-            out_ref[dest, at : at + 2 * BLK, :] = jnp.zeros((2 * BLK, HD), out_ref.dtype)
-    signs = sign_ref[...].astype(jnp.float32)
-    fixed = [signs]
+    for slot in range(slots):
+        held_scr[order_scr[0, first + slot] // slots] = slot
+
+    fixed = [sign_scr[...].astype(jnp.float32)]
     for blk in range(sign_ref.shape[0]):
-        power = jnp.full((1, HD), jnp.left_shift(jnp.int32(1), exponent_ref[blk]), jnp.int32)
+        power = jnp.full((1, HD), jnp.left_shift(jnp.int32(1), exponent_scr[0, blk]), jnp.int32)
         fixed.append(1.0 / power.astype(jnp.float32))
     fixed.append(jnp.zeros((AUX_ROWS - 6, HD), jnp.float32))
     head_of = lax.broadcasted_iota(jnp.int32, (1, HD), 1) // BLK
-    stats = (lse_ref[...].astype(jnp.float32), dots_ref[...].astype(jnp.float32))
+    stats = (lse_scr[0].astype(jnp.float32), dots_scr[0].astype(jnp.float32))
 
     def by_head(array, slot):
         part = slot * BLK // HD * HD
@@ -64,23 +75,32 @@
         return row
 
     for slot in range(slots):
-        dest = order_ref[first + slot] // slots
-        rows = slice(slot * BLK, (slot + 1) * BLK)
+        aux = jnp.concatenate([by_head(array, slot) for array in stats] + fixed, axis=0)
+        aux_scr[slot] = aux.astype(aux_scr.dtype)
+    for load in loads[5:]:
+        load.wait()
+
+    stores = []
+    for dest in range(groups):
+        slot = held_scr[dest]
+        rows = pl.ds(pl.multiple_of(slot * BLK, BLK), BLK)
         for head in range(GROUP):
-            out_ref[dest, head * BLK : (head + 1) * BLK, :] = query_ref[head, rows, :]
+            packed_scr[dest, head * BLK : (head + 1) * BLK, :] = query_scr[0, head, rows, :]
             at = QROWS + head * BLK
-            out_ref[dest, at : at + BLK, :] = grad_ref[head, rows, :]
-        aux = jnp.concatenate([by_head(array, slot) for array in stats] + fixed, axis=0)
-        out_ref[dest, AUX_AT:ROWS, :] = aux.astype(out_ref.dtype)
-        key_blk = key_ref[rows, :]
-        value_blk = value_ref[rows, :]
+            packed_scr[dest, at : at + BLK, :] = grad_scr[0, head, rows, :]
         for span in range(SPAN):
-
-            @pl.when(dest + span < groups)
-            def _():
-                at = KV_AT + span * 2 * BLK
-                out_ref[dest + span, at : at + BLK, :] = key_blk
-                out_ref[dest + span, at + BLK : at + 2 * BLK, :] = value_blk
+            at = KV_AT + span * 2 * BLK
+            if dest >= span:
+                rows = pl.ds(pl.multiple_of(held_scr[dest - span] * BLK, BLK), BLK)
+                packed_scr[dest, at : at + BLK, :] = key_scr[0, 0, rows, :]
+                packed_scr[dest, at + BLK : at + 2 * BLK, :] = value_scr[0, 0, rows, :]
+            else:
+                packed_scr[dest, at : at + 2 * BLK, :] = jnp.zeros((2 * BLK, HD), out_ref.dtype)
+        packed_scr[dest, AUX_AT:ROWS, :] = aux_scr[slot]
+        stores.append(pltpu.make_async_copy(packed_scr.at[dest], out_ref.at[dest], out_sem.at[dest]))
+        stores[-1].start()
+    for store in stores:
+        store.wait()
 
 
 def attend_kernel(
@@ -186,30 +206,48 @@
         other_ref[rows, :] = input_ref[:, pl.ds(at, span)].T
 
 
+def load_all(sources, places, sems):
+    loads = [
+        pltpu.make_async_copy(source, places.at[i], sems.at[i]) for i, source in enumerate(sources)
+    ]
+    for load in loads:
+        load.start()
+    return loads
+
+
+def first_product_kernel(*refs):
+    kv_ref, out_ref, input_scr, sems = refs[-4:]
+    for step, load in enumerate(load_all(refs[:-4], input_scr, sems)):
+        load.wait()
+        out_ref[step] = jnp.dot(input_scr[step], kv_ref[...], preferred_element_type=jnp.float32)
+
+
 def product_kernel(where_ref, *refs):
-    own_refs = refs[: len(refs) // 2 - 2]
-    other_refs = refs[len(own_refs) : 2 * len(own_refs)]
-    own_kv_ref, other_kv_ref, had_ref, aux_ref, out_ref = refs[2 * len(own_refs) :]
+    other_refs = refs[:-7]
+    first_ref, kv_ref, had_ref, aux_ref, out_ref, input_scr, sems = refs[-7:]
+    loads = load_all(other_refs, input_scr, sems)
     core, width = where_ref[0], where_ref[1]
     replicas = out_ref.shape[0]
     span = 2 * HB
-    parts = own_refs[0].shape[0] // span
-    had = had_ref[...].astype(jnp.float32)
-    for step, (own_ref, other_ref) in enumerate(zip(own_refs, other_refs)):
-        source = (width + len(own_refs) - step) % len(own_refs)
-        grad = jnp.dot(own_ref[...], own_kv_ref[...], preferred_element_type=jnp.float32)
-        grad += jnp.dot(other_ref[...], other_kv_ref[...], preferred_element_type=jnp.float32)
+    parts = input_scr.shape[1] // span
+    had = jnp.concatenate([had_ref[...].astype(jnp.float32)] * 2, axis=1)
+    for step, load in enumerate(loads):
+        source = (width + len(loads) - step) % len(loads)
+        load.wait()
+        grad = jnp.dot(input_scr[step], kv_ref[...], preferred_element_type=jnp.float32)
+        grad = grad + first_ref[step]
         for part in range(parts):
             line = source * parts + part
             aux = aux_ref[CORES * line + core].astype(jnp.float32)
             for blk in range(2):
                 at = part * span + blk * HB
                 rows = grad[at : at + HB]
-                table = (had * aux[2 + blk : 3 + blk, :]).astype(jnp.bfloat16)
+                sign = aux[2 + blk : 3 + blk, :]
+                table = (had * jnp.concatenate([sign, sign], axis=1)).astype(jnp.bfloat16)
                 high = rows.astype(jnp.bfloat16)
                 low = (rows - high.astype(jnp.float32)).astype(jnp.bfloat16)
-                rotated = jnp.dot(table, high, preferred_element_type=jnp.float32)
-                rotated += jnp.dot(table, low, preferred_element_type=jnp.float32)
+                both = jnp.concatenate([high, low], axis=0)
+                rotated = jnp.dot(table, both, preferred_element_type=jnp.float32)
                 factor = aux[4 + blk : 5 + blk, :] * (HB ** (-0.5))
                 rotated *= jnp.concatenate([factor] * (rows.shape[1] // HB), axis=1)
                 out_ref[:, line, blk] = rotated.astype(out_ref.dtype).reshape(
@@ -217,21 +255,28 @@
                 )
 
 
-def prefetched(kernel, scalars, out_shape, scratch=()):
+def prefetched(kernel, scalars, out_shape, scratch=(), in_place=0, out_space=pltpu.VMEM):
     vmem = pl.BlockSpec(memory_space=pltpu.VMEM)
+    hbm = pl.BlockSpec(memory_space=pltpu.HBM)
+    out_spec = pl.BlockSpec(memory_space=out_space)
 
     def call(*operands):
+        held = scalars + in_place
+        kept = [
+            pltpu.with_memory_space_constraint(array, pltpu.HBM)
+            for array in operands[scalars:held]
+        ]
         return pl.pallas_call(
             kernel,
             out_shape=out_shape,
             grid_spec=pltpu.PrefetchScalarGridSpec(
                 num_scalar_prefetch=scalars,
-                in_specs=[vmem] * (len(operands) - scalars),
-                out_specs=jax.tree.map(lambda _: vmem, out_shape),
+                in_specs=[hbm] * in_place + [vmem] * (len(operands) - held),
+                out_specs=jax.tree.map(lambda _: out_spec, out_shape),
                 scratch_shapes=list(scratch),
             ),
-            compiler_params=pltpu.CompilerParams(vmem_limit_bytes=48 << 20),
-        )(*operands)
+            compiler_params=pltpu.CompilerParams(vmem_limit_bytes=16 << 20),
+        )(*operands[:scalars], *kept, *operands[held:])
 
     return call
 
@@ -273,18 +318,24 @@
     where = lax.axis_index(context)
     core = lax.axis_index("core")
 
-    packed = prefetched(pack_kernel, 3, jax.ShapeDtypeStruct((groups, ROWS, HD), low))(
-        order_row,
-        where.reshape(1),
-        exponents[0],
-        queries[0],
-        out_grad[0],
-        key_states[0, 0],
-        value_states[0, 0],
-        log_sums[0],
-        grad_dots[0],
-        sign_vector,
-    )
+    raw = (queries, out_grad, key_states, value_states, log_sums, grad_dots, sign_vector)
+    packed = prefetched(
+        pack_kernel,
+        1,
+        pltpu.HBM((groups, ROWS, HD), low),
+        scratch=(
+            *(pltpu.VMEM(array.shape, array.dtype) for array in raw),
+            pltpu.SMEM(stretch_order.shape, jnp.int32),
+            pltpu.SMEM(exponents.shape, jnp.int32),
+            pltpu.SMEM((groups,), jnp.int32),
+            pltpu.VMEM((slots, AUX_ROWS, HD), low),
+            pltpu.VMEM((groups, ROWS, HD), low),
+            pltpu.SemaphoreType.DMA((9,)),
+            pltpu.SemaphoreType.DMA((groups,)),
+        ),
+        in_place=len(raw) + 2,
+        out_space=pltpu.HBM,
+    )(where.reshape(1), *raw, stretch_order, exponents)
     packed, layer_input = lax.optimization_barrier((packed, layer_input))
     recv = lax.all_to_all(packed, context, split_axis=0, concat_axis=0, tiled=True)
 
@@ -296,6 +347,7 @@
     swap = [(0, 1), (1, 0)]
     other_input = lax.ppermute(other_input, "core", swap)
     own_list, other_list = gather_ring(own_input, other_input)
+    recv, own_list, other_list = lax.optimization_barrier((recv, own_list, other_list))
 
     order_grid = order_row.reshape(groups, slots)
     chunk_ids = (where - jnp.arange(SPAN, dtype=jnp.int32))[:, None, None]
@@ -332,15 +384,27 @@
     )
     other_kv = lax.ppermute(own_kv, "core", swap)
 
+    input_scratch = (
+        pltpu.VMEM((len(own_list), half, tokens), low),
+        pltpu.SemaphoreType.DMA((len(own_list),)),
+    )
+    first_product = prefetched(
+        first_product_kernel,
+        0,
+        jax.ShapeDtypeStruct((len(own_list), half, 2 * HD), jnp.float32),
+        scratch=input_scratch,
+        in_place=len(own_list),
+    )(*own_list, own_kv)
     spread = prefetched(
         product_kernel,
         1,
         jax.ShapeDtypeStruct((replicas, lines, 2, HB // replicas, 2 * HD), low),
+        scratch=input_scratch,
+        in_place=len(other_list),
     )(
         jnp.stack([core, lax.axis_index("tensor")]),
-        *own_list,
         *other_list,
-        own_kv,
+        first_product,
         other_kv,
         hadamard_signs(HB),
         recv[:, AUX_AT:ROWS],

time: 174 us -> 145 us (0.83)
  waiting for transfers between devices: 63.4 us -> 41.1 us
  local copies, waits for them, and re-layouts: 10.4 us -> 1.45 us
  Pallas kernels: 13.1 us -> 15.6 us
  starting transfers between devices: 39.8 us -> 42.3 us
  blocking collectives: 43.5 us -> 41.4 us
    all_to_all x1, waiting for transfers between devices: 43.1 us -> 0.01 us  [per_device(): lax.all_to_all(packed, context, split_axis=0, concat_axis=0, tiled=True)]
    all_to_all x1, waiting for transfers between devices: 0.01 us -> 20.6 us  [per_device(): lax.all_to_all(partial_grads, context, split_axis=0, concat_axis=0, tiled...]
    unnamed x27 -> x17, local copies, waits for them, and re-layouts: 10.3 us -> 1.36 us
    pallas_call x5 -> x6, Pallas kernels: 13.1 us -> 15.6 us  [call(): pl.pallas_call(kernel, out_shape=out_shape, grid_spec=pltpu.PrefetchScala...]
    ppermute x1, waiting for transfers between devices: 6.44 us -> 8.93 us  [gather_ring(): own_last = lax.ppermute(own, 'tensor', down)]
    ppermute x1, starting transfers between devices: 1.92 us -> 4.29 us  [per_device(): other_kv = lax.ppermute(own_kv, 'core', swap)]
    all_to_all x1, blocking collectives: 43.5 us -> 41.4 us  [per_device(): lax.all_to_all(spread, ('dp', 'y'), split_axis=0, concat_axis=0, tiled=True)]
  transfers between devices with their start and end apart: 10 -> 10, of which waited for: 6 -> 5; matrix products, arithmetic and copies ran while one was open for 1% -> 1% of each run, Pallas kernels for 1% -> 2%
where the time goes in v3:
time: 145 us; the launch traced here: 144 us
  starting transfers between devices  42.3 us (29%)
  blocking collectives  41.4 us (29%)
  waiting for transfers between devices  41.1 us (28%)
  Pallas kernels  15.6 us (11%)
  other arithmetic  2.26 us (2%)
  local copies, waits for them, and re-layouts  1.45 us (1%)
    all_to_all x1, blocking collectives, per_device(): lax.all_to_all(spread, ('dp', 'y'), split_axis=0, concat_axis=0, tiled=True)  41.4 us
    all_to_all x1, waiting for transfers between devices, per_device(): lax.all_to_all(partial_grads, context, split_axis=0, concat_axis=0, tiled...  20.6 us
    pallas_call x6, Pallas kernels, call(): pl.pallas_call(kernel, out_shape=out_shape, grid_spec=pltpu.PrefetchScala...  15.6 us
    ppermute x1, waiting for transfers between devices, gather_ring(): own_last = lax.ppermute(own, 'tensor', down)  8.93 us
    all_to_all x1, starting transfers between devices, per_device(): lax.all_to_all(partial_grads, context, split_axis=0, concat_axis=0, tiled...  7.99 us
    all_to_all x1, starting transfers between devices, per_device(): lax.all_to_all(packed, context, split_axis=0, concat_axis=0, tiled=True)  7.35 us
    ppermute x1, starting transfers between devices, gather_ring(): own_list += [lax.ppermute(own_list[1], 'tensor', up), own_last]  5.33 us
    ppermute x1, waiting for transfers between devices, gather_ring(): own_list += [lax.ppermute(own_list[1], 'tensor', up), own_last]  4.88 us
  transfers between devices with their start and end apart: 10, of which 5 were waited for; matrix products, arithmetic and copies ran while one was open for 1% of the time, Pallas kernels for 2%

profile of v3, /device:TPU:6, one launch (start us, length us, event | category | flops | bytes accessed | tf_op | source)
XLA Modules:
  0.0 144.4 jit_solution(16704236202848907538)
XLA Ops:
  0.0 2.9 %shard_map.109 = bf16[16,464,128]{2,1,0:T(8,128)(2,1)} custom-call(s32[1]{0:T(128)} %bitcast.2.where_ref, bf16[1,4,512,128]{3,2,1,0:T(8,128)(2,1)} %refs_0_.1, bf16[1,4,512,128]{3,2,1,0:T(8,128)(2,1)} %refs_1_.1, bf16[1,1,512,128]{3,2,1,0:T(8,128)(2,1)} %refs_2_.1, bf16[1,1,512,128]{3,2,1,0:T(8,128)(2,1)} %refs_3_.1, bf16[1,4,512]{2,1,0:T(4,128)(2,1)} %refs_4_.1, ...), custom_call_target="tpu_custom_call" | custom-call | tf_op jit(solution)/shard_map/pallas_call | solution.py:269
  2.9 7.3 %all-to-all-start = ((bf16[16,464,128]{2,1,0:T(8,128)(2,1)}), bf16[16,464,128]{2,1,0:T(8,128)(2,1)S(1)}, u32[]{:S(2)}, u32[]{:S(2)}) async-start(bf16[16,464,128]{2,1,0:T(8,128)(2,1)} %shard_map.109), calls=%async_computation | async-start | bytes 3801088 | tf_op jit(solution)/shard_map/all_to_all | solution.py:340
  10.6 2.3 %collective-permute-start.3 = (bf16[512,512]{1,0:T(8,128)(2,1)S(1)}, bf16[512,512]{1,0:T(8,128)(2,1)S(1)}, u32[]{:S(2)}, u32[]{:S(2)}) collective-permute-start(bf16[512,512]{1,0:T(8,128)(2,1)S(1)} %get-tuple-element.21), channel_id=1, source_target_pairs={{0,4},{4,0},{1,5},{5,1},{2,6},{6,2},{3,7},{7,3},{8,12},{12,8},{9,1... | collective-permute-start | bytes 1572872 | tf_op jit(solution)/shard_map/ppermute | solution.py:348
  13.0 4.2 %collective-permute-start = (bf16[512,512]{1,0:T(8,128)(2,1)S(1)}, bf16[512,512]{1,0:T(8,128)(2,1)}, u32[]{:S(2)}, u32[]{:S(2)}) collective-permute-start(bf16[512,512]{1,0:T(8,128)(2,1)S(1)} %get-tuple-element.26.refs_0_), channel_id=1, source_target_pairs={{0,1},{1,2},{2,3},{3,0},{4,5},{5,6},{6,7},{7,4},{8,9},{9,10},{10,1... | collective-permute-start | bytes 1572872 | tf_op jit(solution)/shard_map/ppermute | solution.py:288
  17.1 1.9 %collective-permute-start.5 = (bf16[512,512]{1,0:T(8,128)(2,1)S(1)}, bf16[512,512]{1,0:T(8,128)(2,1)S(1)}, u32[]{:S(2)}, u32[]{:S(2)}) collective-permute-start(bf16[512,512]{1,0:T(8,128)(2,1)S(1)} %collective-permute-done.3.refs_0_), channel_id=1, source_target_pairs={{0,3},{1,0},{2,1},{3,2},{4,7},{5,4},{6,5},{7,6},{8,11},{9,8},{10,9... | collective-permute-start | bytes 1572872 | tf_op jit(solution)/shard_map/ppermute | solution.py:291
  19.1 2.5 %collective-permute-start.2 = (bf16[512,512]{1,0:T(8,128)(2,1)S(1)}, bf16[512,512]{1,0:T(8,128)(2,1)}, u32[]{:S(2)}, u32[]{:S(2)}) collective-permute-start(bf16[512,512]{1,0:T(8,128)(2,1)S(1)} %get-tuple-element.26.refs_0_), channel_id=1, source_target_pairs={{0,3},{1,0},{2,1},{3,2},{4,7},{5,4},{6,5},{7,6},{8,11},{9,8},{10,9... | collective-permute-start | bytes 1572872 | tf_op jit(solution)/shard_map/ppermute | solution.py:289
  22.3 0.6 reduce.3
  23.0 4.5 %collective-permute-start.4 = (bf16[512,512]{1,0:T(8,128)(2,1)S(1)}, bf16[512,512]{1,0:T(8,128)(2,1)S(1)}, u32[]{:S(2)}, u32[]{:S(2)}) collective-permute-start(bf16[512,512]{1,0:T(8,128)(2,1)S(1)} %collective-permute-done.3.refs_0_), channel_id=1, source_target_pairs={{0,1},{1,2},{2,3},{3,0},{4,5},{5,6},{6,7},{7,4},{8,9},{9,10},{10,1... | collective-permute-start | bytes 1572872 | tf_op jit(solution)/shard_map/ppermute | solution.py:290
  27.6 2.1 %collective-permute-done.refs_1_ = bf16[512,512]{1,0:T(8,128)(2,1)} collective-permute-done((bf16[512,512]{1,0:T(8,128)(2,1)S(1)}, bf16[512,512]{1,0:T(8,128)(2,1)}, u32[]{:S(2)}, u32[]{:S(2)}) %collective-permute-start) | collective-permute-done | bytes 524320 | tf_op jit(solution)/shard_map/ppermute | solution.py:288
  29.7 5.3 %collective-permute-start.1 = (bf16[512,512]{1,0:T(8,128)(2,1)}, bf16[512,512]{1,0:T(8,128)(2,1)S(1)}, u32[]{:S(2)}, u32[]{:S(2)}) collective-permute-start(bf16[512,512]{1,0:T(8,128)(2,1)} %collective-permute-done.refs_1_), channel_id=1, source_target_pairs={{0,1},{1,2},{2,3},{3,0},{4,5},{5,6},{6,7},{7,4},{8,9},{9,10},{10,1... | collective-permute-start | bytes 1572872 | tf_op jit(solution)/shard_map/ppermute | solution.py:292
  35.1 1.9 %collective-permute-start.6 = (bf16[512,512]{1,0:T(8,128)(2,1)S(1)}, bf16[512,512]{1,0:T(8,128)(2,1)}, u32[]{:S(2)}, u32[]{:S(2)}) collective-permute-start(bf16[512,512]{1,0:T(8,128)(2,1)S(1)} %collective-permute-done.5.refs_3_), channel_id=1, source_target_pairs={{0,3},{1,0},{2,1},{3,2},{4,7},{5,4},{6,5},{7,6},{8,11},{9,8},{10,9... | collective-permute-start | bytes 1572872 | tf_op jit(solution)/shard_map/ppermute | solution.py:293
  37.4 8.9 %collective-permute-done.2.refs_3_ = bf16[512,512]{1,0:T(8,128)(2,1)} collective-permute-done((bf16[512,512]{1,0:T(8,128)(2,1)S(1)}, bf16[512,512]{1,0:T(8,128)(2,1)}, u32[]{:S(2)}, u32[]{:S(2)}) %collective-permute-start.2) | collective-permute-done | bytes 524320 | tf_op jit(solution)/shard_map/ppermute | solution.py:289
  46.4 4.9 %collective-permute-done.1.refs_2_ = bf16[512,512]{1,0:T(8,128)(2,1)S(1)} collective-permute-done((bf16[512,512]{1,0:T(8,128)(2,1)}, bf16[512,512]{1,0:T(8,128)(2,1)S(1)}, u32[]{:S(2)}, u32[]{:S(2)}) %collective-permute-start.1) | collective-permute-done | bytes 524320 | tf_op jit(solution)/shard_map/ppermute | solution.py:292
  51.3 0.8 copy-done.5
  52.1 4.5 %collective-permute-done.6.refs_2_ = bf16[512,512]{1,0:T(8,128)(2,1)} collective-permute-done((bf16[512,512]{1,0:T(8,128)(2,1)S(1)}, bf16[512,512]{1,0:T(8,128)(2,1)}, u32[]{:S(2)}, u32[]{:S(2)}) %collective-permute-start.6) | collective-permute-done | bytes 524320 | tf_op jit(solution)/shard_map/ppermute | solution.py:293
  56.6 5.0 %shard_map.111 = bf16[16,3,64,128]{3,2,1,0:T(8,128)(2,1)} custom-call(s32[3,16]{1,0:T(4,128)S(1)} %select_reduce_fusion.slot_ref, s32[4]{0:T(128)S(1)} %broadcast_subtract_fusion.start_ref, bf16[16,464,128]{2,1,0:T(8,128)(2,1)S(1)} %all-to-all-done.recv_ref), custom_call_target="tpu_custom_call" | custom-call | tf_op jit(solution)/shard_map/pallas_call | solution.py:269
  61.6 8.0 %all-to-all-start.1 = ((bf16[16,3,64,128]{3,2,1,0:T(8,128)(2,1)}), bf16[16,3,64,128]{3,2,1,0:T(8,128)(2,1)S(1)}, u32[]{:S(2)}, u32[]{:S(2)}) async-start(bf16[16,3,64,128]{3,2,1,0:T(8,128)(2,1)} %shard_map.111), calls=%async_computation.1 | async-start | bytes 1572864 | tf_op jit(solution)/shard_map/all_to_all | solution.py:380
  69.7 20.6 %all-to-all-done.1.recv_ref = bf16[16,3,64,128]{3,2,1,0:T(8,128)(2,1)S(1)} async-done(((bf16[16,3,64,128]{3,2,1,0:T(8,128)(2,1)}), bf16[16,3,64,128]{3,2,1,0:T(8,128)(2,1)S(1)}, u32[]{:S(2)}, u32[]{:S(2)}) %all-to-all-start.1) | async-done | bytes 786464 | tf_op jit(solution)/shard_map/all_to_all | solution.py:380
  90.3 0.7 shard_map.112.refs_4_
  91.0 4.3 %collective-permute-start.7 = (bf16[512,256]{1,0:T(8,128)(2,1)S(1)}, bf16[512,256]{1,0:T(8,128)(2,1)S(1)}, u32[]{:S(2)}, u32[]{:S(2)}) collective-permute-start(bf16[512,256]{1,0:T(8,128)(2,1)S(1)} %shard_map.112.refs_4_), channel_id=1, source_target_pairs={{0,4},{4,0},{1,5},{5,1},{2,6},{6,2},{3,7},{7,3},{8,12},{12,8},{9,1... | collective-permute-start | bytes 786440 | tf_op jit(solution)/shard_map/ppermute | solution.py:385
  95.4 2.8 %shard_map.113.refs_4_ = f32[4,512,256]{2,1,0:T(8,128)S(1)} custom-call(bf16[512,512]{1,0:T(8,128)(2,1)} %copy-done.1, bf16[512,512]{1,0:T(8,128)(2,1)} %collective-permute-done.refs_1_, bf16[512,512]{1,0:T(8,128)(2,1)} %copy-done.5, bf16[512,512]{1,0:T(8,128)(2,1)} %collective-permute-done.2.refs_3_, bf16[512,256]{1,0:T(8,128)(2,1)S(1)} %shard_map.112.refs_4_), custom_call_target="tpu_custom_call" | custom-call | tf_op jit(solution)/shard_map/pallas_call | solution.py:269
  98.2 4.0 %shard_map.114 = bf16[8,8,2,16,256]{4,3,2,1,0:T(8,128)(2,1)S(1)} custom-call(s32[2]{0:T(128)S(1)} %pad_add_fusion.where_ref, bf16[512,512]{1,0:T(8,128)(2,1)} %copy-done.2, bf16[512,512]{1,0:T(8,128)(2,1)} %copy-done.4, bf16[512,512]{1,0:T(8,128)(2,1)} %collective-permute-done.6.refs_2_, bf16[512,512]{1,0:T(8,128)(2,1)} %copy-done.3, ...), custom_call_target="tpu_custom_call" | custom-call | tf_op jit(solution)/shard_map/pallas_call | solution.py:269
  102.2 41.4 %all_to_all.15 = bf16[64,2,16,256]{3,2,1,0:T(8,128)(2,1)S(1)} all-to-all(bf16[64,2,16,256]{3,2,1,0:T(8,128)(2,1)S(1)} %bitcast.15), channel_id=1, replica_groups=mesh['dp'=8,'y'=8,'core'=2,'tensor'=4] {'dp','y'}, dimensions={0} | all-to-all | bytes 2097152 | tf_op jit(solution)/shard_map/all_to_all | solution.py:413
  143.6 0.8 convert_reduce_fusion
  (34 shorter events, 1.8 us)
Async XLA Ops:
  2.9 7.4 %copy-start = (bf16[1,512,1024]{2,1,0:T(8,128)(2,1)S(1)}, bf16[1,512,1024]{2,1,0:T(8,128)(2,1)}, u32[]{:S(2)}) copy-start(bf16[1,512,1024]{2,1,0:T(8,128)(2,1)} %param.11) | copy-start | bytes 3145732
  2.9 18.7 %copy-start.7 = (s32[1,10]{1,0:T(1,128)S(1)}, s32[1,10]{1,0:T(1,128)}, u32[]{:S(2)}) copy-start(s32[1,10]{1,0:T(1,128)} %param.18) | copy-start | bytes 124
  2.9 19.4 %copy-start.6 = (s32[1,256]{1,0:T(1,128)S(1)}, s32[1,256]{1,0:T(1,128)}, u32[]{:S(2)}) copy-start(s32[1,256]{1,0:T(1,128)} %refs_7_.1) | copy-start | bytes 3076
  2.9 53.7 %all-to-all-start = ((bf16[16,464,128]{2,1,0:T(8,128)(2,1)}), bf16[16,464,128]{2,1,0:T(8,128)(2,1)S(1)}, u32[]{:S(2)}, u32[]{:S(2)}) async-start(bf16[16,464,128]{2,1,0:T(8,128)(2,1)} %shard_map.109), calls=%async_computation | async-start | bytes 3801088 | tf_op jit(solution)/shard_map/all_to_all | solution.py:340
  10.6 51.0 %copy-start.1 = (bf16[512,512]{1,0:T(8,128)(2,1)}, bf16[512,512]{1,0:T(8,128)(2,1)S(1)}, u32[]{:S(2)}) copy-start(bf16[512,512]{1,0:T(8,128)(2,1)S(1)} %get-tuple-element.26.refs_0_) | copy-start | bytes 1572868
  10.6 6.5 %collective-permute-start.3 = (bf16[512,512]{1,0:T(8,128)(2,1)S(1)}, bf16[512,512]{1,0:T(8,128)(2,1)S(1)}, u32[]{:S(2)}, u32[]{:S(2)}) collective-permute-start(bf16[512,512]{1,0:T(8,128)(2,1)S(1)} %get-tuple-element.21), channel_id=1, source_target_pairs={{0,4},{4,0},{1,5},{5,1},{2,6},{6,2},{3,7},{7,3},{8,12},{12,8},{9,1... | collective-permute-start | bytes 1572872 | tf_op jit(solution)/shard_map/ppermute | solution.py:348
  13.0 16.8 %collective-permute-start = (bf16[512,512]{1,0:T(8,128)(2,1)S(1)}, bf16[512,512]{1,0:T(8,128)(2,1)}, u32[]{:S(2)}, u32[]{:S(2)}) collective-permute-start(bf16[512,512]{1,0:T(8,128)(2,1)S(1)} %get-tuple-element.26.refs_0_), channel_id=1, source_target_pairs={{0,1},{1,2},{2,3},{3,0},{4,5},{5,6},{6,7},{7,4},{8,9},{9,10},{10,1... | collective-permute-start | bytes 1572872 | tf_op jit(solution)/shard_map/ppermute | solution.py:288
  17.1 44.5 %copy-start.2 = (bf16[512,512]{1,0:T(8,128)(2,1)}, bf16[512,512]{1,0:T(8,128)(2,1)S(1)}, u32[]{:S(2)}) copy-start(bf16[512,512]{1,0:T(8,128)(2,1)S(1)} %collective-permute-done.3.refs_0_) | copy-start | bytes 1572868
  17.1 17.9 %collective-permute-start.5 = (bf16[512,512]{1,0:T(8,128)(2,1)S(1)}, bf16[512,512]{1,0:T(8,128)(2,1)S(1)}, u32[]{:S(2)}, u32[]{:S(2)}) collective-permute-start(bf16[512,512]{1,0:T(8,128)(2,1)S(1)} %collective-permute-done.3.refs_0_), channel_id=1, source_target_pairs={{0,3},{1,0},{2,1},{3,2},{4,7},{5,4},{6,5},{7,6},{8,11},{9,8},{10,9... | collective-permute-start | bytes 1572872 | tf_op jit(solution)/shard_map/ppermute | solution.py:291
  19.1 27.3 %collective-permute-start.2 = (bf16[512,512]{1,0:T(8,128)(2,1)S(1)}, bf16[512,512]{1,0:T(8,128)(2,1)}, u32[]{:S(2)}, u32[]{:S(2)}) collective-permute-start(bf16[512,512]{1,0:T(8,128)(2,1)S(1)} %get-tuple-element.26.refs_0_), channel_id=1, source_target_pairs={{0,3},{1,0},{2,1},{3,2},{4,7},{5,4},{6,5},{7,6},{8,11},{9,8},{10,9... | collective-permute-start | bytes 1572872 | tf_op jit(solution)/shard_map/ppermute | solution.py:289
  23.0 23.3 %collective-permute-start.4 = (bf16[512,512]{1,0:T(8,128)(2,1)S(1)}, bf16[512,512]{1,0:T(8,128)(2,1)S(1)}, u32[]{:S(2)}, u32[]{:S(2)}) collective-permute-start(bf16[512,512]{1,0:T(8,128)(2,1)S(1)} %collective-permute-done.3.refs_0_), channel_id=1, source_target_pairs={{0,1},{1,2},{2,3},{3,0},{4,5},{5,6},{6,7},{7,4},{8,9},{9,10},{10,1... | collective-permute-start | bytes 1572872 | tf_op jit(solution)/shard_map/ppermute | solution.py:290
  29.7 21.5 %collective-permute-start.1 = (bf16[512,512]{1,0:T(8,128)(2,1)}, bf16[512,512]{1,0:T(8,128)(2,1)S(1)}, u32[]{:S(2)}, u32[]{:S(2)}) collective-permute-start(bf16[512,512]{1,0:T(8,128)(2,1)} %collective-permute-done.refs_1_), channel_id=1, source_target_pairs={{0,1},{1,2},{2,3},{3,0},{4,5},{5,6},{6,7},{7,4},{8,9},{9,10},{10,1... | collective-permute-start | bytes 1572872 | tf_op jit(solution)/shard_map/ppermute | solution.py:292
  35.1 26.5 %copy-start.3 = (bf16[512,512]{1,0:T(8,128)(2,1)}, bf16[512,512]{1,0:T(8,128)(2,1)S(1)}, u32[]{:S(2)}) copy-start(bf16[512,512]{1,0:T(8,128)(2,1)S(1)} %collective-permute-done.5.refs_3_) | copy-start | bytes 1572868
  35.1 21.5 %collective-permute-start.6 = (bf16[512,512]{1,0:T(8,128)(2,1)S(1)}, bf16[512,512]{1,0:T(8,128)(2,1)}, u32[]{:S(2)}, u32[]{:S(2)}) collective-permute-start(bf16[512,512]{1,0:T(8,128)(2,1)S(1)} %collective-permute-done.5.refs_3_), channel_id=1, source_target_pairs={{0,3},{1,0},{2,1},{3,2},{4,7},{5,4},{6,5},{7,6},{8,11},{9,8},{10,9... | collective-permute-start | bytes 1572872 | tf_op jit(solution)/shard_map/ppermute | solution.py:293
  46.4 4.9 %copy-start.4 = (bf16[512,512]{1,0:T(8,128)(2,1)}, bf16[512,512]{1,0:T(8,128)(2,1)S(1)}, u32[]{:S(2)}) copy-start(bf16[512,512]{1,0:T(8,128)(2,1)S(1)} %collective-permute-done.4.refs_1_) | copy-start | bytes 1572868
  51.3 0.8 copy-start.5
  61.6 28.7 %all-to-all-start.1 = ((bf16[16,3,64,128]{3,2,1,0:T(8,128)(2,1)}), bf16[16,3,64,128]{3,2,1,0:T(8,128)(2,1)S(1)}, u32[]{:S(2)}, u32[]{:S(2)}) async-start(bf16[16,3,64,128]{3,2,1,0:T(8,128)(2,1)} %shard_map.111), calls=%async_computation.1 | async-start | bytes 1572864 | tf_op jit(solution)/shard_map/all_to_all | solution.py:380
  91.0 7.2 %collective-permute-start.7 = (bf16[512,256]{1,0:T(8,128)(2,1)S(1)}, bf16[512,256]{1,0:T(8,128)(2,1)S(1)}, u32[]{:S(2)}, u32[]{:S(2)}) collective-permute-start(bf16[512,256]{1,0:T(8,128)(2,1)S(1)} %shard_map.112.refs_4_), channel_id=1, source_target_pairs={{0,4},{4,0},{1,5},{5,1},{2,6},{6,2},{3,7},{7,3},{8,12},{12,8},{9,1... | collective-permute-start | bytes 786440 | tf_op jit(solution)/shard_map/ppermute | solution.py:385

commit v4 on v3

--- a/solution.py
+++ b/solution.py
@@ -17,7 +17,7 @@
 
 QROWS = GROUP * BLK
 KV_AT = 2 * QROWS
-AUX_AT = KV_AT + SPAN * 2 * BLK
+AUX_AT = KV_AT + 2 * BLK
 AUX_ROWS = 16
 ROWS = AUX_AT + AUX_ROWS
 UNIT_BLKS = PAD // BLK
@@ -88,14 +88,8 @@
             packed_scr[dest, head * BLK : (head + 1) * BLK, :] = query_scr[0, head, rows, :]
             at = QROWS + head * BLK
             packed_scr[dest, at : at + BLK, :] = grad_scr[0, head, rows, :]
-        for span in range(SPAN):
-            at = KV_AT + span * 2 * BLK
-            if dest >= span:
-                rows = pl.ds(pl.multiple_of(held_scr[dest - span] * BLK, BLK), BLK)
-                packed_scr[dest, at : at + BLK, :] = key_scr[0, 0, rows, :]
-                packed_scr[dest, at + BLK : at + 2 * BLK, :] = value_scr[0, 0, rows, :]
-            else:
-                packed_scr[dest, at : at + 2 * BLK, :] = jnp.zeros((2 * BLK, HD), out_ref.dtype)
+        packed_scr[dest, KV_AT : KV_AT + BLK, :] = key_scr[0, 0, rows, :]
+        packed_scr[dest, KV_AT + BLK : AUX_AT, :] = value_scr[0, 0, rows, :]
         packed_scr[dest, AUX_AT:ROWS, :] = aux_scr[slot]
         stores.append(pltpu.make_async_copy(packed_scr.at[dest], out_ref.at[dest], out_sem.at[dest]))
         stores[-1].start()
@@ -103,82 +97,125 @@
         store.wait()
 
 
-def attend_kernel(
-    slot_ref, start_ref, recv_ref, out_ref,
-    query_scr, grad_scr, query_turned, grad_turned, stat_scr,
+def pair_grads(key_blk, value_blk, query_refs, cols, lse, dots, live):
+    query_ref, grad_ref, query_turned, grad_turned = query_refs
+    scores = jnp.dot(key_blk, query_turned[:, cols], preferred_element_type=jnp.float32)
+    dprobs = jnp.dot(value_blk, grad_turned[:, cols], preferred_element_type=jnp.float32)
+    probs = jnp.where(live, jnp.exp2(scores * (HD ** (-0.5) * LOG2E) - lse), 0.0)
+    dscores = (probs * (dprobs - dots)).astype(jnp.bfloat16)
+    value_part = jnp.dot(
+        probs.astype(jnp.bfloat16), grad_ref[cols, :], preferred_element_type=jnp.float32
+    )
+    key_part = jnp.dot(dscores, query_ref[cols, :], preferred_element_type=jnp.float32)
+    return key_part, value_part
+
+
+def unit_stats(stat_ref, unit):
+    blocks = range(unit * UNIT_BLKS, (unit + 1) * UNIT_BLKS)
+    lse = jnp.concatenate([stat_ref[b, 0:1, :] for b in blocks], axis=1) * LOG2E
+    dots = jnp.concatenate([stat_ref[b, 1:2, :] for b in blocks], axis=1)
+    return lse, dots
+
+
+def own_attend_kernel(
+    slot_ref, start_ref, recv_ref,
+    query_ref, grad_ref, query_turned, grad_turned, stat_ref, out_ref,
     key_scr, value_scr, dkey_scr, dvalue_scr,
 ):
     groups = recv_ref.shape[0]
-    chunk = key_scr.shape[0] // SPAN
-    units = chunk // PAD
+    units = key_scr.shape[0] // PAD
     width = UNIT_BLKS * QROWS
-    pair = 2 * PAD
-    dkey_scr[...] = jnp.zeros_like(dkey_scr)
-    dvalue_scr[...] = jnp.zeros_like(dvalue_scr)
     for src in range(groups):
         slot = slot_ref[0, src]
         at = pl.multiple_of(slot * QROWS, QROWS)
         query_blk = recv_ref[src, 0:QROWS, :]
         grad_blk = recv_ref[src, QROWS : 2 * QROWS, :]
-        query_scr[pl.ds(at, QROWS), :] = query_blk
-        grad_scr[pl.ds(at, QROWS), :] = grad_blk
+        query_ref[pl.ds(at, QROWS), :] = query_blk
+        grad_ref[pl.ds(at, QROWS), :] = grad_blk
         query_turned[:, pl.ds(at, QROWS)] = query_blk.T
         grad_turned[:, pl.ds(at, QROWS)] = grad_blk.T
-        stat_scr[slot] = recv_ref[src, AUX_AT:ROWS, :].astype(jnp.float32)
-        for span in range(SPAN):
-            row = (SPAN - 1 - span) * chunk + slot_ref[span, src] * BLK
-            row = pl.multiple_of(row, BLK)
-            at = KV_AT + span * 2 * BLK
-            key_scr[pl.ds(row, BLK), :] = recv_ref[src, at : at + BLK, :]
-            value_scr[pl.ds(row, BLK), :] = recv_ref[src, at + BLK : at + 2 * BLK, :]
-
-    scale = HD ** (-0.5)
+        stat_ref[slot] = recv_ref[src, AUX_AT:ROWS, :].astype(jnp.float32)
+        row = pl.multiple_of(slot * BLK, BLK)
+        key_scr[pl.ds(row, BLK), :] = recv_ref[src, KV_AT : KV_AT + BLK, :]
+        value_scr[pl.ds(row, BLK), :] = recv_ref[src, KV_AT + BLK : AUX_AT, :]
+
+    queries = (query_ref, grad_ref, query_turned, grad_turned)
+    dkey_scr[...] = jnp.zeros_like(dkey_scr)
+    dvalue_scr[...] = jnp.zeros_like(dvalue_scr)
+    for unit in range(units):
+        rows = slice(0, (unit + 1) * PAD)
+        cols = slice(unit * width, (unit + 1) * width)
+        lse, dots = unit_stats(stat_ref, unit)
+        key_at = lax.broadcasted_iota(jnp.int32, (rows.stop, width), 0)
+        column = lax.broadcasted_iota(jnp.int32, (rows.stop, width), 1)
+        query_at = unit * PAD + (column // QROWS) * BLK + column % BLK
+        first = (start_ref[unit] - (SPAN - 1) * units) * PAD
+        live = (key_at <= query_at) & (key_at >= first)
+        key_part, value_part = pair_grads(
+            key_scr[rows, :], value_scr[rows, :], queries, cols, lse, dots, live
+        )
+        dkey_scr[rows, :] += key_part
+        dvalue_scr[rows, :] += value_part
+
+    for src in range(groups):
+        rows = pl.ds(pl.multiple_of(slot_ref[0, src] * BLK, BLK), BLK)
+        dkey = dkey_scr[rows, :] * HD ** (-0.5)
+        out_ref[src, 0:BLK, :] = dkey.astype(out_ref.dtype)
+        out_ref[src, BLK : 2 * BLK, :] = dvalue_scr[rows, :].astype(out_ref.dtype)
+
+
+def earlier_attend_kernel(slot_ref, start_ref, *refs):
+    earlier_refs, refs = refs[: SPAN - 1], refs[SPAN - 1 :]
+    query_ref, grad_ref, query_turned, grad_turned, stat_ref, own_ref, out_ref = refs[:7]
+    key_scr, value_scr, dkey_scr, dvalue_scr = refs[7:]
+    groups = out_ref.shape[0]
+    chunk = key_scr.shape[0] // (SPAN - 1)
+    units = chunk // PAD
+    width = UNIT_BLKS * QROWS
+    pair = 2 * PAD
+    edge = (SPAN - 1) * units
+
+    def rows_of(span, src):
+        row = (SPAN - 1 - span) * chunk + slot_ref[span, src] * BLK
+        return pl.ds(pl.multiple_of(row, BLK), BLK)
+
+    for src in range(groups):
+        for span in range(1, SPAN):
+            rows = rows_of(span, src)
+            key_scr[rows, :] = earlier_refs[span - 1][src, 0:BLK, :]
+            value_scr[rows, :] = earlier_refs[span - 1][src, BLK : 2 * BLK, :]
+    dkey_scr[...] = jnp.zeros_like(dkey_scr)
+    dvalue_scr[...] = jnp.zeros_like(dvalue_scr)
+    queries = (query_ref, grad_ref, query_turned, grad_turned)
     key_at = lax.broadcasted_iota(jnp.int32, (pair, width), 0)
-    column = lax.broadcasted_iota(jnp.int32, (pair, width), 1)
-    query_at = (column // QROWS) * BLK + column % BLK
-    causal = key_at - PAD <= query_at
-
     for unit in range(units):
         cols = slice(unit * width, (unit + 1) * width)
-        blocks = range(unit * UNIT_BLKS, (unit + 1) * UNIT_BLKS)
-        lse = jnp.concatenate([stat_scr[b, 0:1, :] for b in blocks], axis=1) * LOG2E
-        dots = jnp.concatenate([stat_scr[b, 1:2, :] for b in blocks], axis=1)
-
-        def visit(row, live):
-            rows = pl.ds(row, pair)
-            scores = jnp.dot(
-                key_scr[rows, :], query_turned[:, cols], preferred_element_type=jnp.float32
+        lse, dots = unit_stats(stat_ref, unit)
+        first = jnp.minimum(start_ref[unit], edge)
+
+        @pl.loop(0, (edge - first + 1) // 2)
+        def _(step):
+            base = edge - 2 - 2 * step
+            rows = pl.ds(pl.multiple_of(base * PAD, pair), pair)
+            key_part, value_part = pair_grads(
+                key_scr[rows, :],
+                value_scr[rows, :],
+                queries,
+                cols,
+                lse,
+                dots,
+                key_at >= (first - base) * PAD,
             )
-            dprobs = jnp.dot(
-                value_scr[rows, :], grad_turned[:, cols], preferred_element_type=jnp.float32
-            )
-            probs = jnp.where(live, jnp.exp2(scores * (scale * LOG2E) - lse), 0.0)
-            dscores = (probs * (dprobs - dots)).astype(jnp.bfloat16)
-            dvalue_scr[rows, :] += jnp.dot(
-                probs.astype(jnp.bfloat16), grad_scr[cols, :], preferred_element_type=jnp.float32
-            )
-            dkey_scr[rows, :] += jnp.dot(
-                dscores, query_scr[cols, :], preferred_element_type=jnp.float32
-            )
-
-        first = start_ref[unit]
-        last = (SPAN - 1) * units + unit
-        visit((last - 1) * PAD, causal & (key_at >= (first - (last - 1)) * PAD))
-
-        @pl.loop(1, (last - first + 2) // 2)
-        def _(step):
-            base = last - 1 - 2 * step
-            visit(pl.multiple_of(base * PAD, PAD), key_at >= (first - base) * PAD)
+            dkey_scr[rows, :] += key_part
+            dvalue_scr[rows, :] += value_part
 
     for src in range(groups):
-        for span in range(SPAN):
-            row = (SPAN - 1 - span) * chunk + slot_ref[span, src] * BLK
-            row = pl.multiple_of(row, BLK)
-            dkey = dkey_scr[pl.ds(row, BLK), :] * scale
+        out_ref[src, 0] = own_ref[src]
+        for span in range(1, SPAN):
+            rows = rows_of(span, src)
+            dkey = dkey_scr[rows, :] * HD ** (-0.5)
             out_ref[src, span, 0:BLK, :] = dkey.astype(out_ref.dtype)
-            out_ref[src, span, BLK : 2 * BLK, :] = dvalue_scr[pl.ds(row, BLK), :].astype(
-                out_ref.dtype
-            )
+            out_ref[src, span, BLK : 2 * BLK, :] = dvalue_scr[rows, :].astype(out_ref.dtype)
 
 
 def collect_kernel(target_ref, recv_ref, out_ref):
@@ -281,17 +318,12 @@
     return call
 
 
-def gather_ring(own, other):
-    count = lax.axis_size("tensor")
-    up = [(i, (i + 1) % count) for i in range(count)]
-    down = [(i, (i - 1) % count) for i in range(count)]
-    own_list = [own, lax.ppermute(own, "tensor", up)]
-    own_last = lax.ppermute(own, "tensor", down)
-    other_list = [other, lax.ppermute(other, "tensor", up)]
-    other_last = lax.ppermute(other, "tensor", down)
-    own_list += [lax.ppermute(own_list[1], "tensor", up), own_last]
-    other_list += [lax.ppermute(other_last, "tensor", down), other_last]
-    return own_list, other_list
+def around(count, step):
+    return [(i, (i + step) % count) for i in range(count)]
+
+
+def onward(count, step):
+    return [(i, i + step) for i in range(count - step)]
 
 
 def per_device(
@@ -346,8 +378,16 @@
     )
     swap = [(0, 1), (1, 0)]
     other_input = lax.ppermute(other_input, "core", swap)
-    own_list, other_list = gather_ring(own_input, other_input)
-    recv, own_list, other_list = lax.optimization_barrier((recv, own_list, other_list))
+    widths = lax.axis_size("tensor")
+    up, down = around(widths, 1), around(widths, -1)
+    near = [
+        lax.ppermute(array, "tensor", way)
+        for array in (own_input, other_input)
+        for way in (up, down)
+    ]
+    recv, near = lax.optimization_barrier((recv, near))
+    held = recv[:, KV_AT:AUX_AT]
+    earlier = [lax.ppermute(held, context, onward(groups, span)) for span in range(1, SPAN)]
 
     order_grid = order_row.reshape(groups, slots)
     chunk_ids = (where - jnp.arange(SPAN, dtype=jnp.int32))[:, None, None]
@@ -360,23 +400,36 @@
     doc_start = jnp.max(jnp.where(ends[None, :] <= unit_ids[:, None], ends[None, :], 0), axis=1)
     starts = doc_start - (where - (SPAN - 1)) * chunk_units
 
-    window = SPAN * tokens
+    sorted_rows = jax.ShapeDtypeStruct((slots * QROWS, HD), low)
+    turned_rows = jax.ShapeDtypeStruct((HD, slots * QROWS), low)
+    own_work = prefetched(
+        own_attend_kernel,
+        2,
+        (
+            sorted_rows,
+            sorted_rows,
+            turned_rows,
+            turned_rows,
+            jax.ShapeDtypeStruct((slots, AUX_ROWS, HD), jnp.float32),
+            jax.ShapeDtypeStruct((groups, 2 * BLK, HD), low),
+        ),
+        scratch=tuple(
+            pltpu.VMEM((tokens, HD), dtype) for dtype in (low, low, jnp.float32, jnp.float32)
+        ),
+    )(slot_map, starts, recv)
     partial_grads = prefetched(
-        attend_kernel,
+        earlier_attend_kernel,
         2,
         jax.ShapeDtypeStruct((groups, SPAN, 2 * BLK, HD), low),
-        scratch=(
-            pltpu.VMEM((slots * QROWS, HD), low),
-            pltpu.VMEM((slots * QROWS, HD), low),
-            pltpu.VMEM((HD, slots * QROWS), low),
-            pltpu.VMEM((HD, slots * QROWS), low),
-            pltpu.VMEM((slots, AUX_ROWS, HD), jnp.float32),
-            pltpu.VMEM((window, HD), low),
-            pltpu.VMEM((window, HD), low),
-            pltpu.VMEM((window, HD), jnp.float32),
-            pltpu.VMEM((window, HD), jnp.float32),
+        scratch=tuple(
+            pltpu.VMEM(((SPAN - 1) * tokens, HD), dtype)
+            for dtype in (low, low, jnp.float32, jnp.float32)
         ),
-    )(slot_map, starts, recv)
+    )(slot_map, starts, *earlier, *own_work)
+    partial_grads, near = lax.optimization_barrier((partial_grads, near))
+    own_up, own_down, other_up, other_down = near
+    own_list = [own_input, own_up, lax.ppermute(own_up, "tensor", up), own_down]
+    other_list = [other_input, other_up, lax.ppermute(other_down, "tensor", down), other_down]
     returned = lax.all_to_all(partial_grads, context, split_axis=0, concat_axis=0, tiled=True)
     targets = lax.dynamic_slice_in_dim(order_row, where * slots, slots, 0) // slots
     own_kv = prefetched(collect_kernel, 1, jax.ShapeDtypeStruct((tokens, 2 * HD), low))(

time: 145 us -> 150 us (1.034)
  the two profiles are of different devices: /device:TPU:6 before, /device:TPU:8 now
where the time goes in v4:
time: 150 us; the launch traced here: 149 us
  blocking collectives  47 us (31%)
  starting transfers between devices  46.3 us (31%)
  waiting for transfers between devices  32.5 us (22%)
  Pallas kernels  17.1 us (11%)
  local copies, waits for them, and re-layouts  3.73 us (2%)
  other arithmetic  2.25 us (2%)
    all_to_all x1, blocking collectives, per_device(): lax.all_to_all(spread, ('dp', 'y'), split_axis=0, concat_axis=0, tiled=True)  47 us
    pallas_call x7, Pallas kernels, call(): pl.pallas_call(kernel, out_shape=out_shape, grid_spec=pltpu.PrefetchScala...  17.1 us
    ppermute x4, waiting for transfers between devices, per_device(): lax.ppermute(array, 'tensor', way)  16.9 us
    all_to_all x1, waiting for transfers between devices, per_device(): lax.all_to_all(partial_grads, context, split_axis=0, concat_axis=0, tiled...  11.9 us
    ppermute x4, starting transfers between devices, per_device(): lax.ppermute(array, 'tensor', way)  11.9 us
    all_to_all x1, starting transfers between devices, per_device(): lax.all_to_all(packed, context, split_axis=0, concat_axis=0, tiled=True)  9.33 us
    all_to_all x1, starting transfers between devices, per_device(): lax.all_to_all(partial_grads, context, split_axis=0, concat_axis=0, tiled...  8.44 us
    ppermute x2, starting transfers between devices, per_device(): lax.ppermute(held, context, onward(groups, span))  5.28 us
  transfers between devices with their start and end apart: 12, of which 7 were waited for; matrix products, arithmetic and copies ran while one was open for 1% of the time, Pallas kernels for 5%

profile of v4, /device:TPU:8, one launch (start us, length us, event | category | flops | bytes accessed | tf_op | source)
XLA Modules:
  0.0 149.2 jit_solution(6468029348654447675)
XLA Ops:
  0.0 2.8 %shard_map.109 = bf16[16,336,128]{2,1,0:T(8,128)(2,1)} custom-call(s32[1]{0:T(128)} %bitcast.2.where_ref, bf16[1,4,512,128]{3,2,1,0:T(8,128)(2,1)} %refs_0_.1, bf16[1,4,512,128]{3,2,1,0:T(8,128)(2,1)} %refs_1_.1, bf16[1,1,512,128]{3,2,1,0:T(8,128)(2,1)} %refs_2_.1, bf16[1,1,512,128]{3,2,1,0:T(8,128)(2,1)} %refs_3_.1, bf16[1,4,512]{2,1,0:T(4,128)(2,1)} %refs_4_.1, ...), custom_call_target="tpu_custom_call" | custom-call | tf_op jit(solution)/shard_map/pallas_call | solution.py:306
  2.8 9.3 %all-to-all-start = ((bf16[16,336,128]{2,1,0:T(8,128)(2,1)}), bf16[16,336,128]{2,1,0:T(8,128)(2,1)S(1)}, u32[]{:S(2)}, u32[]{:S(2)}) async-start(bf16[16,336,128]{2,1,0:T(8,128)(2,1)} %shard_map.109), calls=%async_computation | async-start | bytes 2752512 | tf_op jit(solution)/shard_map/all_to_all | solution.py:372
  12.5 2.1 %collective-permute-start = (bf16[512,512]{1,0:T(8,128)(2,1)S(1)}, bf16[512,512]{1,0:T(8,128)(2,1)S(1)}, u32[]{:S(2)}, u32[]{:S(2)}) collective-permute-start(bf16[512,512]{1,0:T(8,128)(2,1)S(1)} %get-tuple-element.26), channel_id=1, source_target_pairs={{0,4},{4,0},{1,5},{5,1},{2,6},{6,2},{3,7},{7,3},{8,12},{12,8},{9,1... | collective-permute-start | bytes 1572872 | tf_op jit(solution)/shard_map/ppermute | solution.py:380
  14.6 2.9 %collective-permute-start.2 = (bf16[512,512]{1,0:T(8,128)(2,1)S(1)}, bf16[512,512]{1,0:T(8,128)(2,1)S(1)}, u32[]{:S(2)}, u32[]{:S(2)}) collective-permute-start(bf16[512,512]{1,0:T(8,128)(2,1)S(1)} %get-tuple-element.28.refs_0_), channel_id=1, source_target_pairs={{0,3},{1,0},{2,1},{3,2},{4,7},{5,4},{6,5},{7,6},{8,11},{9,8},{10,9... | collective-permute-start | bytes 1572872 | tf_op jit(solution)/shard_map/ppermute | solution.py:384
  17.5 2.9 %collective-permute-start.1 = (bf16[512,512]{1,0:T(8,128)(2,1)S(1)}, bf16[512,512]{1,0:T(8,128)(2,1)}, u32[]{:S(2)}, u32[]{:S(2)}) collective-permute-start(bf16[512,512]{1,0:T(8,128)(2,1)S(1)} %get-tuple-element.28.refs_0_), channel_id=1, source_target_pairs={{0,1},{1,2},{2,3},{3,0},{4,5},{5,6},{6,7},{7,4},{8,9},{9,10},{10,1... | collective-permute-start | bytes 1572872 | tf_op jit(solution)/shard_map/ppermute | solution.py:384
  21.9 4.1 %collective-permute-start.4 = (bf16[512,512]{1,0:T(8,128)(2,1)S(1)}, bf16[512,512]{1,0:T(8,128)(2,1)S(1)}, u32[]{:S(2)}, u32[]{:S(2)}) collective-permute-start(bf16[512,512]{1,0:T(8,128)(2,1)S(1)} %collective-permute-done.refs_0_), channel_id=1, source_target_pairs={{0,3},{1,0},{2,1},{3,2},{4,7},{5,4},{6,5},{7,6},{8,11},{9,8},{10,9... | collective-permute-start | bytes 1572872 | tf_op jit(solution)/shard_map/ppermute | solution.py:384
  26.0 1.9 %collective-permute-start.3 = (bf16[512,512]{1,0:T(8,128)(2,1)S(1)}, bf16[512,512]{1,0:T(8,128)(2,1)}, u32[]{:S(2)}, u32[]{:S(2)}) collective-permute-start(bf16[512,512]{1,0:T(8,128)(2,1)S(1)} %collective-permute-done.refs_0_), channel_id=1, source_target_pairs={{0,1},{1,2},{2,3},{3,0},{4,5},{5,6},{6,7},{7,4},{8,9},{9,10},{10,1... | collective-permute-start | bytes 1572872 | tf_op jit(solution)/shard_map/ppermute | solution.py:384
  28.2 3.1 %collective-permute-done.2.refs_3_ = bf16[512,512]{1,0:T(8,128)(2,1)S(1)} collective-permute-done((bf16[512,512]{1,0:T(8,128)(2,1)S(1)}, bf16[512,512]{1,0:T(8,128)(2,1)S(1)}, u32[]{:S(2)}, u32[]{:S(2)}) %collective-permute-start.2) | collective-permute-done | bytes 524320 | tf_op jit(solution)/shard_map/ppermute | solution.py:384
  31.2 4.3 %collective-permute-done.1.refs_1_ = bf16[512,512]{1,0:T(8,128)(2,1)} collective-permute-done((bf16[512,512]{1,0:T(8,128)(2,1)S(1)}, bf16[512,512]{1,0:T(8,128)(2,1)}, u32[]{:S(2)}, u32[]{:S(2)}) %collective-permute-start.1) | collective-permute-done | bytes 524320 | tf_op jit(solution)/shard_map/ppermute | solution.py:384
  35.5 6.4 %collective-permute-done.4.refs_3_ = bf16[512,512]{1,0:T(8,128)(2,1)S(1)} collective-permute-done((bf16[512,512]{1,0:T(8,128)(2,1)S(1)}, bf16[512,512]{1,0:T(8,128)(2,1)S(1)}, u32[]{:S(2)}, u32[]{:S(2)}) %collective-permute-start.4) | collective-permute-done | bytes 524320 | tf_op jit(solution)/shard_map/ppermute | solution.py:384
  42.7 3.1 %collective-permute-done.3.refs_1_ = bf16[512,512]{1,0:T(8,128)(2,1)} collective-permute-done((bf16[512,512]{1,0:T(8,128)(2,1)S(1)}, bf16[512,512]{1,0:T(8,128)(2,1)}, u32[]{:S(2)}, u32[]{:S(2)}) %collective-permute-start.3) | collective-permute-done | bytes 524320 | tf_op jit(solution)/shard_map/ppermute | solution.py:384
  46.6 3.4 %collective-permute-start.6 = (bf16[16,64,128]{2,1,0:T(8,128)(2,1)}, bf16[16,64,128]{2,1,0:T(8,128)(2,1)S(1)}, u32[]{:S(2)}, u32[]{:S(2)}) collective-permute-start(bf16[16,64,128]{2,1,0:T(8,128)(2,1)} %slice.6), channel_id=1, source_target_pairs={{0,8},{4,12},{8,16},{12,20},{16,24},{20,28},{24,32},{28,36},{32,40... | collective-permute-start | bytes 786440 | tf_op jit(solution)/shard_map/ppermute | solution.py:390
  49.9 1.9 %collective-permute-start.5 = (bf16[16,64,128]{2,1,0:T(8,128)(2,1)}, bf16[16,64,128]{2,1,0:T(8,128)(2,1)S(1)}, u32[]{:S(2)}, u32[]{:S(2)}) collective-permute-start(bf16[16,64,128]{2,1,0:T(8,128)(2,1)} %slice.6), channel_id=1, source_target_pairs={{0,4},{4,8},{8,12},{12,16},{16,20},{20,24},{24,28},{28,32},{32,36}... | collective-permute-start | bytes 786440 | tf_op jit(solution)/shard_map/ppermute | solution.py:390
  52.1 3.1 %shard_map.111 = (bf16[2048,128]{1,0:T(8,128)(2,1)S(1)}, bf16[2048,128]{1,0:T(8,128)(2,1)S(1)}, bf16[128,2048]{1,0:T(8,128)(2,1)S(1)}, bf16[128,2048]{1,0:T(8,12...) custom-call(s32[3,16]{1,0:T(4,128)S(1)} %select_reduce_fusion.slot_ref, ...), custom_call_target="tpu_custom_call" | custom-call | tf_op jit(solution)/shard_map/pallas_call | solution.py:306
  55.2 1.9 %collective-permute-done.6.refs_1_ = bf16[16,64,128]{2,1,0:T(8,128)(2,1)S(1)} collective-permute-done((bf16[16,64,128]{2,1,0:T(8,128)(2,1)}, bf16[16,64,128]{2,1,0:T(8,128)(2,1)S(1)}, u32[]{:S(2)}, u32[]{:S(2)}) %collective-permute-start.6) | collective-permute-done | bytes 262176 | tf_op jit(solution)/shard_map/ppermute | solution.py:390
  58.9 3.4 %shard_map.112 = bf16[16,3,64,128]{3,2,1,0:T(8,128)(2,1)} custom-call(s32[3,16]{1,0:T(4,128)S(1)} %select_reduce_fusion.slot_ref, s32[4]{0:T(128)S(1)} %broadcast_subtract_fusion.start_ref, bf16[16,64,128]{2,1,0:T(8,128)(2,1)S(1)} %collective-permute-done.5.refs_0_, bf16[16,64,128]{2,1,0:T(8,128)(2,1)S(1)} %collective-permute-done.6.refs_1_, ...), custom_call_target="tpu_custom_call" | custom-call | tf_op jit(solution)/shard_map/pallas_call | solution.py:306
  62.4 8.4 %all-to-all-start.1 = ((bf16[16,3,64,128]{3,2,1,0:T(8,128)(2,1)}), bf16[16,3,64,128]{3,2,1,0:T(8,128)(2,1)S(1)}, u32[]{:S(2)}, u32[]{:S(2)}) async-start(bf16[16,3,64,128]{3,2,1,0:T(8,128)(2,1)} %shard_map.112), calls=%async_computation.1 | async-start | bytes 1572864 | tf_op jit(solution)/shard_map/all_to_all | solution.py:433
  70.8 1.9 %collective-permute-start.8 = (bf16[512,512]{1,0:T(8,128)(2,1)}, bf16[512,512]{1,0:T(8,128)(2,1)S(1)}, u32[]{:S(2)}, u32[]{:S(2)}) collective-permute-start(bf16[512,512]{1,0:T(8,128)(2,1)} %collective-permute-done.1.refs_1_), channel_id=1, source_target_pairs={{0,1},{1,2},{2,3},{3,0},{4,5},{5,6},{6,7},{7,4},{8,9},{9,10},{10,1... | collective-permute-start | bytes 1572872 | tf_op jit(solution)/shard_map/ppermute | solution.py:431
  72.7 5.1 %collective-permute-start.7 = (bf16[512,512]{1,0:T(8,128)(2,1)}, bf16[512,512]{1,0:T(8,128)(2,1)S(1)}, u32[]{:S(2)}, u32[]{:S(2)}) collective-permute-start(bf16[512,512]{1,0:T(8,128)(2,1)} %copy-done.4), channel_id=1, source_target_pairs={{0,3},{1,0},{2,1},{3,2},{4,7},{5,4},{6,5},{7,6},{8,11},{9,8},{10,9... | collective-permute-start | bytes 1572872 | tf_op jit(solution)/shard_map/ppermute | solution.py:432
  77.9 11.9 %all-to-all-done.1.recv_ref = bf16[16,3,64,128]{3,2,1,0:T(8,128)(2,1)S(1)} async-done(((bf16[16,3,64,128]{3,2,1,0:T(8,128)(2,1)}), bf16[16,3,64,128]{3,2,1,0:T(8,128)(2,1)S(1)}, u32[]{:S(2)}, u32[]{:S(2)}) %all-to-all-start.1) | async-done | bytes 786464 | tf_op jit(solution)/shard_map/all_to_all | solution.py:433
  90.6 2.2 %collective-permute-start.9 = (bf16[512,256]{1,0:T(8,128)(2,1)S(1)}, bf16[512,256]{1,0:T(8,128)(2,1)S(1)}, u32[]{:S(2)}, u32[]{:S(2)}) collective-permute-start(bf16[512,256]{1,0:T(8,128)(2,1)S(1)} %shard_map.113.refs_4_), channel_id=1, source_target_pairs={{0,4},{4,0},{1,5},{5,1},{2,6},{6,2},{3,7},{7,3},{8,12},{12,8},{9,1... | collective-permute-start | bytes 786440 | tf_op jit(solution)/shard_map/ppermute | solution.py:438
  93.8 2.8 %shard_map.114.refs_4_ = f32[4,512,256]{2,1,0:T(8,128)S(1)} custom-call(bf16[512,512]{1,0:T(8,128)(2,1)} %copy-done.1, bf16[512,512]{1,0:T(8,128)(2,1)} %collective-permute-done.1.refs_1_, bf16[512,512]{1,0:T(8,128)(2,1)} %copy-done.6, bf16[512,512]{1,0:T(8,128)(2,1)} %copy-done.3, bf16[512,256]{1,0:T(8,128)(2,1)S(1)} %shard_map.113.refs_4_), custom_call_target="tpu_custom_call" | custom-call | tf_op jit(solution)/shard_map/pallas_call | solution.py:306
  97.4 4.0 %shard_map.115 = bf16[8,8,2,16,256]{4,3,2,1,0:T(8,128)(2,1)S(1)} custom-call(s32[2]{0:T(128)S(1)} %pad_add_fusion.where_ref, bf16[512,512]{1,0:T(8,128)(2,1)} %copy-done.2, bf16[512,512]{1,0:T(8,128)(2,1)} %collective-permute-done.3.refs_1_, bf16[512,512]{1,0:T(8,128)(2,1)} %copy-done.5, bf16[512,512]{1,0:T(8,128)(2,1)} %copy-done.4, ...), custom_call_target="tpu_custom_call" | custom-call | tf_op jit(solution)/shard_map/pallas_call | solution.py:306
  101.4 47.0 %all_to_all.15 = bf16[64,2,16,256]{3,2,1,0:T(8,128)(2,1)S(1)} all-to-all(bf16[64,2,16,256]{3,2,1,0:T(8,128)(2,1)S(1)} %bitcast.15), channel_id=1, replica_groups=mesh['dp'=8,'y'=8,'core'=2,'tensor'=4] {'dp','y'}, dimensions={0} | all-to-all | bytes 2097152 | tf_op jit(solution)/shard_map/all_to_all | solution.py:466
  (42 shorter events, 8.8 us)
Async XLA Ops:
  0.0 12.2 %copy-start = (bf16[1,512,1024]{2,1,0:T(8,128)(2,1)S(1)}, bf16[1,512,1024]{2,1,0:T(8,128)(2,1)}, u32[]{:S(2)}) copy-start(bf16[1,512,1024]{2,1,0:T(8,128)(2,1)} %param.11) | copy-start | bytes 3145732
  2.8 17.6 %copy-start.8 = (s32[1,10]{1,0:T(1,128)S(1)}, s32[1,10]{1,0:T(1,128)}, u32[]{:S(2)}) copy-start(s32[1,10]{1,0:T(1,128)} %param.18) | copy-start | bytes 124
  2.8 18.3 %copy-start.7 = (s32[1,256]{1,0:T(1,128)S(1)}, s32[1,256]{1,0:T(1,128)}, u32[]{:S(2)}) copy-start(s32[1,256]{1,0:T(1,128)} %refs_7_.1) | copy-start | bytes 3076
  2.8 43.0 %all-to-all-start = ((bf16[16,336,128]{2,1,0:T(8,128)(2,1)}), bf16[16,336,128]{2,1,0:T(8,128)(2,1)S(1)}, u32[]{:S(2)}, u32[]{:S(2)}) async-start(bf16[16,336,128]{2,1,0:T(8,128)(2,1)} %shard_map.109), calls=%async_computation | async-start | bytes 2752512 | tf_op jit(solution)/shard_map/all_to_all | solution.py:372
  12.5 49.9 %copy-start.1 = (bf16[512,512]{1,0:T(8,128)(2,1)}, bf16[512,512]{1,0:T(8,128)(2,1)S(1)}, u32[]{:S(2)}) copy-start(bf16[512,512]{1,0:T(8,128)(2,1)S(1)} %get-tuple-element.28.refs_0_) | copy-start | bytes 1572868
  12.5 9.4 %collective-permute-start = (bf16[512,512]{1,0:T(8,128)(2,1)S(1)}, bf16[512,512]{1,0:T(8,128)(2,1)S(1)}, u32[]{:S(2)}, u32[]{:S(2)}) collective-permute-start(bf16[512,512]{1,0:T(8,128)(2,1)S(1)} %get-tuple-element.26), channel_id=1, source_target_pairs={{0,4},{4,0},{1,5},{5,1},{2,6},{6,2},{3,7},{7,3},{8,12},{12,8},{9,1... | collective-permute-start | bytes 1572872 | tf_op jit(solution)/shard_map/ppermute | solution.py:380
  14.6 16.6 %collective-permute-start.2 = (bf16[512,512]{1,0:T(8,128)(2,1)S(1)}, bf16[512,512]{1,0:T(8,128)(2,1)S(1)}, u32[]{:S(2)}, u32[]{:S(2)}) collective-permute-start(bf16[512,512]{1,0:T(8,128)(2,1)S(1)} %get-tuple-element.28.refs_0_), channel_id=1, source_target_pairs={{0,3},{1,0},{2,1},{3,2},{4,7},{5,4},{6,5},{7,6},{8,11},{9,8},{10,9... | collective-permute-start | bytes 1572872 | tf_op jit(solution)/shard_map/ppermute | solution.py:384
  17.5 18.0 %collective-permute-start.1 = (bf16[512,512]{1,0:T(8,128)(2,1)S(1)}, bf16[512,512]{1,0:T(8,128)(2,1)}, u32[]{:S(2)}, u32[]{:S(2)}) collective-permute-start(bf16[512,512]{1,0:T(8,128)(2,1)S(1)} %get-tuple-element.28.refs_0_), channel_id=1, source_target_pairs={{0,1},{1,2},{2,3},{3,0},{4,5},{5,6},{6,7},{7,4},{8,9},{9,10},{10,1... | collective-permute-start | bytes 1572872 | tf_op jit(solution)/shard_map/ppermute | solution.py:384
  21.9 40.5 %copy-start.2 = (bf16[512,512]{1,0:T(8,128)(2,1)}, bf16[512,512]{1,0:T(8,128)(2,1)S(1)}, u32[]{:S(2)}) copy-start(bf16[512,512]{1,0:T(8,128)(2,1)S(1)} %collective-permute-done.refs_0_) | copy-start | bytes 1572868
  21.9 20.0 %collective-permute-start.4 = (bf16[512,512]{1,0:T(8,128)(2,1)S(1)}, bf16[512,512]{1,0:T(8,128)(2,1)S(1)}, u32[]{:S(2)}, u32[]{:S(2)}) collective-permute-start(bf16[512,512]{1,0:T(8,128)(2,1)S(1)} %collective-permute-done.refs_0_), channel_id=1, source_target_pairs={{0,3},{1,0},{2,1},{3,2},{4,7},{5,4},{6,5},{7,6},{8,11},{9,8},{10,9... | collective-permute-start | bytes 1572872 | tf_op jit(solution)/shard_map/ppermute | solution.py:384
  26.0 19.8 %collective-permute-start.3 = (bf16[512,512]{1,0:T(8,128)(2,1)S(1)}, bf16[512,512]{1,0:T(8,128)(2,1)}, u32[]{:S(2)}, u32[]{:S(2)}) collective-permute-start(bf16[512,512]{1,0:T(8,128)(2,1)S(1)} %collective-permute-done.refs_0_), channel_id=1, source_target_pairs={{0,1},{1,2},{2,3},{3,0},{4,5},{5,6},{6,7},{7,4},{8,9},{9,10},{10,1... | collective-permute-start | bytes 1572872 | tf_op jit(solution)/shard_map/ppermute | solution.py:384
  31.2 31.2 %copy-start.3 = (bf16[512,512]{1,0:T(8,128)(2,1)}, bf16[512,512]{1,0:T(8,128)(2,1)S(1)}, u32[]{:S(2)}) copy-start(bf16[512,512]{1,0:T(8,128)(2,1)S(1)} %collective-permute-done.2.refs_3_) | copy-start | bytes 1572868
  41.9 0.8 copy-start.4
  46.6 10.5 %collective-permute-start.6 = (bf16[16,64,128]{2,1,0:T(8,128)(2,1)}, bf16[16,64,128]{2,1,0:T(8,128)(2,1)S(1)}, u32[]{:S(2)}, u32[]{:S(2)}) collective-permute-start(bf16[16,64,128]{2,1,0:T(8,128)(2,1)} %slice.6), channel_id=1, source_target_pairs={{0,8},{4,12},{8,16},{12,20},{16,24},{20,28},{24,32},{28,36},{32,40... | collective-permute-start | bytes 786440 | tf_op jit(solution)/shard_map/ppermute | solution.py:390
  49.9 9.0 %collective-permute-start.5 = (bf16[16,64,128]{2,1,0:T(8,128)(2,1)}, bf16[16,64,128]{2,1,0:T(8,128)(2,1)S(1)}, u32[]{:S(2)}, u32[]{:S(2)}) collective-permute-start(bf16[16,64,128]{2,1,0:T(8,128)(2,1)} %slice.6), channel_id=1, source_target_pairs={{0,4},{4,8},{8,12},{12,16},{16,20},{20,24},{24,28},{28,32},{32,36}... | collective-permute-start | bytes 786440 | tf_op jit(solution)/shard_map/ppermute | solution.py:390
  62.4 27.5 %all-to-all-start.1 = ((bf16[16,3,64,128]{3,2,1,0:T(8,128)(2,1)}), bf16[16,3,64,128]{3,2,1,0:T(8,128)(2,1)S(1)}, u32[]{:S(2)}, u32[]{:S(2)}) async-start(bf16[16,3,64,128]{3,2,1,0:T(8,128)(2,1)} %shard_map.112), calls=%async_computation.1 | async-start | bytes 1572864 | tf_op jit(solution)/shard_map/all_to_all | solution.py:433
  70.8 22.2 %collective-permute-start.8 = (bf16[512,512]{1,0:T(8,128)(2,1)}, bf16[512,512]{1,0:T(8,128)(2,1)S(1)}, u32[]{:S(2)}, u32[]{:S(2)}) collective-permute-start(bf16[512,512]{1,0:T(8,128)(2,1)} %collective-permute-done.1.refs_1_), channel_id=1, source_target_pairs={{0,1},{1,2},{2,3},{3,0},{4,5},{5,6},{6,7},{7,4},{8,9},{9,10},{10,1... | collective-permute-start | bytes 1572872 | tf_op jit(solution)/shard_map/ppermute | solution.py:431
  72.7 23.9 %collective-permute-start.7 = (bf16[512,512]{1,0:T(8,128)(2,1)}, bf16[512,512]{1,0:T(8,128)(2,1)S(1)}, u32[]{:S(2)}, u32[]{:S(2)}) collective-permute-start(bf16[512,512]{1,0:T(8,128)(2,1)} %copy-done.4), channel_id=1, source_target_pairs={{0,3},{1,0},{2,1},{3,2},{4,7},{5,4},{6,5},{7,6},{8,11},{9,8},{10,9... | collective-permute-start | bytes 1572872 | tf_op jit(solution)/shard_map/ppermute | solution.py:432
  90.6 6.0 %collective-permute-start.9 = (bf16[512,256]{1,0:T(8,128)(2,1)S(1)}, bf16[512,256]{1,0:T(8,128)(2,1)S(1)}, u32[]{:S(2)}, u32[]{:S(2)}) collective-permute-start(bf16[512,256]{1,0:T(8,128)(2,1)S(1)} %shard_map.113.refs_4_), channel_id=1, source_target_pairs={{0,4},{4,0},{1,5},{5,1},{2,6},{6,2},{3,7},{7,3},{8,12},{12,8},{9,1... | collective-permute-start | bytes 786440 | tf_op jit(solution)/shard_map/ppermute | solution.py:438
  93.0 0.8 copy-start.6
  96.6 0.8 copy-start.5

commit v5 on v3

--- a/solution.py
+++ b/solution.py
@@ -18,9 +18,10 @@
 QROWS = GROUP * BLK
 KV_AT = 2 * QROWS
 AUX_AT = KV_AT + SPAN * 2 * BLK
-AUX_ROWS = 16
+AUX_ROWS = 8
 ROWS = AUX_AT + AUX_ROWS
 UNIT_BLKS = PAD // BLK
+HOPS = (0, 1, 3, 2)
 
 
 def hadamard_signs(table_size):
@@ -216,25 +217,32 @@
 
 
 def first_product_kernel(*refs):
-    kv_ref, out_ref, input_scr, sems = refs[-4:]
-    for step, load in enumerate(load_all(refs[:-4], input_scr, sems)):
+    far_ref, kv_ref, out_ref, input_scr, sems = refs[-5:]
+    loads = load_all(refs[:-5], input_scr, sems)
+    last = len(loads)
+    out_ref[last] = jnp.dot(far_ref[...], kv_ref[...], preferred_element_type=jnp.float32)
+    for step, load in enumerate(loads):
         load.wait()
         out_ref[step] = jnp.dot(input_scr[step], kv_ref[...], preferred_element_type=jnp.float32)
 
 
 def product_kernel(where_ref, *refs):
-    other_refs = refs[:-7]
-    first_ref, kv_ref, had_ref, aux_ref, out_ref, input_scr, sems = refs[-7:]
-    loads = load_all(other_refs, input_scr, sems)
+    far_ref, first_ref, kv_ref, had_ref, aux_ref, out_ref, input_scr, sems = refs[-8:]
+    loads = load_all(refs[:-8], input_scr, sems)
     core, width = where_ref[0], where_ref[1]
     replicas = out_ref.shape[0]
     span = 2 * HB
-    parts = input_scr.shape[1] // span
+    parts = far_ref.shape[0] // span
     had = jnp.concatenate([had_ref[...].astype(jnp.float32)] * 2, axis=1)
-    for step, load in enumerate(loads):
-        source = (width + len(loads) - step) % len(loads)
-        load.wait()
-        grad = jnp.dot(input_scr[step], kv_ref[...], preferred_element_type=jnp.float32)
+    widths = len(HOPS)
+    for step in (widths - 1, *range(widths - 1)):
+        source = (width + widths - HOPS[step]) % widths
+        if step < len(loads):
+            loads[step].wait()
+            inputs = input_scr[step]
+        else:
+            inputs = far_ref[...]
+        grad = jnp.dot(inputs, kv_ref[...], preferred_element_type=jnp.float32)
         grad = grad + first_ref[step]
         for part in range(parts):
             line = source * parts + part
@@ -281,17 +289,8 @@
     return call
 
 
-def gather_ring(own, other):
-    count = lax.axis_size("tensor")
-    up = [(i, (i + 1) % count) for i in range(count)]
-    down = [(i, (i - 1) % count) for i in range(count)]
-    own_list = [own, lax.ppermute(own, "tensor", up)]
-    own_last = lax.ppermute(own, "tensor", down)
-    other_list = [other, lax.ppermute(other, "tensor", up)]
-    other_last = lax.ppermute(other, "tensor", down)
-    own_list += [lax.ppermute(own_list[1], "tensor", up), own_last]
-    other_list += [lax.ppermute(other_last, "tensor", down), other_last]
-    return own_list, other_list
+def around(count, step):
+    return [(i, (i + step) % count) for i in range(count)]
 
 
 def per_device(
@@ -346,8 +345,14 @@
     )
     swap = [(0, 1), (1, 0)]
     other_input = lax.ppermute(other_input, "core", swap)
-    own_list, other_list = gather_ring(own_input, other_input)
-    recv, own_list, other_list = lax.optimization_barrier((recv, own_list, other_list))
+    widths = lax.axis_size("tensor")
+    up, down = around(widths, 1), around(widths, -1)
+    near = [
+        lax.ppermute(array, "tensor", way)
+        for array in (own_input, other_input)
+        for way in (up, down)
+    ]
+    recv, near = lax.optimization_barrier((recv, near))
 
     order_grid = order_row.reshape(groups, slots)
     chunk_ids = (where - jnp.arange(SPAN, dtype=jnp.int32))[:, None, None]
@@ -377,6 +382,10 @@
             pltpu.VMEM((window, HD), jnp.float32),
         ),
     )(slot_map, starts, recv)
+    partial_grads, near = lax.optimization_barrier((partial_grads, near))
+    own_up, own_down, other_up, other_down = near
+    own_list = [own_input, own_up, own_down, lax.ppermute(own_up, "tensor", up)]
+    other_list = [other_input, other_up, other_down, lax.ppermute(other_down, "tensor", down)]
     returned = lax.all_to_all(partial_grads, context, split_axis=0, concat_axis=0, tiled=True)
     targets = lax.dynamic_slice_in_dim(order_row, where * slots, slots, 0) // slots
     own_kv = prefetched(collect_kernel, 1, jax.ShapeDtypeStruct((tokens, 2 * HD), low))(
@@ -385,22 +394,22 @@
     other_kv = lax.ppermute(own_kv, "core", swap)
 
     input_scratch = (
-        pltpu.VMEM((len(own_list), half, tokens), low),
-        pltpu.SemaphoreType.DMA((len(own_list),)),
+        pltpu.VMEM((widths - 1, half, tokens), low),
+        pltpu.SemaphoreType.DMA((widths - 1,)),
     )
     first_product = prefetched(
         first_product_kernel,
         0,
         jax.ShapeDtypeStruct((len(own_list), half, 2 * HD), jnp.float32),
         scratch=input_scratch,
-        in_place=len(own_list),
+        in_place=widths - 1,
     )(*own_list, own_kv)
     spread = prefetched(
         product_kernel,
         1,
         jax.ShapeDtypeStruct((replicas, lines, 2, HB // replicas, 2 * HD), low),
         scratch=input_scratch,
-        in_place=len(other_list),
+        in_place=widths - 1,
     )(
         jnp.stack([core, lax.axis_index("tensor")]),
         *other_list,

time: 145 us -> 143 us (0.986)
  waiting for transfers between devices: 41.1 us -> 38.5 us
    all_to_all x1, waiting for transfers between devices: 0.01 us -> 11.1 us  [per_device(): lax.all_to_all(packed, context, split_axis=0, concat_axis=0, tiled=True)]
    ppermute x6, waiting for transfers between devices: 20.5 us -> 12.9 us  [the longest x4 12.9 us: per_device(): lax.ppermute(array, 'tensor', way)]
    all_to_all x1, waiting for transfers between devices: 20.6 us -> 14.5 us  [per_device(): lax.all_to_all(partial_grads, context, split_axis=0, concat_axis=0, tiled...]
  transfers between devices with their start and end apart: 10 -> 10, of which waited for: 5 -> 6; matrix products, arithmetic and copies ran while one was open for 1% -> 1% of each run, Pallas kernels for 2% -> 4%
where the time goes in v5:
time: 143 us
  blocking collectives  42.3 us (30%)
  starting transfers between devices  41.5 us (29%)
  waiting for transfers between devices  38.5 us (27%)
  Pallas kernels  16.4 us (11%)
  other arithmetic  2.2 us (2%)
    all_to_all x1, blocking collectives, per_device(): lax.all_to_all(spread, ('dp', 'y'), split_axis=0, concat_axis=0, tiled=True)  42.3 us
    pallas_call x6, Pallas kernels, call(): pl.pallas_call(kernel, out_shape=out_shape, grid_spec=pltpu.PrefetchScala...  16.4 us
    all_to_all x1, waiting for transfers between devices, per_device(): lax.all_to_all(partial_grads, context, split_axis=0, concat_axis=0, tiled...  14.5 us
    ppermute x4, starting transfers between devices, per_device(): lax.ppermute(array, 'tensor', way)  14.1 us
    ppermute x4, waiting for transfers between devices, per_device(): lax.ppermute(array, 'tensor', way)  12.9 us
    all_to_all x1, waiting for transfers between devices, per_device(): lax.all_to_all(packed, context, split_axis=0, concat_axis=0, tiled=True)  11.1 us
    all_to_all x1, starting transfers between devices, per_device(): lax.all_to_all(partial_grads, context, split_axis=0, concat_axis=0, tiled...  7.37 us
    all_to_all x1, starting transfers between devices, per_device(): lax.all_to_all(packed, context, split_axis=0, concat_axis=0, tiled=True)  7.35 us
  transfers between devices with their start and end apart: 10, of which 6 were waited for; matrix products, arithmetic and copies ran while one was open for 1% of the time, Pallas kernels for 4%

profile of v5, /device:TPU:6, one launch (start us, length us, event | category | flops | bytes accessed | tf_op | source)
XLA Modules:
  0.0 142.6 jit_solution(12603340120094861075)
XLA Ops:
  0.0 2.8 %shard_map.109 = bf16[16,456,128]{2,1,0:T(8,128)(2,1)} custom-call(s32[1]{0:T(128)} %bitcast.2.where_ref, bf16[1,4,512,128]{3,2,1,0:T(8,128)(2,1)} %refs_0_.1, bf16[1,4,512,128]{3,2,1,0:T(8,128)(2,1)} %refs_1_.1, bf16[1,1,512,128]{3,2,1,0:T(8,128)(2,1)} %refs_2_.1, bf16[1,1,512,128]{3,2,1,0:T(8,128)(2,1)} %refs_3_.1, bf16[1,4,512]{2,1,0:T(4,128)(2,1)} %refs_4_.1, ...), custom_call_target="tpu_custom_call" | custom-call | tf_op jit(solution)/shard_map/pallas_call | solution.py:277
  2.9 7.3 %all-to-all-start = ((bf16[16,456,128]{2,1,0:T(8,128)(2,1)}), bf16[16,456,128]{2,1,0:T(8,128)(2,1)S(1)}, u32[]{:S(2)}, u32[]{:S(2)}) async-start(bf16[16,456,128]{2,1,0:T(8,128)(2,1)} %shard_map.109), calls=%async_computation | async-start | bytes 3735552 | tf_op jit(solution)/shard_map/all_to_all | solution.py:339
  10.3 1.1 shard_map.110
  11.4 2.3 %collective-permute-start = (bf16[512,512]{1,0:T(8,128)(2,1)}, bf16[512,512]{1,0:T(8,128)(2,1)S(1)}, u32[]{:S(2)}, u32[]{:S(2)}) collective-permute-start(bf16[512,512]{1,0:T(8,128)(2,1)} %get-tuple-element.20), channel_id=1, source_target_pairs={{0,4},{4,0},{1,5},{5,1},{2,6},{6,2},{3,7},{7,3},{8,12},{12,8},{9,1... | collective-permute-start | bytes 1572872 | tf_op jit(solution)/shard_map/ppermute | solution.py:347
  13.7 2.7 %collective-permute-start.2 = (bf16[512,512]{1,0:T(8,128)(2,1)S(1)}, bf16[512,512]{1,0:T(8,128)(2,1)S(1)}, u32[]{:S(2)}, u32[]{:S(2)}) collective-permute-start(bf16[512,512]{1,0:T(8,128)(2,1)S(1)} %get-tuple-element.22.refs_0_), channel_id=1, source_target_pairs={{0,3},{1,0},{2,1},{3,2},{4,7},{5,4},{6,5},{7,6},{8,11},{9,8},{10,9... | collective-permute-start | bytes 1572872 | tf_op jit(solution)/shard_map/ppermute | solution.py:351
  16.4 4.3 %collective-permute-start.1 = (bf16[512,512]{1,0:T(8,128)(2,1)S(1)}, bf16[512,512]{1,0:T(8,128)(2,1)}, u32[]{:S(2)}, u32[]{:S(2)}) collective-permute-start(bf16[512,512]{1,0:T(8,128)(2,1)S(1)} %get-tuple-element.22.refs_0_), channel_id=1, source_target_pairs={{0,1},{1,2},{2,3},{3,0},{4,5},{5,6},{6,7},{7,4},{8,9},{9,10},{10,1... | collective-permute-start | bytes 1572872 | tf_op jit(solution)/shard_map/ppermute | solution.py:351
  22.2 1.9 %collective-permute-start.4 = (bf16[512,512]{1,0:T(8,128)(2,1)S(1)}, bf16[512,512]{1,0:T(8,128)(2,1)S(1)}, u32[]{:S(2)}, u32[]{:S(2)}) collective-permute-start(bf16[512,512]{1,0:T(8,128)(2,1)S(1)} %collective-permute-done.refs_0_), channel_id=1, source_target_pairs={{0,3},{1,0},{2,1},{3,2},{4,7},{5,4},{6,5},{7,6},{8,11},{9,8},{10,9... | collective-permute-start | bytes 1572872 | tf_op jit(solution)/shard_map/ppermute | solution.py:351
  24.1 5.1 %collective-permute-start.3 = (bf16[512,512]{1,0:T(8,128)(2,1)S(1)}, bf16[512,512]{1,0:T(8,128)(2,1)}, u32[]{:S(2)}, u32[]{:S(2)}) collective-permute-start(bf16[512,512]{1,0:T(8,128)(2,1)S(1)} %collective-permute-done.refs_0_), channel_id=1, source_target_pairs={{0,1},{1,2},{2,3},{3,0},{4,5},{5,6},{6,7},{7,4},{8,9},{9,10},{10,1... | collective-permute-start | bytes 1572872 | tf_op jit(solution)/shard_map/ppermute | solution.py:351
  29.7 1.9 %collective-permute-done.2.refs_2_ = bf16[512,512]{1,0:T(8,128)(2,1)S(1)} collective-permute-done((bf16[512,512]{1,0:T(8,128)(2,1)S(1)}, bf16[512,512]{1,0:T(8,128)(2,1)S(1)}, u32[]{:S(2)}, u32[]{:S(2)}) %collective-permute-start.2) | collective-permute-done | bytes 524320 | tf_op jit(solution)/shard_map/ppermute | solution.py:351
  31.6 1.7 %collective-permute-done.1.refs_1_ = bf16[512,512]{1,0:T(8,128)(2,1)} collective-permute-done((bf16[512,512]{1,0:T(8,128)(2,1)S(1)}, bf16[512,512]{1,0:T(8,128)(2,1)}, u32[]{:S(2)}, u32[]{:S(2)}) %collective-permute-start.1) | collective-permute-done | bytes 524320 | tf_op jit(solution)/shard_map/ppermute | solution.py:351
  33.3 8.7 %collective-permute-done.4.refs_2_ = bf16[512,512]{1,0:T(8,128)(2,1)S(1)} collective-permute-done((bf16[512,512]{1,0:T(8,128)(2,1)S(1)}, bf16[512,512]{1,0:T(8,128)(2,1)S(1)}, u32[]{:S(2)}, u32[]{:S(2)}) %collective-permute-start.4) | collective-permute-done | bytes 524320 | tf_op jit(solution)/shard_map/ppermute | solution.py:351
  42.0 0.8 copy-done.4
  43.3 11.1 %all-to-all-done.recv_ref = bf16[16,456,128]{2,1,0:T(8,128)(2,1)S(1)} async-done(((bf16[16,456,128]{2,1,0:T(8,128)(2,1)}), bf16[16,456,128]{2,1,0:T(8,128)(2,1)S(1)}, u32[]{:S(2)}, u32[]{:S(2)}) %all-to-all-start) | async-done | bytes 1867808 | tf_op jit(solution)/shard_map/all_to_all | solution.py:339
  54.5 5.0 %shard_map.111 = bf16[16,3,64,128]{3,2,1,0:T(8,128)(2,1)} custom-call(s32[3,16]{1,0:T(4,128)S(1)} %select_reduce_fusion.slot_ref, s32[4]{0:T(128)S(1)} %broadcast_subtract_fusion.start_ref, bf16[16,456,128]{2,1,0:T(8,128)(2,1)S(1)} %all-to-all-done.recv_ref), custom_call_target="tpu_custom_call" | custom-call | tf_op jit(solution)/shard_map/pallas_call | solution.py:277
  59.5 7.4 %all-to-all-start.1 = ((bf16[16,3,64,128]{3,2,1,0:T(8,128)(2,1)}), bf16[16,3,64,128]{3,2,1,0:T(8,128)(2,1)S(1)}, u32[]{:S(2)}, u32[]{:S(2)}) async-start(bf16[16,3,64,128]{3,2,1,0:T(8,128)(2,1)} %shard_map.111), calls=%async_computation.1 | async-start | bytes 1572864 | tf_op jit(solution)/shard_map/all_to_all | solution.py:389
  66.8 4.2 %collective-permute-start.6 = (bf16[512,512]{1,0:T(8,128)(2,1)}, bf16[512,512]{1,0:T(8,128)(2,1)}, u32[]{:S(2)}, u32[]{:S(2)}) collective-permute-start(bf16[512,512]{1,0:T(8,128)(2,1)} %collective-permute-done.1.refs_1_), channel_id=1, source_target_pairs={{0,1},{1,2},{2,3},{3,0},{4,5},{5,6},{6,7},{7,4},{8,9},{9,10},{10,1... | collective-permute-start | bytes 1572872 | tf_op jit(solution)/shard_map/ppermute | solution.py:387
  71.0 1.9 %collective-permute-start.5 = (bf16[512,512]{1,0:T(8,128)(2,1)}, bf16[512,512]{1,0:T(8,128)(2,1)S(1)}, u32[]{:S(2)}, u32[]{:S(2)}) collective-permute-start(bf16[512,512]{1,0:T(8,128)(2,1)} %copy-done.4), channel_id=1, source_target_pairs={{0,3},{1,0},{2,1},{3,2},{4,7},{5,4},{6,5},{7,6},{8,11},{9,8},{10,9... | collective-permute-start | bytes 1572872 | tf_op jit(solution)/shard_map/ppermute | solution.py:388
  73.0 14.5 %all-to-all-done.1.recv_ref = bf16[16,3,64,128]{3,2,1,0:T(8,128)(2,1)S(1)} async-done(((bf16[16,3,64,128]{3,2,1,0:T(8,128)(2,1)}), bf16[16,3,64,128]{3,2,1,0:T(8,128)(2,1)S(1)}, u32[]{:S(2)}, u32[]{:S(2)}) %all-to-all-start.1) | async-done | bytes 786464 | tf_op jit(solution)/shard_map/all_to_all | solution.py:389
  87.5 0.7 shard_map.112.refs_4_
  88.2 4.3 %collective-permute-start.7 = (bf16[512,256]{1,0:T(8,128)(2,1)S(1)}, bf16[512,256]{1,0:T(8,128)(2,1)S(1)}, u32[]{:S(2)}, u32[]{:S(2)}) collective-permute-start(bf16[512,256]{1,0:T(8,128)(2,1)S(1)} %shard_map.112.refs_4_), channel_id=1, source_target_pairs={{0,4},{4,0},{1,5},{5,1},{2,6},{6,2},{3,7},{7,3},{8,12},{12,8},{9,1... | collective-permute-start | bytes 786440 | tf_op jit(solution)/shard_map/ppermute | solution.py:394
  92.7 3.4 %shard_map.113.refs_4_ = f32[4,512,256]{2,1,0:T(8,128)S(1)} custom-call(bf16[512,512]{1,0:T(8,128)(2,1)} %copy-done.1, bf16[512,512]{1,0:T(8,128)(2,1)} %collective-permute-done.1.refs_1_, bf16[512,512]{1,0:T(8,128)(2,1)} %copy-done.3, bf16[512,512]{1,0:T(8,128)(2,1)} %collective-permute-done.6.refs_3_, bf16[512,256]{1,0:T(8,128)(2,1)S(1)} %shard_map.112.refs_4_), custom_call_target="tpu_custom_call" | custom-call | tf_op jit(solution)/shard_map/pallas_call | solution.py:277
  96.1 3.4 %shard_map.114 = bf16[8,8,2,16,256]{4,3,2,1,0:T(8,128)(2,1)S(1)} custom-call(s32[2]{0:T(128)S(1)} %pad_add_fusion.where_ref, bf16[512,512]{1,0:T(8,128)(2,1)} %copy-done.2, bf16[512,512]{1,0:T(8,128)(2,1)} %collective-permute-done.3.refs_1_, bf16[512,512]{1,0:T(8,128)(2,1)} %copy-done.4, bf16[512,512]{1,0:T(8,128)(2,1)S(1)} %collective-permute-done.5.refs_3_, ...), custom_call_target="tpu_custom_call" | custom-call | tf_op jit(solution)/shard_map/pallas_call | solution.py:277
  99.5 42.3 %all_to_all.15 = bf16[64,2,16,256]{3,2,1,0:T(8,128)(2,1)S(1)} all-to-all(bf16[64,2,16,256]{3,2,1,0:T(8,128)(2,1)S(1)} %bitcast.15), channel_id=1, replica_groups=mesh['dp'=8,'y'=8,'core'=2,'tensor'=4] {'dp','y'}, dimensions={0} | all-to-all | bytes 2097152 | tf_op jit(solution)/shard_map/all_to_all | solution.py:422
  141.8 0.8 convert_reduce_fusion
  (32 shorter events, 2.6 us)
Async XLA Ops:
  2.9 7.4 %copy-start = (bf16[1,512,1024]{2,1,0:T(8,128)(2,1)S(1)}, bf16[1,512,1024]{2,1,0:T(8,128)(2,1)}, u32[]{:S(2)}) copy-start(bf16[1,512,1024]{2,1,0:T(8,128)(2,1)} %param.11) | copy-start | bytes 3145732
  2.9 17.9 %copy-start.6 = (s32[1,10]{1,0:T(1,128)S(1)}, s32[1,10]{1,0:T(1,128)}, u32[]{:S(2)}) copy-start(s32[1,10]{1,0:T(1,128)} %param.18) | copy-start | bytes 124
  2.9 18.6 %copy-start.5 = (s32[1,256]{1,0:T(1,128)S(1)}, s32[1,256]{1,0:T(1,128)}, u32[]{:S(2)}) copy-start(s32[1,256]{1,0:T(1,128)} %refs_7_.1) | copy-start | bytes 3076
  2.9 51.6 %all-to-all-start = ((bf16[16,456,128]{2,1,0:T(8,128)(2,1)}), bf16[16,456,128]{2,1,0:T(8,128)(2,1)S(1)}, u32[]{:S(2)}, u32[]{:S(2)}) async-start(bf16[16,456,128]{2,1,0:T(8,128)(2,1)} %shard_map.109), calls=%async_computation | async-start | bytes 3735552 | tf_op jit(solution)/shard_map/all_to_all | solution.py:339
  11.4 48.1 %copy-start.1 = (bf16[512,512]{1,0:T(8,128)(2,1)}, bf16[512,512]{1,0:T(8,128)(2,1)S(1)}, u32[]{:S(2)}) copy-start(bf16[512,512]{1,0:T(8,128)(2,1)S(1)} %get-tuple-element.22.refs_0_) | copy-start | bytes 1572868
  11.4 10.8 %collective-permute-start = (bf16[512,512]{1,0:T(8,128)(2,1)}, bf16[512,512]{1,0:T(8,128)(2,1)S(1)}, u32[]{:S(2)}, u32[]{:S(2)}) collective-permute-start(bf16[512,512]{1,0:T(8,128)(2,1)} %get-tuple-element.20), channel_id=1, source_target_pairs={{0,4},{4,0},{1,5},{5,1},{2,6},{6,2},{3,7},{7,3},{8,12},{12,8},{9,1... | collective-permute-start | bytes 1572872 | tf_op jit(solution)/shard_map/ppermute | solution.py:347
  13.7 17.9 %collective-permute-start.2 = (bf16[512,512]{1,0:T(8,128)(2,1)S(1)}, bf16[512,512]{1,0:T(8,128)(2,1)S(1)}, u32[]{:S(2)}, u32[]{:S(2)}) collective-permute-start(bf16[512,512]{1,0:T(8,128)(2,1)S(1)} %get-tuple-element.22.refs_0_), channel_id=1, source_target_pairs={{0,3},{1,0},{2,1},{3,2},{4,7},{5,4},{6,5},{7,6},{8,11},{9,8},{10,9... | collective-permute-start | bytes 1572872 | tf_op jit(solution)/shard_map/ppermute | solution.py:351
  16.4 16.8 %collective-permute-start.1 = (bf16[512,512]{1,0:T(8,128)(2,1)S(1)}, bf16[512,512]{1,0:T(8,128)(2,1)}, u32[]{:S(2)}, u32[]{:S(2)}) collective-permute-start(bf16[512,512]{1,0:T(8,128)(2,1)S(1)} %get-tuple-element.22.refs_0_), channel_id=1, source_target_pairs={{0,1},{1,2},{2,3},{3,0},{4,5},{5,6},{6,7},{7,4},{8,9},{9,10},{10,1... | collective-permute-start | bytes 1572872 | tf_op jit(solution)/shard_map/ppermute | solution.py:351
  22.2 37.3 %copy-start.2 = (bf16[512,512]{1,0:T(8,128)(2,1)}, bf16[512,512]{1,0:T(8,128)(2,1)S(1)}, u32[]{:S(2)}) copy-start(bf16[512,512]{1,0:T(8,128)(2,1)S(1)} %collective-permute-done.refs_0_) | copy-start | bytes 1572868
  22.2 19.8 %collective-permute-start.4 = (bf16[512,512]{1,0:T(8,128)(2,1)S(1)}, bf16[512,512]{1,0:T(8,128)(2,1)S(1)}, u32[]{:S(2)}, u32[]{:S(2)}) collective-permute-start(bf16[512,512]{1,0:T(8,128)(2,1)S(1)} %collective-permute-done.refs_0_), channel_id=1, source_target_pairs={{0,3},{1,0},{2,1},{3,2},{4,7},{5,4},{6,5},{7,6},{8,11},{9,8},{10,9... | collective-permute-start | bytes 1572872 | tf_op jit(solution)/shard_map/ppermute | solution.py:351
  24.1 19.2 %collective-permute-start.3 = (bf16[512,512]{1,0:T(8,128)(2,1)S(1)}, bf16[512,512]{1,0:T(8,128)(2,1)}, u32[]{:S(2)}, u32[]{:S(2)}) collective-permute-start(bf16[512,512]{1,0:T(8,128)(2,1)S(1)} %collective-permute-done.refs_0_), channel_id=1, source_target_pairs={{0,1},{1,2},{2,3},{3,0},{4,5},{5,6},{6,7},{7,4},{8,9},{9,10},{10,1... | collective-permute-start | bytes 1572872 | tf_op jit(solution)/shard_map/ppermute | solution.py:351
  31.6 27.9 %copy-start.3 = (bf16[512,512]{1,0:T(8,128)(2,1)}, bf16[512,512]{1,0:T(8,128)(2,1)S(1)}, u32[]{:S(2)}) copy-start(bf16[512,512]{1,0:T(8,128)(2,1)S(1)} %collective-permute-done.2.refs_2_) | copy-start | bytes 1572868
  42.0 0.8 copy-start.4
  59.5 28.1 %all-to-all-start.1 = ((bf16[16,3,64,128]{3,2,1,0:T(8,128)(2,1)}), bf16[16,3,64,128]{3,2,1,0:T(8,128)(2,1)S(1)}, u32[]{:S(2)}, u32[]{:S(2)}) async-start(bf16[16,3,64,128]{3,2,1,0:T(8,128)(2,1)} %shard_map.111), calls=%async_computation.1 | async-start | bytes 1572864 | tf_op jit(solution)/shard_map/all_to_all | solution.py:389
  66.8 25.9 %collective-permute-start.6 = (bf16[512,512]{1,0:T(8,128)(2,1)}, bf16[512,512]{1,0:T(8,128)(2,1)}, u32[]{:S(2)}, u32[]{:S(2)}) collective-permute-start(bf16[512,512]{1,0:T(8,128)(2,1)} %collective-permute-done.1.refs_1_), channel_id=1, source_target_pairs={{0,1},{1,2},{2,3},{3,0},{4,5},{5,6},{6,7},{7,4},{8,9},{9,10},{10,1... | collective-permute-start | bytes 1572872 | tf_op jit(solution)/shard_map/ppermute | solution.py:387
  71.0 25.1 %collective-permute-start.5 = (bf16[512,512]{1,0:T(8,128)(2,1)}, bf16[512,512]{1,0:T(8,128)(2,1)S(1)}, u32[]{:S(2)}, u32[]{:S(2)}) collective-permute-start(bf16[512,512]{1,0:T(8,128)(2,1)} %copy-done.4), channel_id=1, source_target_pairs={{0,3},{1,0},{2,1},{3,2},{4,7},{5,4},{6,5},{7,6},{8,11},{9,8},{10,9... | collective-permute-start | bytes 1572872 | tf_op jit(solution)/shard_map/ppermute | solution.py:388
  88.2 7.9 %collective-permute-start.7 = (bf16[512,256]{1,0:T(8,128)(2,1)S(1)}, bf16[512,256]{1,0:T(8,128)(2,1)S(1)}, u32[]{:S(2)}, u32[]{:S(2)}) collective-permute-start(bf16[512,256]{1,0:T(8,128)(2,1)S(1)} %shard_map.112.refs_4_), channel_id=1, source_target_pairs={{0,4},{4,0},{1,5},{5,1},{2,6},{6,2},{3,7},{7,3},{8,12},{12,8},{9,1... | collective-permute-start | bytes 786440 | tf_op jit(solution)/shard_map/ppermute | solution.py:394

commit v6 on v4

--- a/solution.py
+++ b/solution.py
@@ -1,3 +1,5 @@
+import functools
+
 import jax
 import jax.numpy as jnp
 from jax import lax
@@ -13,14 +15,16 @@
 HB = 128
 CORES = 2
 SPAN = 3
+SENT = (0, 2)
 LOG2E = 1.4426950408889634
 
 QROWS = GROUP * BLK
 KV_AT = 2 * QROWS
-AUX_AT = KV_AT + 2 * BLK
-AUX_ROWS = 16
+AUX_AT = KV_AT + len(SENT) * 2 * BLK
+AUX_ROWS = 8
 ROWS = AUX_AT + AUX_ROWS
 UNIT_BLKS = PAD // BLK
+HOPS = (0, 1, 3, 2)
 
 
 def hadamard_signs(table_size):
@@ -88,8 +92,14 @@
             packed_scr[dest, head * BLK : (head + 1) * BLK, :] = query_scr[0, head, rows, :]
             at = QROWS + head * BLK
             packed_scr[dest, at : at + BLK, :] = grad_scr[0, head, rows, :]
-        packed_scr[dest, KV_AT : KV_AT + BLK, :] = key_scr[0, 0, rows, :]
-        packed_scr[dest, KV_AT + BLK : AUX_AT, :] = value_scr[0, 0, rows, :]
+        for place, span in enumerate(SENT):
+            at = KV_AT + place * 2 * BLK
+            if dest >= span:
+                rows = pl.ds(pl.multiple_of(held_scr[dest - span] * BLK, BLK), BLK)
+                packed_scr[dest, at : at + BLK, :] = key_scr[0, 0, rows, :]
+                packed_scr[dest, at + BLK : at + 2 * BLK, :] = value_scr[0, 0, rows, :]
+            else:
+                packed_scr[dest, at : at + 2 * BLK, :] = jnp.zeros((2 * BLK, HD), out_ref.dtype)
         packed_scr[dest, AUX_AT:ROWS, :] = aux_scr[slot]
         stores.append(pltpu.make_async_copy(packed_scr.at[dest], out_ref.at[dest], out_sem.at[dest]))
         stores[-1].start()
@@ -97,7 +107,7 @@
         store.wait()
 
 
-def pair_grads(key_blk, value_blk, query_refs, cols, lse, dots, live):
+def block_grads(key_blk, value_blk, query_refs, cols, lse, dots, live):
     query_ref, grad_ref, query_turned, grad_turned = query_refs
     scores = jnp.dot(key_blk, query_turned[:, cols], preferred_element_type=jnp.float32)
     dprobs = jnp.dot(value_blk, grad_turned[:, cols], preferred_element_type=jnp.float32)
@@ -117,15 +127,26 @@
     return lse, dots
 
 
+def rows_of(slot_ref, span, src):
+    return pl.ds(pl.multiple_of(slot_ref[span, src] * BLK, BLK), BLK)
+
+
+def store_slab(slot_ref, span, dkey_scr, dvalue_scr, out_ref):
+    for src in range(out_ref.shape[0]):
+        rows = rows_of(slot_ref, span, src)
+        dkey = dkey_scr[rows, :] * HD ** (-0.5)
+        out_ref[src, 0:BLK, :] = dkey.astype(out_ref.dtype)
+        out_ref[src, BLK : 2 * BLK, :] = dvalue_scr[rows, :].astype(out_ref.dtype)
+
+
 def own_attend_kernel(
     slot_ref, start_ref, recv_ref,
     query_ref, grad_ref, query_turned, grad_turned, stat_ref, out_ref,
     key_scr, value_scr, dkey_scr, dvalue_scr,
 ):
-    groups = recv_ref.shape[0]
     units = key_scr.shape[0] // PAD
     width = UNIT_BLKS * QROWS
-    for src in range(groups):
+    for src in range(recv_ref.shape[0]):
         slot = slot_ref[0, src]
         at = pl.multiple_of(slot * QROWS, QROWS)
         query_blk = recv_ref[src, 0:QROWS, :]
@@ -135,9 +156,9 @@
         query_turned[:, pl.ds(at, QROWS)] = query_blk.T
         grad_turned[:, pl.ds(at, QROWS)] = grad_blk.T
         stat_ref[slot] = recv_ref[src, AUX_AT:ROWS, :].astype(jnp.float32)
-        row = pl.multiple_of(slot * BLK, BLK)
-        key_scr[pl.ds(row, BLK), :] = recv_ref[src, KV_AT : KV_AT + BLK, :]
-        value_scr[pl.ds(row, BLK), :] = recv_ref[src, KV_AT + BLK : AUX_AT, :]
+        rows = rows_of(slot_ref, 0, src)
+        key_scr[rows, :] = recv_ref[src, KV_AT : KV_AT + BLK, :]
+        value_scr[rows, :] = recv_ref[src, KV_AT + BLK : KV_AT + 2 * BLK, :]
 
     queries = (query_ref, grad_ref, query_turned, grad_turned)
     dkey_scr[...] = jnp.zeros_like(dkey_scr)
@@ -151,53 +172,37 @@
         query_at = unit * PAD + (column // QROWS) * BLK + column % BLK
         first = (start_ref[unit] - (SPAN - 1) * units) * PAD
         live = (key_at <= query_at) & (key_at >= first)
-        key_part, value_part = pair_grads(
+        key_part, value_part = block_grads(
             key_scr[rows, :], value_scr[rows, :], queries, cols, lse, dots, live
         )
         dkey_scr[rows, :] += key_part
         dvalue_scr[rows, :] += value_part
-
-    for src in range(groups):
-        rows = pl.ds(pl.multiple_of(slot_ref[0, src] * BLK, BLK), BLK)
-        dkey = dkey_scr[rows, :] * HD ** (-0.5)
-        out_ref[src, 0:BLK, :] = dkey.astype(out_ref.dtype)
-        out_ref[src, BLK : 2 * BLK, :] = dvalue_scr[rows, :].astype(out_ref.dtype)
-
-
-def earlier_attend_kernel(slot_ref, start_ref, *refs):
-    earlier_refs, refs = refs[: SPAN - 1], refs[SPAN - 1 :]
-    query_ref, grad_ref, query_turned, grad_turned, stat_ref, own_ref, out_ref = refs[:7]
-    key_scr, value_scr, dkey_scr, dvalue_scr = refs[7:]
-    groups = out_ref.shape[0]
-    chunk = key_scr.shape[0] // (SPAN - 1)
-    units = chunk // PAD
+    store_slab(slot_ref, 0, dkey_scr, dvalue_scr, out_ref)
+
+
+def earlier_attend_kernel(span, slot_ref, start_ref, kv_ref, *refs):
+    queries, refs = refs[:4], refs[4:]
+    stat_ref, out_ref, key_scr, value_scr, dkey_scr, dvalue_scr = refs
+    units = key_scr.shape[0] // PAD
     width = UNIT_BLKS * QROWS
     pair = 2 * PAD
-    edge = (SPAN - 1) * units
-
-    def rows_of(span, src):
-        row = (SPAN - 1 - span) * chunk + slot_ref[span, src] * BLK
-        return pl.ds(pl.multiple_of(row, BLK), BLK)
-
-    for src in range(groups):
-        for span in range(1, SPAN):
-            rows = rows_of(span, src)
-            key_scr[rows, :] = earlier_refs[span - 1][src, 0:BLK, :]
-            value_scr[rows, :] = earlier_refs[span - 1][src, BLK : 2 * BLK, :]
+    for src in range(kv_ref.shape[0]):
+        rows = rows_of(slot_ref, span, src)
+        key_scr[rows, :] = kv_ref[src, 0:BLK, :]
+        value_scr[rows, :] = kv_ref[src, BLK : 2 * BLK, :]
     dkey_scr[...] = jnp.zeros_like(dkey_scr)
     dvalue_scr[...] = jnp.zeros_like(dvalue_scr)
-    queries = (query_ref, grad_ref, query_turned, grad_turned)
     key_at = lax.broadcasted_iota(jnp.int32, (pair, width), 0)
     for unit in range(units):
         cols = slice(unit * width, (unit + 1) * width)
         lse, dots = unit_stats(stat_ref, unit)
-        first = jnp.minimum(start_ref[unit], edge)
-
-        @pl.loop(0, (edge - first + 1) // 2)
+        first = jnp.clip(start_ref[unit] - (SPAN - 1 - span) * units, 0, units)
+
+        @pl.loop(0, (units - first + 1) // 2)
         def _(step):
-            base = edge - 2 - 2 * step
+            base = units - 2 - 2 * step
             rows = pl.ds(pl.multiple_of(base * PAD, pair), pair)
-            key_part, value_part = pair_grads(
+            key_part, value_part = block_grads(
                 key_scr[rows, :],
                 value_scr[rows, :],
                 queries,
@@ -209,13 +214,17 @@
             dkey_scr[rows, :] += key_part
             dvalue_scr[rows, :] += value_part
 
-    for src in range(groups):
-        out_ref[src, 0] = own_ref[src]
-        for span in range(1, SPAN):
-            rows = rows_of(span, src)
-            dkey = dkey_scr[rows, :] * HD ** (-0.5)
-            out_ref[src, span, 0:BLK, :] = dkey.astype(out_ref.dtype)
-            out_ref[src, span, BLK : 2 * BLK, :] = dvalue_scr[rows, :].astype(out_ref.dtype)
+    store_slab(slot_ref, span, dkey_scr, dvalue_scr, out_ref)
+
+
+def merge_kernel(core_ref, own_ref, far_ref, shared_ref, out_ref):
+    core = core_ref[0]
+    for src in range(out_ref.shape[0]):
+        shared = shared_ref[src].astype(jnp.float32)
+        own = own_ref[src] + jnp.where(core == 0, shared, 0.0)
+        far = far_ref[src] + jnp.where(core == 0, 0.0, shared)
+        out_ref[src, 0] = own.astype(out_ref.dtype)
+        out_ref[src, 1] = far.astype(out_ref.dtype)
 
 
 def collect_kernel(target_ref, recv_ref, out_ref):
@@ -223,9 +232,9 @@
     for slot in range(out_ref.shape[0] // BLK):
         owner = target_ref[slot]
         total = recv_ref[owner, 0].astype(jnp.float32)
-        for span in range(1, SPAN):
-            extra = recv_ref[jnp.minimum(owner + span, groups - 1), span].astype(jnp.float32)
-            total = total + jnp.where(owner + span < groups, extra, 0.0)
+        later = owner + SENT[1]
+        extra = recv_ref[jnp.minimum(later, groups - 1), 1].astype(jnp.float32)
+        total = total + jnp.where(later < groups, extra, 0.0)
         rows = slice(slot * BLK, (slot + 1) * BLK)
         total = total.astype(out_ref.dtype)
         out_ref[rows, 0:HD] = total[0:BLK]
@@ -253,25 +262,32 @@
 
 
 def first_product_kernel(*refs):
-    kv_ref, out_ref, input_scr, sems = refs[-4:]
-    for step, load in enumerate(load_all(refs[:-4], input_scr, sems)):
+    far_ref, kv_ref, out_ref, input_scr, sems = refs[-5:]
+    loads = load_all(refs[:-5], input_scr, sems)
+    last = len(loads)
+    out_ref[last] = jnp.dot(far_ref[...], kv_ref[...], preferred_element_type=jnp.float32)
+    for step, load in enumerate(loads):
         load.wait()
         out_ref[step] = jnp.dot(input_scr[step], kv_ref[...], preferred_element_type=jnp.float32)
 
 
 def product_kernel(where_ref, *refs):
-    other_refs = refs[:-7]
-    first_ref, kv_ref, had_ref, aux_ref, out_ref, input_scr, sems = refs[-7:]
-    loads = load_all(other_refs, input_scr, sems)
+    far_ref, first_ref, kv_ref, had_ref, aux_ref, out_ref, input_scr, sems = refs[-8:]
+    loads = load_all(refs[:-8], input_scr, sems)
     core, width = where_ref[0], where_ref[1]
     replicas = out_ref.shape[0]
     span = 2 * HB
-    parts = input_scr.shape[1] // span
+    parts = far_ref.shape[0] // span
     had = jnp.concatenate([had_ref[...].astype(jnp.float32)] * 2, axis=1)
-    for step, load in enumerate(loads):
-        source = (width + len(loads) - step) % len(loads)
-        load.wait()
-        grad = jnp.dot(input_scr[step], kv_ref[...], preferred_element_type=jnp.float32)
+    widths = len(HOPS)
+    for step in (widths - 1, *range(widths - 1)):
+        source = (width + widths - HOPS[step]) % widths
+        if step < len(loads):
+            loads[step].wait()
+            inputs = input_scr[step]
+        else:
+            inputs = far_ref[...]
+        grad = jnp.dot(inputs, kv_ref[...], preferred_element_type=jnp.float32)
         grad = grad + first_ref[step]
         for part in range(parts):
             line = source * parts + part
@@ -320,10 +336,6 @@
 
 def around(count, step):
     return [(i, (i + step) % count) for i in range(count)]
-
-
-def onward(count, step):
-    return [(i, i + step) for i in range(count - step)]
 
 
 def per_device(
@@ -386,8 +398,6 @@
         for way in (up, down)
     ]
     recv, near = lax.optimization_barrier((recv, near))
-    held = recv[:, KV_AT:AUX_AT]
-    earlier = [lax.ppermute(held, context, onward(groups, span)) for span in range(1, SPAN)]
 
     order_grid = order_row.reshape(groups, slots)
     chunk_ids = (where - jnp.arange(SPAN, dtype=jnp.int32))[:, None, None]
@@ -400,9 +410,15 @@
     doc_start = jnp.max(jnp.where(ends[None, :] <= unit_ids[:, None], ends[None, :], 0), axis=1)
     starts = doc_start - (where - (SPAN - 1)) * chunk_units
 
+    at = KV_AT + lax.axis_index("core") * 2 * BLK
+    shared_kv = lax.ppermute(lax.dynamic_slice_in_dim(recv, at, 2 * BLK, 1), "core", swap)
     sorted_rows = jax.ShapeDtypeStruct((slots * QROWS, HD), low)
     turned_rows = jax.ShapeDtypeStruct((HD, slots * QROWS), low)
-    own_work = prefetched(
+    slab = (groups, 2 * BLK, HD)
+    chunk_scratch = tuple(
+        pltpu.VMEM((tokens, HD), dtype) for dtype in (low, low, jnp.float32, jnp.float32)
+    )
+    *shared_work, own_slab = prefetched(
         own_attend_kernel,
         2,
         (
@@ -411,25 +427,30 @@
             turned_rows,
             turned_rows,
             jax.ShapeDtypeStruct((slots, AUX_ROWS, HD), jnp.float32),
-            jax.ShapeDtypeStruct((groups, 2 * BLK, HD), low),
+            jax.ShapeDtypeStruct(slab, jnp.float32),
         ),
-        scratch=tuple(
-            pltpu.VMEM((tokens, HD), dtype) for dtype in (low, low, jnp.float32, jnp.float32)
-        ),
+        scratch=chunk_scratch,
     )(slot_map, starts, recv)
+    before_slab = prefetched(
+        functools.partial(earlier_attend_kernel, 1),
+        2,
+        jax.ShapeDtypeStruct(slab, low),
+        scratch=chunk_scratch,
+    )(slot_map, starts, shared_kv, *shared_work)
+    shared_slab = lax.ppermute(before_slab, "core", swap)
+    far_slab = prefetched(
+        functools.partial(earlier_attend_kernel, 2),
+        2,
+        jax.ShapeDtypeStruct(slab, jnp.float32),
+        scratch=chunk_scratch,
+    )(slot_map, starts, recv[:, KV_AT + 2 * BLK : AUX_AT], *shared_work)
     partial_grads = prefetched(
-        earlier_attend_kernel,
-        2,
-        jax.ShapeDtypeStruct((groups, SPAN, 2 * BLK, HD), low),
-        scratch=tuple(
-            pltpu.VMEM(((SPAN - 1) * tokens, HD), dtype)
-            for dtype in (low, low, jnp.float32, jnp.float32)
-        ),
-    )(slot_map, starts, *earlier, *own_work)
+        merge_kernel, 1, jax.ShapeDtypeStruct((groups, len(SENT), 2 * BLK, HD), low)
+    )(core.reshape(1), own_slab, far_slab, shared_slab)
     partial_grads, near = lax.optimization_barrier((partial_grads, near))
     own_up, own_down, other_up, other_down = near
-    own_list = [own_input, own_up, lax.ppermute(own_up, "tensor", up), own_down]
-    other_list = [other_input, other_up, lax.ppermute(other_down, "tensor", down), other_down]
+    own_list = [own_input, own_up, own_down, lax.ppermute(own_up, "tensor", up)]
+    other_list = [other_input, other_up, other_down, lax.ppermute(other_down, "tensor", down)]
     returned = lax.all_to_all(partial_grads, context, split_axis=0, concat_axis=0, tiled=True)
     targets = lax.dynamic_slice_in_dim(order_row, where * slots, slots, 0) // slots
     own_kv = prefetched(collect_kernel, 1, jax.ShapeDtypeStruct((tokens, 2 * HD), low))(
@@ -438,22 +459,22 @@
     other_kv = lax.ppermute(own_kv, "core", swap)
 
     input_scratch = (
-        pltpu.VMEM((len(own_list), half, tokens), low),
-        pltpu.SemaphoreType.DMA((len(own_list),)),
+        pltpu.VMEM((widths - 1, half, tokens), low),
+        pltpu.SemaphoreType.DMA((widths - 1,)),
     )
     first_product = prefetched(
         first_product_kernel,
         0,
         jax.ShapeDtypeStruct((len(own_list), half, 2 * HD), jnp.float32),
         scratch=input_scratch,
-        in_place=len(own_list),
+        in_place=widths - 1,
     )(*own_list, own_kv)
     spread = prefetched(
         product_kernel,
         1,
         jax.ShapeDtypeStruct((replicas, lines, 2, HB // replicas, 2 * HD), low),
         scratch=input_scratch,
-        in_place=len(other_list),
+        in_place=widths - 1,
     )(
         jnp.stack([core, lax.axis_index("tensor")]),
         *other_list,

time: 150 us -> 137 us (0.913)
  the two profiles are of different devices: /device:TPU:8 before, /device:TPU:6 now
where the time goes in v6:
time: 137 us
  starting transfers between devices  46 us (34%)
  blocking collectives  42.3 us (31%)
  waiting for transfers between devices  28.7 us (21%)
  Pallas kernels  15.8 us (12%)
  other arithmetic  2.27 us (2%)
  local copies, waits for them, and re-layouts  1.49 us (1%)
    all_to_all x1, blocking collectives, per_device(): lax.all_to_all(spread, ('dp', 'y'), split_axis=0, concat_axis=0, tiled=True)  42.3 us
    pallas_call x9, Pallas kernels, call(): pl.pallas_call(kernel, out_shape=out_shape, grid_spec=pltpu.PrefetchScala...  15.8 us
    ppermute x4, starting transfers between devices, per_device(): lax.ppermute(array, 'tensor', way)  14.1 us
    ppermute x4, waiting for transfers between devices, per_device(): lax.ppermute(array, 'tensor', way)  13 us
    all_to_all x1, waiting for transfers between devices, per_device(): lax.all_to_all(partial_grads, context, split_axis=0, concat_axis=0, tiled...  9.84 us
    all_to_all x1, starting transfers between devices, per_device(): lax.all_to_all(packed, context, split_axis=0, concat_axis=0, tiled=True)  7.35 us
    all_to_all x1, waiting for transfers between devices, per_device(): lax.all_to_all(packed, context, split_axis=0, concat_axis=0, tiled=True)  5.46 us
    all_to_all x1, starting transfers between devices, per_device(): lax.all_to_all(partial_grads, context, split_axis=0, concat_axis=0, tiled...  5.22 us
  transfers between devices with their start and end apart: 12, of which 7 were waited for; matrix products, arithmetic and copies ran while one was open for 2% of the time, Pallas kernels for 6%

profile of v6, /device:TPU:6, one launch (start us, length us, event | category | flops | bytes accessed | tf_op | source)
XLA Modules:
  0.0 136.8 jit_solution(17928575284168474827)
XLA Ops:
  0.0 2.8 %shard_map.109 = bf16[16,392,128]{2,1,0:T(8,128)(2,1)} custom-call(s32[1]{0:T(128)} %bitcast.2.where_ref, bf16[1,4,512,128]{3,2,1,0:T(8,128)(2,1)} %refs_0_.1, bf16[1,4,512,128]{3,2,1,0:T(8,128)(2,1)} %refs_1_.1, bf16[1,1,512,128]{3,2,1,0:T(8,128)(2,1)} %refs_2_.1, bf16[1,1,512,128]{3,2,1,0:T(8,128)(2,1)} %refs_3_.1, bf16[1,4,512]{2,1,0:T(4,128)(2,1)} %refs_4_.1, ...), custom_call_target="tpu_custom_call" | custom-call | tf_op jit(solution)/shard_map/pallas_call | solution.py:322
  2.8 7.3 %all-to-all-start = ((bf16[16,392,128]{2,1,0:T(8,128)(2,1)}), bf16[16,392,128]{2,1,0:T(8,128)(2,1)S(1)}, u32[]{:S(2)}, u32[]{:S(2)}) async-start(bf16[16,392,128]{2,1,0:T(8,128)(2,1)} %shard_map.109), calls=%async_computation | async-start | bytes 3211264 | tf_op jit(solution)/shard_map/all_to_all | solution.py:384
  10.2 1.1 shard_map.110
  11.3 2.3 %collective-permute-start = (bf16[512,512]{1,0:T(8,128)(2,1)}, bf16[512,512]{1,0:T(8,128)(2,1)S(1)}, u32[]{:S(2)}, u32[]{:S(2)}) collective-permute-start(bf16[512,512]{1,0:T(8,128)(2,1)} %get-tuple-element.26), channel_id=1, source_target_pairs={{0,4},{4,0},{1,5},{5,1},{2,6},{6,2},{3,7},{7,3},{8,12},{12,8},{9,1... | collective-permute-start | bytes 1572872 | tf_op jit(solution)/shard_map/ppermute | solution.py:392
  13.6 2.7 %collective-permute-start.2 = (bf16[512,512]{1,0:T(8,128)(2,1)S(1)}, bf16[512,512]{1,0:T(8,128)(2,1)S(1)}, u32[]{:S(2)}, u32[]{:S(2)}) collective-permute-start(bf16[512,512]{1,0:T(8,128)(2,1)S(1)} %get-tuple-element.28.refs_0_), channel_id=1, source_target_pairs={{0,3},{1,0},{2,1},{3,2},{4,7},{5,4},{6,5},{7,6},{8,11},{9,8},{10,9... | collective-permute-start | bytes 1572872 | tf_op jit(solution)/shard_map/ppermute | solution.py:396
  16.4 4.3 %collective-permute-start.1 = (bf16[512,512]{1,0:T(8,128)(2,1)S(1)}, bf16[512,512]{1,0:T(8,128)(2,1)}, u32[]{:S(2)}, u32[]{:S(2)}) collective-permute-start(bf16[512,512]{1,0:T(8,128)(2,1)S(1)} %get-tuple-element.28.refs_0_), channel_id=1, source_target_pairs={{0,1},{1,2},{2,3},{3,0},{4,5},{5,6},{6,7},{7,4},{8,9},{9,10},{10,1... | collective-permute-start | bytes 1572872 | tf_op jit(solution)/shard_map/ppermute | solution.py:396
  22.2 1.9 %collective-permute-start.4 = (bf16[512,512]{1,0:T(8,128)(2,1)S(1)}, bf16[512,512]{1,0:T(8,128)(2,1)S(1)}, u32[]{:S(2)}, u32[]{:S(2)}) collective-permute-start(bf16[512,512]{1,0:T(8,128)(2,1)S(1)} %collective-permute-done.refs_0_), channel_id=1, source_target_pairs={{0,3},{1,0},{2,1},{3,2},{4,7},{5,4},{6,5},{7,6},{8,11},{9,8},{10,9... | collective-permute-start | bytes 1572872 | tf_op jit(solution)/shard_map/ppermute | solution.py:396
  24.1 5.1 %collective-permute-start.3 = (bf16[512,512]{1,0:T(8,128)(2,1)S(1)}, bf16[512,512]{1,0:T(8,128)(2,1)}, u32[]{:S(2)}, u32[]{:S(2)}) collective-permute-start(bf16[512,512]{1,0:T(8,128)(2,1)S(1)} %collective-permute-done.refs_0_), channel_id=1, source_target_pairs={{0,1},{1,2},{2,3},{3,0},{4,5},{5,6},{6,7},{7,4},{8,9},{9,10},{10,1... | collective-permute-start | bytes 1572872 | tf_op jit(solution)/shard_map/ppermute | solution.py:396
  29.5 2.0 %collective-permute-done.2.refs_2_ = bf16[512,512]{1,0:T(8,128)(2,1)S(1)} collective-permute-done((bf16[512,512]{1,0:T(8,128)(2,1)S(1)}, bf16[512,512]{1,0:T(8,128)(2,1)S(1)}, u32[]{:S(2)}, u32[]{:S(2)}) %collective-permute-start.2) | collective-permute-done | bytes 524320 | tf_op jit(solution)/shard_map/ppermute | solution.py:396
  31.5 1.7 %collective-permute-done.1.refs_1_ = bf16[512,512]{1,0:T(8,128)(2,1)} collective-permute-done((bf16[512,512]{1,0:T(8,128)(2,1)S(1)}, bf16[512,512]{1,0:T(8,128)(2,1)}, u32[]{:S(2)}, u32[]{:S(2)}) %collective-permute-start.1) | collective-permute-done | bytes 524320 | tf_op jit(solution)/shard_map/ppermute | solution.py:396
  33.2 8.7 %collective-permute-done.4.refs_2_ = bf16[512,512]{1,0:T(8,128)(2,1)S(1)} collective-permute-done((bf16[512,512]{1,0:T(8,128)(2,1)S(1)}, bf16[512,512]{1,0:T(8,128)(2,1)S(1)}, u32[]{:S(2)}, u32[]{:S(2)}) %collective-permute-start.4) | collective-permute-done | bytes 524320 | tf_op jit(solution)/shard_map/ppermute | solution.py:396
  43.3 5.5 %all-to-all-done.recv_ref = bf16[16,392,128]{2,1,0:T(8,128)(2,1)S(1)} async-done(((bf16[16,392,128]{2,1,0:T(8,128)(2,1)}), bf16[16,392,128]{2,1,0:T(8,128)(2,1)S(1)}, u32[]{:S(2)}, u32[]{:S(2)}) %all-to-all-start) | async-done | bytes 1605664 | tf_op jit(solution)/shard_map/all_to_all | solution.py:384
  48.8 2.9 %collective-permute-start.5 = (bf16[16,64,128]{2,1,0:T(8,128)(2,1)S(1)}, bf16[16,64,128]{2,1,0:T(8,128)(2,1)S(1)}, u32[]{:S(2)}, u32[]{:S(2)}) collective-permute-start(bf16[16,64,128]{2,1,0:T(8,128)(2,1)S(1)} %get-tuple-element.45), channel_id=1, source_target_pairs={{0,4},{4,0},{1,5},{5,1},{2,6},{6,2},{3,7},{7,3},{8,12},{12,8},{9,1... | collective-permute-start | bytes 786440 | tf_op jit(solution)/shard_map/ppermute | solution.py:414
  51.9 3.1 %shard_map.111 = (bf16[2048,128]{1,0:T(8,128)(2,1)S(1)}, bf16[2048,128]{1,0:T(8,128)(2,1)S(1)}, bf16[128,2048]{1,0:T(8,128)(2,1)S(1)}, bf16[128,2048]{1,0:T(8,12...) custom-call(s32[3,16]{1,0:T(4,128)S(1)} %select_reduce_fusion.slot_ref, ...), custom_call_target="tpu_custom_call" | custom-call | tf_op jit(solution)/shard_map/pallas_call | solution.py:322
  55.8 4.5 %collective-permute-start.6 = (bf16[16,64,128]{2,1,0:T(8,128)(2,1)S(1)}, bf16[16,64,128]{2,1,0:T(8,128)(2,1)S(1)}, u32[]{:S(2)}, u32[]{:S(2)}) collective-permute-start(bf16[16,64,128]{2,1,0:T(8,128)(2,1)S(1)} %shard_map.113), channel_id=1, source_target_pairs={{0,4},{4,0},{1,5},{5,1},{2,6},{6,2},{3,7},{7,3},{8,12},{12,8},{9,1... | collective-permute-start | bytes 786440 | tf_op jit(solution)/shard_map/ppermute | solution.py:440
  61.4 0.9 shard_map.114
  62.3 5.2 %all-to-all-start.1 = ((bf16[16,2,64,128]{3,2,1,0:T(8,128)(2,1)}), bf16[16,2,64,128]{3,2,1,0:T(8,128)(2,1)S(1)}, u32[]{:S(2)}, u32[]{:S(2)}) async-start(bf16[16,2,64,128]{3,2,1,0:T(8,128)(2,1)} %shard_map.114), calls=%async_computation.1 | async-start | bytes 1048576 | tf_op jit(solution)/shard_map/all_to_all | solution.py:454
  67.5 4.2 %collective-permute-start.8 = (bf16[512,512]{1,0:T(8,128)(2,1)}, bf16[512,512]{1,0:T(8,128)(2,1)S(1)}, u32[]{:S(2)}, u32[]{:S(2)}) collective-permute-start(bf16[512,512]{1,0:T(8,128)(2,1)} %collective-permute-done.1.refs_1_), channel_id=1, source_target_pairs={{0,1},{1,2},{2,3},{3,0},{4,5},{5,6},{6,7},{7,4},{8,9},{9,10},{10,1... | collective-permute-start | bytes 1572872 | tf_op jit(solution)/shard_map/ppermute | solution.py:452
  71.7 1.9 %collective-permute-start.7 = (bf16[512,512]{1,0:T(8,128)(2,1)}, bf16[512,512]{1,0:T(8,128)(2,1)S(1)}, u32[]{:S(2)}, u32[]{:S(2)}) collective-permute-start(bf16[512,512]{1,0:T(8,128)(2,1)} %copy-done.4), channel_id=1, source_target_pairs={{0,3},{1,0},{2,1},{3,2},{4,7},{5,4},{6,5},{7,6},{8,11},{9,8},{10,9... | collective-permute-start | bytes 1572872 | tf_op jit(solution)/shard_map/ppermute | solution.py:453
  73.7 9.8 %all-to-all-done.1.recv_ref = bf16[16,2,64,128]{3,2,1,0:T(8,128)(2,1)S(1)} async-done(((bf16[16,2,64,128]{3,2,1,0:T(8,128)(2,1)}), bf16[16,2,64,128]{3,2,1,0:T(8,128)(2,1)S(1)}, u32[]{:S(2)}, u32[]{:S(2)}) %all-to-all-start.1) | async-done | bytes 524320 | tf_op jit(solution)/shard_map/all_to_all | solution.py:454
  84.2 3.6 %collective-permute-start.9 = (bf16[512,256]{1,0:T(8,128)(2,1)S(1)}, bf16[512,256]{1,0:T(8,128)(2,1)S(1)}, u32[]{:S(2)}, u32[]{:S(2)}) collective-permute-start(bf16[512,256]{1,0:T(8,128)(2,1)S(1)} %shard_map.115.refs_4_), channel_id=1, source_target_pairs={{0,4},{4,0},{1,5},{5,1},{2,6},{6,2},{3,7},{7,3},{8,12},{12,8},{9,1... | collective-permute-start | bytes 786440 | tf_op jit(solution)/shard_map/ppermute | solution.py:459
  88.0 2.3 %shard_map.116.refs_4_ = f32[4,512,256]{2,1,0:T(8,128)S(1)} custom-call(bf16[512,512]{1,0:T(8,128)(2,1)} %copy-done.1, bf16[512,512]{1,0:T(8,128)(2,1)} %collective-permute-done.1.refs_1_, bf16[512,512]{1,0:T(8,128)(2,1)} %copy-done.3, bf16[512,512]{1,0:T(8,128)(2,1)S(1)} %collective-permute-done.8.refs_3_, bf16[512,256]{1,0:T(8,128)(2,1)S(1)} %shard_map.115.refs_4_), custom_call_target="tpu_custom_call" | custom-call | tf_op jit(solution)/shard_map/pallas_call | solution.py:322
  90.3 3.4 %shard_map.117 = bf16[8,8,2,16,256]{4,3,2,1,0:T(8,128)(2,1)S(1)} custom-call(s32[2]{0:T(128)S(1)} %pad_add_fusion.where_ref, bf16[512,512]{1,0:T(8,128)(2,1)} %copy-done.2, bf16[512,512]{1,0:T(8,128)(2,1)} %collective-permute-done.3.refs_1_, bf16[512,512]{1,0:T(8,128)(2,1)} %copy-done.4, bf16[512,512]{1,0:T(8,128)(2,1)S(1)} %collective-permute-done.7.refs_3_, ...), custom_call_target="tpu_custom_call" | custom-call | tf_op jit(solution)/shard_map/pallas_call | solution.py:322
  93.8 42.3 %all_to_all.15 = bf16[64,2,16,256]{3,2,1,0:T(8,128)(2,1)S(1)} all-to-all(bf16[64,2,16,256]{3,2,1,0:T(8,128)(2,1)S(1)} %bitcast.15), channel_id=1, replica_groups=mesh['dp'=8,'y'=8,'core'=2,'tensor'=4] {'dp','y'}, dimensions={0} | all-to-all | bytes 2097152 | tf_op jit(solution)/shard_map/all_to_all | solution.py:487
  (40 shorter events, 6.8 us)
Async XLA Ops:
  2.8 7.4 %copy-start = (bf16[1,512,1024]{2,1,0:T(8,128)(2,1)S(1)}, bf16[1,512,1024]{2,1,0:T(8,128)(2,1)}, u32[]{:S(2)}) copy-start(bf16[1,512,1024]{2,1,0:T(8,128)(2,1)} %param.11) | copy-start | bytes 3145732
  2.8 17.9 %copy-start.6 = (s32[1,10]{1,0:T(1,128)S(1)}, s32[1,10]{1,0:T(1,128)}, u32[]{:S(2)}) copy-start(s32[1,10]{1,0:T(1,128)} %param.18) | copy-start | bytes 124
  2.8 18.6 %copy-start.5 = (s32[1,256]{1,0:T(1,128)S(1)}, s32[1,256]{1,0:T(1,128)}, u32[]{:S(2)}) copy-start(s32[1,256]{1,0:T(1,128)} %refs_7_.1) | copy-start | bytes 3076
  2.8 45.9 %all-to-all-start = ((bf16[16,392,128]{2,1,0:T(8,128)(2,1)}), bf16[16,392,128]{2,1,0:T(8,128)(2,1)S(1)}, u32[]{:S(2)}, u32[]{:S(2)}) async-start(bf16[16,392,128]{2,1,0:T(8,128)(2,1)} %shard_map.109), calls=%async_computation | async-start | bytes 3211264 | tf_op jit(solution)/shard_map/all_to_all | solution.py:384
  11.3 44.4 %copy-start.1 = (bf16[512,512]{1,0:T(8,128)(2,1)}, bf16[512,512]{1,0:T(8,128)(2,1)S(1)}, u32[]{:S(2)}) copy-start(bf16[512,512]{1,0:T(8,128)(2,1)S(1)} %get-tuple-element.28.refs_0_) | copy-start | bytes 1572868
  11.3 10.9 %collective-permute-start = (bf16[512,512]{1,0:T(8,128)(2,1)}, bf16[512,512]{1,0:T(8,128)(2,1)S(1)}, u32[]{:S(2)}, u32[]{:S(2)}) collective-permute-start(bf16[512,512]{1,0:T(8,128)(2,1)} %get-tuple-element.26), channel_id=1, source_target_pairs={{0,4},{4,0},{1,5},{5,1},{2,6},{6,2},{3,7},{7,3},{8,12},{12,8},{9,1... | collective-permute-start | bytes 1572872 | tf_op jit(solution)/shard_map/ppermute | solution.py:392
  13.6 17.9 %collective-permute-start.2 = (bf16[512,512]{1,0:T(8,128)(2,1)S(1)}, bf16[512,512]{1,0:T(8,128)(2,1)S(1)}, u32[]{:S(2)}, u32[]{:S(2)}) collective-permute-start(bf16[512,512]{1,0:T(8,128)(2,1)S(1)} %get-tuple-element.28.refs_0_), channel_id=1, source_target_pairs={{0,3},{1,0},{2,1},{3,2},{4,7},{5,4},{6,5},{7,6},{8,11},{9,8},{10,9... | collective-permute-start | bytes 1572872 | tf_op jit(solution)/shard_map/ppermute | solution.py:396
  16.4 16.8 %collective-permute-start.1 = (bf16[512,512]{1,0:T(8,128)(2,1)S(1)}, bf16[512,512]{1,0:T(8,128)(2,1)}, u32[]{:S(2)}, u32[]{:S(2)}) collective-permute-start(bf16[512,512]{1,0:T(8,128)(2,1)S(1)} %get-tuple-element.28.refs_0_), channel_id=1, source_target_pairs={{0,1},{1,2},{2,3},{3,0},{4,5},{5,6},{6,7},{7,4},{8,9},{9,10},{10,1... | collective-permute-start | bytes 1572872 | tf_op jit(solution)/shard_map/ppermute | solution.py:396
  22.2 21.1 %copy-start.2 = (bf16[512,512]{1,0:T(8,128)(2,1)}, bf16[512,512]{1,0:T(8,128)(2,1)S(1)}, u32[]{:S(2)}) copy-start(bf16[512,512]{1,0:T(8,128)(2,1)S(1)} %collective-permute-done.refs_0_) | copy-start | bytes 1572868
  22.2 19.7 %collective-permute-start.4 = (bf16[512,512]{1,0:T(8,128)(2,1)S(1)}, bf16[512,512]{1,0:T(8,128)(2,1)S(1)}, u32[]{:S(2)}, u32[]{:S(2)}) collective-permute-start(bf16[512,512]{1,0:T(8,128)(2,1)S(1)} %collective-permute-done.refs_0_), channel_id=1, source_target_pairs={{0,3},{1,0},{2,1},{3,2},{4,7},{5,4},{6,5},{7,6},{8,11},{9,8},{10,9... | collective-permute-start | bytes 1572872 | tf_op jit(solution)/shard_map/ppermute | solution.py:396
  24.1 19.2 %collective-permute-start.3 = (bf16[512,512]{1,0:T(8,128)(2,1)S(1)}, bf16[512,512]{1,0:T(8,128)(2,1)}, u32[]{:S(2)}, u32[]{:S(2)}) collective-permute-start(bf16[512,512]{1,0:T(8,128)(2,1)S(1)} %collective-permute-done.refs_0_), channel_id=1, source_target_pairs={{0,1},{1,2},{2,3},{3,0},{4,5},{5,6},{6,7},{7,4},{8,9},{9,10},{10,1... | collective-permute-start | bytes 1572872 | tf_op jit(solution)/shard_map/ppermute | solution.py:396
  31.5 20.1 %copy-start.3 = (bf16[512,512]{1,0:T(8,128)(2,1)}, bf16[512,512]{1,0:T(8,128)(2,1)S(1)}, u32[]{:S(2)}) copy-start(bf16[512,512]{1,0:T(8,128)(2,1)S(1)} %collective-permute-done.2.refs_2_) | copy-start | bytes 1572868
  41.9 0.8 copy-start.4
  48.8 6.2 %collective-permute-start.5 = (bf16[16,64,128]{2,1,0:T(8,128)(2,1)S(1)}, bf16[16,64,128]{2,1,0:T(8,128)(2,1)S(1)}, u32[]{:S(2)}, u32[]{:S(2)}) collective-permute-start(bf16[16,64,128]{2,1,0:T(8,128)(2,1)S(1)} %get-tuple-element.45), channel_id=1, source_target_pairs={{0,4},{4,0},{1,5},{5,1},{2,6},{6,2},{3,7},{7,3},{8,12},{12,8},{9,1... | collective-permute-start | bytes 786440 | tf_op jit(solution)/shard_map/ppermute | solution.py:414
  55.8 5.6 %collective-permute-start.6 = (bf16[16,64,128]{2,1,0:T(8,128)(2,1)S(1)}, bf16[16,64,128]{2,1,0:T(8,128)(2,1)S(1)}, u32[]{:S(2)}, u32[]{:S(2)}) collective-permute-start(bf16[16,64,128]{2,1,0:T(8,128)(2,1)S(1)} %shard_map.113), channel_id=1, source_target_pairs={{0,4},{4,0},{1,5},{5,1},{2,6},{6,2},{3,7},{7,3},{8,12},{12,8},{9,1... | collective-permute-start | bytes 786440 | tf_op jit(solution)/shard_map/ppermute | solution.py:440
  62.3 21.3 %all-to-all-start.1 = ((bf16[16,2,64,128]{3,2,1,0:T(8,128)(2,1)}), bf16[16,2,64,128]{3,2,1,0:T(8,128)(2,1)S(1)}, u32[]{:S(2)}, u32[]{:S(2)}) async-start(bf16[16,2,64,128]{3,2,1,0:T(8,128)(2,1)} %shard_map.114), calls=%async_computation.1 | async-start | bytes 1048576 | tf_op jit(solution)/shard_map/all_to_all | solution.py:454
  67.5 20.5 %collective-permute-start.8 = (bf16[512,512]{1,0:T(8,128)(2,1)}, bf16[512,512]{1,0:T(8,128)(2,1)S(1)}, u32[]{:S(2)}, u32[]{:S(2)}) collective-permute-start(bf16[512,512]{1,0:T(8,128)(2,1)} %collective-permute-done.1.refs_1_), channel_id=1, source_target_pairs={{0,1},{1,2},{2,3},{3,0},{4,5},{5,6},{6,7},{7,4},{8,9},{9,10},{10,1... | collective-permute-start | bytes 1572872 | tf_op jit(solution)/shard_map/ppermute | solution.py:452
  71.7 18.6 %collective-permute-start.7 = (bf16[512,512]{1,0:T(8,128)(2,1)}, bf16[512,512]{1,0:T(8,128)(2,1)S(1)}, u32[]{:S(2)}, u32[]{:S(2)}) collective-permute-start(bf16[512,512]{1,0:T(8,128)(2,1)} %copy-done.4), channel_id=1, source_target_pairs={{0,3},{1,0},{2,1},{3,2},{4,7},{5,4},{6,5},{7,6},{8,11},{9,8},{10,9... | collective-permute-start | bytes 1572872 | tf_op jit(solution)/shard_map/ppermute | solution.py:453
  84.2 6.2 %collective-permute-start.9 = (bf16[512,256]{1,0:T(8,128)(2,1)S(1)}, bf16[512,256]{1,0:T(8,128)(2,1)S(1)}, u32[]{:S(2)}, u32[]{:S(2)}) collective-permute-start(bf16[512,256]{1,0:T(8,128)(2,1)S(1)} %shard_map.115.refs_4_), channel_id=1, source_target_pairs={{0,4},{4,0},{1,5},{5,1},{2,6},{6,2},{3,7},{7,3},{8,12},{12,8},{9,1... | collective-permute-start | bytes 786440 | tf_op jit(solution)/shard_map/ppermute | solution.py:459

commit v7 on v6

--- a/solution.py
+++ b/solution.py
@@ -227,9 +227,14 @@
         out_ref[src, 1] = far.astype(out_ref.dtype)
 
 
-def collect_kernel(target_ref, recv_ref, out_ref):
+def collect_kernel(target_ref, recv_ref, aux_ref, out_ref):
     groups = recv_ref.shape[0]
-    for slot in range(out_ref.shape[0] // BLK):
+    tokens = out_ref.shape[0] - groups
+    for blk in range(2):
+        factors = [aux_ref[i].astype(jnp.float32)[4 + blk : 5 + blk, :] for i in range(groups)]
+        factors = jnp.concatenate(factors, axis=0).astype(out_ref.dtype)
+        out_ref[tokens:, blk * HD : (blk + 1) * HD] = factors
+    for slot in range(tokens // BLK):
         owner = target_ref[slot]
         total = recv_ref[owner, 0].astype(jnp.float32)
         later = owner + SENT[1]
@@ -241,15 +246,20 @@
         out_ref[rows, HD : 2 * HD] = total[BLK : 2 * BLK]
 
 
-def turn_kernel(core_ref, input_ref, own_ref, other_ref):
-    span = 2 * HB
-    core = core_ref[0]
-    for part in range(own_ref.shape[0] // span):
-        rows = slice(part * span, (part + 1) * span)
-        at = pl.multiple_of((CORES * part + core) * span, span)
-        own_ref[rows, :] = input_ref[:, pl.ds(at, span)].T
-        at = pl.multiple_of((CORES * part + 1 - core) * span, span)
-        other_ref[rows, :] = input_ref[:, pl.ds(at, span)].T
+def turn_kernel(where_ref, input_ref, keep_ref, core_ref, line_ref):
+    core, half = where_ref[0], where_ref[1]
+    rows = keep_ref.shape[0] // 2
+    places = (
+        (keep_ref, 0, core, half),
+        (core_ref, 0, 1 - core, half),
+        (line_ref, 0, core, 1 - half),
+        (line_ref, 2 * rows, 1 - core, 1 - half),
+    )
+    for ref, start, parity, blk in places:
+        for part in range(2):
+            at = pl.multiple_of((CORES * part + parity) * 2 * HB + blk * HB, HB)
+            begin = start + part * rows
+            ref[begin : begin + rows, :] = input_ref[:, pl.ds(at, HB)].T
 
 
 def load_all(sources, places, sems):
@@ -261,51 +271,65 @@
     return loads
 
 
-def first_product_kernel(*refs):
-    far_ref, kv_ref, out_ref, input_scr, sems = refs[-5:]
-    loads = load_all(refs[:-5], input_scr, sems)
-    last = len(loads)
-    out_ref[last] = jnp.dot(far_ref[...], kv_ref[...], preferred_element_type=jnp.float32)
-    for step, load in enumerate(loads):
-        load.wait()
-        out_ref[step] = jnp.dot(input_scr[step], kv_ref[...], preferred_element_type=jnp.float32)
-
-
-def product_kernel(where_ref, *refs):
-    far_ref, first_ref, kv_ref, had_ref, aux_ref, out_ref, input_scr, sems = refs[-8:]
-    loads = load_all(refs[:-8], input_scr, sems)
-    core, width = where_ref[0], where_ref[1]
-    replicas = out_ref.shape[0]
-    span = 2 * HB
-    parts = far_ref.shape[0] // span
-    had = jnp.concatenate([had_ref[...].astype(jnp.float32)] * 2, axis=1)
-    widths = len(HOPS)
-    for step in (widths - 1, *range(widths - 1)):
-        source = (width + widths - HOPS[step]) % widths
+def paired_products(refs, far_ref, kv_refs, input_scr, sems):
+    loads = load_all(refs, input_scr, sems)
+    for step in (len(loads), *range(len(loads))):
         if step < len(loads):
             loads[step].wait()
             inputs = input_scr[step]
         else:
             inputs = far_ref[...]
-        grad = jnp.dot(inputs, kv_ref[...], preferred_element_type=jnp.float32)
-        grad = grad + first_ref[step]
-        for part in range(parts):
-            line = source * parts + part
+        half, tokens = inputs.shape[0] // 2, inputs.shape[1]
+        grad = jnp.dot(inputs[:half], kv_refs[0][:tokens], preferred_element_type=jnp.float32)
+        grad += jnp.dot(inputs[half:], kv_refs[1][:tokens], preferred_element_type=jnp.float32)
+        yield step, grad
+
+
+def first_product_kernel(*refs):
+    far_ref, own_ref, other_ref, out_ref, input_scr, sems = refs[-6:]
+    kv_refs = (own_ref, other_ref)
+    for step, grad in paired_products(refs[:-6], far_ref, kv_refs, input_scr, sems):
+        out_ref[step] = grad
+
+
+def product_kernel(where_ref, *refs):
+    far_ref, own_ref, other_ref, first_ref, had_ref, aux_ref = refs[-9:-3]
+    out_ref, input_scr, sems = refs[-3:]
+    core, half, width = where_ref[0], where_ref[1], where_ref[2]
+    replicas = out_ref.shape[0]
+    had = jnp.concatenate([had_ref[...].astype(jnp.float32)] * 2, axis=1)
+    widths = len(HOPS)
+    kv_refs = (own_ref, other_ref)
+    tokens = input_scr.shape[2]
+    paired_factors = own_ref[tokens:, :].astype(jnp.float32)
+    paired_factors = jnp.where(half == 0, paired_factors[:, :HD], paired_factors[:, HD:])
+    context_of = lax.broadcasted_iota(jnp.int32, paired_factors.shape, 0)
+
+    def chosen(aux, at):
+        return jnp.where(half == 0, aux[at : at + 1, :], aux[at + 1 : at + 2, :])
+
+    for step, grad in paired_products(refs[:-9], far_ref, kv_refs, input_scr, sems):
+        source = (width + widths - HOPS[step]) % widths
+        for part in range(2):
+            line = source * 2 + part
             aux = aux_ref[CORES * line + core].astype(jnp.float32)
-            for blk in range(2):
-                at = part * span + blk * HB
-                rows = grad[at : at + HB]
-                sign = aux[2 + blk : 3 + blk, :]
-                table = (had * jnp.concatenate([sign, sign], axis=1)).astype(jnp.bfloat16)
-                high = rows.astype(jnp.bfloat16)
-                low = (rows - high.astype(jnp.float32)).astype(jnp.bfloat16)
-                both = jnp.concatenate([high, low], axis=0)
-                rotated = jnp.dot(table, both, preferred_element_type=jnp.float32)
-                factor = aux[4 + blk : 5 + blk, :] * (HB ** (-0.5))
-                rotated *= jnp.concatenate([factor] * (rows.shape[1] // HB), axis=1)
-                out_ref[:, line, blk] = rotated.astype(out_ref.dtype).reshape(
-                    replicas, HB // replicas, rows.shape[1]
-                )
+            mine = context_of == CORES * line + core
+            paired = jnp.sum(jnp.where(mine, paired_factors, 0.0), axis=0, keepdims=True)
+            at = slice(part * HB, (part + 1) * HB)
+            factor, paired = [
+                jnp.concatenate([row * HB ** (-0.5)] * 2, axis=1)
+                for row in (chosen(aux, 4), paired)
+            ]
+            rows = first_ref[step, at] * factor + grad[at] * paired
+            sign = chosen(aux, 2)
+            table = (had * jnp.concatenate([sign, sign], axis=1)).astype(jnp.bfloat16)
+            high = rows.astype(jnp.bfloat16)
+            low = (rows - high.astype(jnp.float32)).astype(jnp.bfloat16)
+            both = jnp.concatenate([high, low], axis=0)
+            rotated = jnp.dot(table, both, preferred_element_type=jnp.float32)
+            out_ref[:, line] = rotated.astype(out_ref.dtype).reshape(
+                replicas, HB // replicas, rows.shape[1]
+            )
 
 
 def prefetched(kernel, scalars, out_shape, scratch=(), in_place=0, out_space=pltpu.VMEM):
@@ -357,10 +381,11 @@
     slots = tokens // BLK
     groups = lax.axis_size(context)
     lines = lax.axis_size("y")
-    replicas = lax.axis_size("dp")
+    sequences = ("zh", "zl")
+    replicas = lax.axis_size(sequences)
     order_row = stretch_order[0]
     where = lax.axis_index(context)
-    core = lax.axis_index("core")
+    core, half = lax.axis_index("core"), lax.axis_index("zl")
 
     raw = (queries, out_grad, key_states, value_states, log_sums, grad_dots, sign_vector)
     packed = prefetched(
@@ -383,13 +408,17 @@
     packed, layer_input = lax.optimization_barrier((packed, layer_input))
     recv = lax.all_to_all(packed, context, split_axis=0, concat_axis=0, tiled=True)
 
-    half = layer_input.shape[2] // CORES
-    turned = jax.ShapeDtypeStruct((half, tokens), low)
-    own_input, other_input = prefetched(turn_kernel, 1, (turned, turned))(
-        core.reshape(1), layer_input[0]
-    )
     swap = [(0, 1), (1, 0)]
-    other_input = lax.ppermute(other_input, "core", swap)
+    piece = layer_input.shape[2] // (2 * CORES)
+    keep, to_core, to_line = prefetched(
+        turn_kernel,
+        1,
+        tuple(jax.ShapeDtypeStruct((rows, tokens), low) for rows in (piece, piece, 2 * piece)),
+    )(jnp.stack([core, half]), layer_input[0])
+    from_line = lax.ppermute(to_line, "zl", swap)
+    own_input = jnp.concatenate([keep, lax.ppermute(to_core, "core", swap)], axis=0)
+    diagonal = lax.ppermute(from_line[piece:], "core", swap)
+    other_input = jnp.concatenate([from_line[:piece], diagonal], axis=0)
     widths = lax.axis_size("tensor")
     up, down = around(widths, 1), around(widths, -1)
     near = [
@@ -449,68 +478,77 @@
     )(core.reshape(1), own_slab, far_slab, shared_slab)
     partial_grads, near = lax.optimization_barrier((partial_grads, near))
     own_up, own_down, other_up, other_down = near
-    own_list = [own_input, own_up, own_down, lax.ppermute(own_up, "tensor", up)]
-    other_list = [other_input, other_up, other_down, lax.ppermute(other_down, "tensor", down)]
+    own_far = lax.ppermute(own_up, "tensor", up)
+    other_far = lax.ppermute(other_down, "tensor", down)
     returned = lax.all_to_all(partial_grads, context, split_axis=0, concat_axis=0, tiled=True)
+    returned, own_far, other_far = lax.optimization_barrier((returned, own_far, other_far))
+    own_list = [own_input, own_up, own_down, own_far]
+    other_list = [other_input, other_up, other_down, other_far]
     targets = lax.dynamic_slice_in_dim(order_row, where * slots, slots, 0) // slots
-    own_kv = prefetched(collect_kernel, 1, jax.ShapeDtypeStruct((tokens, 2 * HD), low))(
-        targets, returned
-    )
-    other_kv = lax.ppermute(own_kv, "core", swap)
+    aux = recv[:, AUX_AT:ROWS]
+    own_kv = prefetched(collect_kernel, 1, jax.ShapeDtypeStruct((tokens + groups, 2 * HD), low))(
+        targets, returned, aux
+    )
+    line_kv = lax.ppermute(own_kv, "zl", swap)
+    core_kv = lax.ppermute(own_kv, "core", swap)
 
     input_scratch = (
-        pltpu.VMEM((widths - 1, half, tokens), low),
+        pltpu.VMEM((widths - 1, 2 * piece, tokens), low),
         pltpu.SemaphoreType.DMA((widths - 1,)),
     )
     first_product = prefetched(
         first_product_kernel,
         0,
-        jax.ShapeDtypeStruct((len(own_list), half, 2 * HD), jnp.float32),
+        jax.ShapeDtypeStruct((widths, piece, 2 * HD), jnp.float32),
         scratch=input_scratch,
         in_place=widths - 1,
-    )(*own_list, own_kv)
+    )(*own_list, own_kv, core_kv)
+    diagonal_kv = lax.ppermute(line_kv, "core", swap)
     spread = prefetched(
         product_kernel,
         1,
-        jax.ShapeDtypeStruct((replicas, lines, 2, HB // replicas, 2 * HD), low),
+        jax.ShapeDtypeStruct((replicas, lines, HB // replicas, 2 * HD), low),
         scratch=input_scratch,
         in_place=widths - 1,
     )(
-        jnp.stack([core, lax.axis_index("tensor")]),
+        jnp.stack([core, half, lax.axis_index("tensor")]),
         *other_list,
+        line_kv,
+        diagonal_kv,
         first_product,
-        other_kv,
         hadamard_signs(HB),
-        recv[:, AUX_AT:ROWS],
-    )
-    spread = spread.reshape(replicas * lines, 2, HB // replicas, 2 * HD)
-    shares = lax.all_to_all(spread, ("dp", "y"), split_axis=0, concat_axis=0, tiled=True)
-    return jnp.sum(shares.astype(jnp.float32), axis=0)
+        aux,
+    )
+    spread = spread.reshape(replicas * lines, HB // replicas, 2 * HD)
+    shares = lax.all_to_all(spread, (*sequences, "y"), split_axis=0, concat_axis=0, tiled=True)
+    shares = shares.reshape(replicas // 2, 2, lines, HB // replicas, 2 * HD)
+    return jnp.sum(shares.astype(jnp.float32), axis=(0, 2))
 
 
 def solution(mesh):
     replicas, groups, widths = mesh.devices.shape
     split = Mesh(
-        mesh.devices.reshape(replicas, groups // CORES, CORES, widths),
-        ("dp", "y", "core", "tensor"),
+        mesh.devices.reshape(replicas // 2, 2, groups // CORES, CORES, widths),
+        ("zh", "zl", "y", "core", "tensor"),
     )
     context = ("y", "core")
+    sequences = ("zh", "zl")
     return jax.shard_map(
         per_device,
         mesh=split,
         in_specs=(
-            P("dp", context, "tensor"),
-            P("dp", "tensor", context, None),
-            P("dp", "tensor", context, None),
-            P("dp", "tensor", context, None),
-            P("dp", "tensor", context, None),
-            P("dp", "tensor", context),
-            P("dp", "tensor", context),
-            P("dp", None),
-            P("dp", None),
+            P(sequences, context, "tensor"),
+            P(sequences, "tensor", context, None),
+            P(sequences, "tensor", context, None),
+            P(sequences, "tensor", context, None),
+            P(sequences, "tensor", context, None),
+            P(sequences, "tensor", context),
+            P(sequences, "tensor", context),
+            P(sequences, None),
+            P(sequences, None),
             P(context, None),
-            P("dp", context),
+            P(sequences, context),
         ),
-        out_specs=P(context, "dp", "tensor"),
+        out_specs=P(context, sequences, "tensor"),
         check_vma=False,
     )

time: 137 us -> 160 us (1.17)
  the two profiles are of different devices: /device:TPU:6 before, /device:TPU:8 now
where the time goes in v7:
time: 160 us; the launch traced here: 159 us
  starting transfers between devices  53.3 us (33%)
  waiting for transfers between devices  49.1 us (31%)
  blocking collectives  36.1 us (23%)
  Pallas kernels  17.2 us (11%)
  other arithmetic  2.34 us (1%)
    all_to_all x1, blocking collectives, per_device(): lax.all_to_all(spread, (*sequences, 'y'), split_axis=0, concat_axis=0, ti...  36.1 us
    ppermute x4, waiting for transfers between devices, per_device(): lax.ppermute(array, 'tensor', way)  19.2 us
    pallas_call x9, Pallas kernels, call(): pl.pallas_call(kernel, out_shape=out_shape, grid_spec=pltpu.PrefetchScala...  17.2 us
    ppermute x4, starting transfers between devices, per_device(): lax.ppermute(array, 'tensor', way)  12.5 us
    ppermute x1, waiting for transfers between devices, per_device(): from_line = lax.ppermute(to_line, 'zl', swap)  11.4 us
    ppermute x1, waiting for transfers between devices, per_device(): other_far = lax.ppermute(other_down, 'tensor', down)  10.1 us
    all_to_all x1, starting transfers between devices, per_device(): lax.all_to_all(packed, context, split_axis=0, concat_axis=0, tiled=True)  9.47 us
    all_to_all x1, starting transfers between devices, per_device(): lax.all_to_all(partial_grads, context, split_axis=0, concat_axis=0, tiled...  7.25 us
  transfers between devices with their start and end apart: 16, of which 9 were waited for; matrix products, arithmetic and copies ran while one was open for 2% of the time, Pallas kernels for 4%

profile of v7, /device:TPU:8, one launch (start us, length us, event | category | flops | bytes accessed | tf_op | source)
XLA Modules:
  0.0 159.2 jit_solution(9107627433412477963)
XLA Ops:
  0.0 2.8 %shard_map.109 = bf16[16,392,128]{2,1,0:T(8,128)(2,1)} custom-call(s32[1]{0:T(128)} %bitcast.3.where_ref, bf16[1,4,512,128]{3,2,1,0:T(8,128)(2,1)} %refs_0_.1, bf16[1,4,512,128]{3,2,1,0:T(8,128)(2,1)} %refs_1_.1, bf16[1,1,512,128]{3,2,1,0:T(8,128)(2,1)} %refs_2_.1, bf16[1,1,512,128]{3,2,1,0:T(8,128)(2,1)} %refs_3_.1, bf16[1,4,512]{2,1,0:T(4,128)(2,1)} %refs_4_.1, ...), custom_call_target="tpu_custom_call" | custom-call | tf_op jit(solution)/shard_map/pallas_call | solution.py:346
  2.8 9.5 %all-to-all-start = ((bf16[16,392,128]{2,1,0:T(8,128)(2,1)}), bf16[16,392,128]{2,1,0:T(8,128)(2,1)S(1)}, u32[]{:S(2)}, u32[]{:S(2)}) async-start(bf16[16,392,128]{2,1,0:T(8,128)(2,1)} %shard_map.109), calls=%async_computation | async-start | bytes 3211264 | tf_op jit(solution)/shard_map/all_to_all | solution.py:409
  13.3 2.5 %collective-permute-start = (bf16[512,512]{1,0:T(8,128)(2,1)S(1)}, bf16[512,512]{1,0:T(8,128)(2,1)S(1)}, u32[]{:S(2)}, u32[]{:S(2)}) collective-permute-start(bf16[512,512]{1,0:T(8,128)(2,1)S(1)} %get-tuple-element.30), channel_id=1, source_target_pairs={{0,64},{64,0},{1,65},{65,1},{2,66},{66,2},{3,67},{67,3},{4,68},{68... | collective-permute-start | bytes 1572872 | tf_op jit(solution)/shard_map/ppermute | solution.py:418
  17.7 11.4 %collective-permute-done = bf16[512,512]{1,0:T(8,128)(2,1)S(1)} collective-permute-done((bf16[512,512]{1,0:T(8,128)(2,1)S(1)}, bf16[512,512]{1,0:T(8,128)(2,1)S(1)}, u32[]{:S(2)}, u32[]{:S(2)}) %collective-permute-start) | collective-permute-done | bytes 524320 | tf_op jit(solution)/shard_map/ppermute | solution.py:418
  32.7 3.5 %collective-permute-start.4 = (bf16[512,512]{1,0:T(8,128)(2,1)S(1)}, bf16[512,512]{1,0:T(8,128)(2,1)S(1)}, u32[]{:S(2)}, u32[]{:S(2)}) collective-permute-start(bf16[512,512]{1,0:T(8,128)(2,1)S(1)} %constant_dynamic-update-slice_fusion.refs_0_), channel_id=1, source_target_pairs={{0,3},{1,0},{2,1},{3,2},{4,7},{5,4},{6,5},{7,6},{8,11},{9,8},{10,9... | collective-permute-start | bytes 1572872 | tf_op jit(solution)/shard_map/ppermute | solution.py:425
  36.3 2.3 %collective-permute-start.3 = (bf16[512,512]{1,0:T(8,128)(2,1)S(1)}, bf16[512,512]{1,0:T(8,128)(2,1)S(1)}, u32[]{:S(2)}, u32[]{:S(2)}) collective-permute-start(bf16[512,512]{1,0:T(8,128)(2,1)S(1)} %constant_dynamic-update-slice_fusion.refs_0_), channel_id=1, source_target_pairs={{0,1},{1,2},{2,3},{3,0},{4,5},{5,6},{6,7},{7,4},{8,9},{9,10},{10,1... | collective-permute-start | bytes 1572872 | tf_op jit(solution)/shard_map/ppermute | solution.py:425
  38.7 4.8 %collective-permute-start.6 = (bf16[512,512]{1,0:T(8,128)(2,1)S(1)}, bf16[512,512]{1,0:T(8,128)(2,1)}, u32[]{:S(2)}, u32[]{:S(2)}) collective-permute-start(bf16[512,512]{1,0:T(8,128)(2,1)S(1)} %pad_maximum_fusion.refs_0_), channel_id=1, source_target_pairs={{0,3},{1,0},{2,1},{3,2},{4,7},{5,4},{6,5},{7,6},{8,11},{9,8},{10,9... | collective-permute-start | bytes 1572872 | tf_op jit(solution)/shard_map/ppermute | solution.py:425
  43.4 1.9 %collective-permute-start.5 = (bf16[512,512]{1,0:T(8,128)(2,1)S(1)}, bf16[512,512]{1,0:T(8,128)(2,1)}, u32[]{:S(2)}, u32[]{:S(2)}) collective-permute-start(bf16[512,512]{1,0:T(8,128)(2,1)S(1)} %pad_maximum_fusion.refs_0_), channel_id=1, source_target_pairs={{0,1},{1,2},{2,3},{3,0},{4,5},{5,6},{6,7},{7,4},{8,9},{9,10},{10,1... | collective-permute-start | bytes 1572872 | tf_op jit(solution)/shard_map/ppermute | solution.py:425
  45.6 3.8 %collective-permute-done.4.refs_2_ = bf16[512,512]{1,0:T(8,128)(2,1)S(1)} collective-permute-done((bf16[512,512]{1,0:T(8,128)(2,1)S(1)}, bf16[512,512]{1,0:T(8,128)(2,1)S(1)}, u32[]{:S(2)}, u32[]{:S(2)}) %collective-permute-start.4) | collective-permute-done | bytes 524320 | tf_op jit(solution)/shard_map/ppermute | solution.py:425
  49.4 4.8 %collective-permute-done.3.refs_1_ = bf16[512,512]{1,0:T(8,128)(2,1)S(1)} collective-permute-done((bf16[512,512]{1,0:T(8,128)(2,1)S(1)}, bf16[512,512]{1,0:T(8,128)(2,1)S(1)}, u32[]{:S(2)}, u32[]{:S(2)}) %collective-permute-start.3) | collective-permute-done | bytes 524320 | tf_op jit(solution)/shard_map/ppermute | solution.py:425
  54.2 6.1 %collective-permute-done.6.refs_2_ = bf16[512,512]{1,0:T(8,128)(2,1)} collective-permute-done((bf16[512,512]{1,0:T(8,128)(2,1)S(1)}, bf16[512,512]{1,0:T(8,128)(2,1)}, u32[]{:S(2)}, u32[]{:S(2)}) %collective-permute-start.6) | collective-permute-done | bytes 524320 | tf_op jit(solution)/shard_map/ppermute | solution.py:425
  60.3 4.5 %collective-permute-done.5.refs_1_ = bf16[512,512]{1,0:T(8,128)(2,1)} collective-permute-done((bf16[512,512]{1,0:T(8,128)(2,1)S(1)}, bf16[512,512]{1,0:T(8,128)(2,1)}, u32[]{:S(2)}, u32[]{:S(2)}) %collective-permute-start.5) | collective-permute-done | bytes 524320 | tf_op jit(solution)/shard_map/ppermute | solution.py:425
  67.0 3.1 %shard_map.111 = (bf16[2048,128]{1,0:T(8,128)(2,1)S(1)}, bf16[2048,128]{1,0:T(8,128)(2,1)S(1)}, bf16[128,2048]{1,0:T(8,128)(2,1)S(1)}, bf16[128,2048]{1,0:T(8,12...) custom-call(s32[3,16]{1,0:T(4,128)S(1)} %select_reduce_fusion.slot_ref, ...), custom_call_target="tpu_custom_call" | custom-call | tf_op jit(solution)/shard_map/pallas_call | solution.py:346
  70.1 2.4 %shard_map.113 = bf16[16,64,128]{2,1,0:T(8,128)(2,1)S(1)} custom-call(s32[3,16]{1,0:T(4,128)S(1)} %select_reduce_fusion.slot_ref, s32[4]{0:T(128)S(1)} %broadcast_subtract_fusion.start_ref, bf16[16,64,128]{2,1,0:T(8,128)(2,1)S(1)} %collective-permute-done.7.kv_ref, bf16[2048,128]{1,0:T(8,128)(2,1)S(1)} %get-tuple-element.36.refs_0_, ...), custom_call_target="tpu_custom_call" | custom-call | tf_op jit(solution)/shard_map/pallas_call | solution.py:346
  72.6 3.3 %collective-permute-start.8 = (bf16[16,64,128]{2,1,0:T(8,128)(2,1)S(1)}, bf16[16,64,128]{2,1,0:T(8,128)(2,1)S(1)}, u32[]{:S(2)}, u32[]{:S(2)}) collective-permute-start(bf16[16,64,128]{2,1,0:T(8,128)(2,1)S(1)} %shard_map.113), channel_id=1, source_target_pairs={{0,4},{4,0},{1,5},{5,1},{2,6},{6,2},{3,7},{7,3},{8,12},{12,8},{9,1... | collective-permute-start | bytes 786440 | tf_op jit(solution)/shard_map/ppermute | solution.py:469
  77.9 7.2 %all-to-all-start.1 = ((bf16[16,2,64,128]{3,2,1,0:T(8,128)(2,1)}), bf16[16,2,64,128]{3,2,1,0:T(8,128)(2,1)S(1)}, u32[]{:S(2)}, u32[]{:S(2)}) async-start(bf16[16,2,64,128]{3,2,1,0:T(8,128)(2,1)} %shard_map.114), calls=%async_computation.1 | async-start | bytes 1048576 | tf_op jit(solution)/shard_map/all_to_all | solution.py:483
  87.1 3.9 %collective-permute-start.9 = (bf16[512,512]{1,0:T(8,128)(2,1)}, bf16[512,512]{1,0:T(8,128)(2,1)S(1)}, u32[]{:S(2)}, u32[]{:S(2)}) collective-permute-start(bf16[512,512]{1,0:T(8,128)(2,1)} %copy-done.4), channel_id=1, source_target_pairs={{0,1},{1,2},{2,3},{3,0},{4,5},{5,6},{6,7},{7,4},{8,9},{9,10},{10,1... | collective-permute-start | bytes 1572872 | tf_op jit(solution)/shard_map/ppermute | solution.py:481
  91.1 10.1 %collective-permute-done.10.refs_3_ = bf16[512,512]{1,0:T(8,128)(2,1)S(1)} collective-permute-done((bf16[512,512]{1,0:T(8,128)(2,1)}, bf16[512,512]{1,0:T(8,128)(2,1)S(1)}, u32[]{:S(2)}, u32[]{:S(2)}) %collective-permute-start.10) | collective-permute-done | bytes 524320 | tf_op jit(solution)/shard_map/ppermute | solution.py:482
  101.2 3.1 %collective-permute-done.9.refs_3_ = bf16[512,512]{1,0:T(8,128)(2,1)S(1)} collective-permute-done((bf16[512,512]{1,0:T(8,128)(2,1)}, bf16[512,512]{1,0:T(8,128)(2,1)S(1)}, u32[]{:S(2)}, u32[]{:S(2)}) %collective-permute-start.9) | collective-permute-done | bytes 524320 | tf_op jit(solution)/shard_map/ppermute | solution.py:481
  105.0 2.8 %collective-permute-start.11 = (bf16[528,256]{1,0:T(8,128)(2,1)S(1)}, bf16[528,256]{1,0:T(8,128)(2,1)S(1)}, u32[]{:S(2)}, u32[]{:S(2)}) collective-permute-start(bf16[528,256]{1,0:T(8,128)(2,1)S(1)} %shard_map.115.refs_4_), channel_id=1, source_target_pairs={{0,64},{64,0},{1,65},{65,1},{2,66},{66,2},{3,67},{67,3},{4,68},{68... | collective-permute-start | bytes 811016 | tf_op jit(solution)/shard_map/ppermute | solution.py:492
  109.8 4.8 %collective-permute-done.11.refs_4_ = bf16[528,256]{1,0:T(8,128)(2,1)S(1)} collective-permute-done((bf16[528,256]{1,0:T(8,128)(2,1)S(1)}, bf16[528,256]{1,0:T(8,128)(2,1)S(1)}, u32[]{:S(2)}, u32[]{:S(2)}) %collective-permute-start.11) | collective-permute-done | bytes 270368 | tf_op jit(solution)/shard_map/ppermute | solution.py:492
  116.7 2.3 %shard_map.116.refs_6_ = f32[4,256,256]{2,1,0:T(8,128)S(1)} custom-call(bf16[512,512]{1,0:T(8,128)(2,1)} %copy-done.2, bf16[512,512]{1,0:T(8,128)(2,1)} %copy-done.4, bf16[512,512]{1,0:T(8,128)(2,1)} %copy-done.3, bf16[512,512]{1,0:T(8,128)(2,1)S(1)} %collective-permute-done.9.refs_3_, bf16[528,256]{1,0:T(8,128)(2,1)S(1)} %shard_map.115.refs_4_, ...), custom_call_target="tpu_custom_call" | custom-call | tf_op jit(solution)/shard_map/pallas_call | solution.py:346
  119.1 3.4 %shard_map.117 = bf16[8,8,16,256]{3,2,1,0:T(8,128)(2,1)S(1)} custom-call(s32[3]{0:T(128)S(1)} %pad_add_fusion.where_ref, bf16[512,512]{1,0:T(8,128)(2,1)} %copy-done.1, bf16[512,512]{1,0:T(8,128)(2,1)} %collective-permute-done.5.refs_1_, bf16[512,512]{1,0:T(8,128)(2,1)} %collective-permute-done.6.refs_2_, ...), custom_call_target="tpu_custom_call" | custom-call | tf_op jit(solution)/shard_map/pallas_call | solution.py:346
  122.5 36.1 %all_to_all.15 = bf16[64,16,256]{2,1,0:T(8,128)(2,1)S(1)} all-to-all(bf16[64,16,256]{2,1,0:T(8,128)(2,1)S(1)} %bitcast.18), channel_id=1, replica_groups=mesh['zh'=4,'zl'=2,'y'=8,'core'=2,'tensor'=4] {'zh','zl','y'}, dimensions={0} | all-to-all | bytes 1048576 | tf_op jit(solution)/shard_map/all_to_all | solution.py:523
  (53 shorter events, 18.2 us)
Async XLA Ops:
  2.8 9.6 %copy-start = (bf16[1,512,1024]{2,1,0:T(8,128)(2,1)S(1)}, bf16[1,512,1024]{2,1,0:T(8,128)(2,1)}, u32[]{:S(2)}) copy-start(bf16[1,512,1024]{2,1,0:T(8,128)(2,1)} %param.11) | copy-start | bytes 3145732
  2.8 62.0 %all-to-all-start = ((bf16[16,392,128]{2,1,0:T(8,128)(2,1)}), bf16[16,392,128]{2,1,0:T(8,128)(2,1)S(1)}, u32[]{:S(2)}, u32[]{:S(2)}) async-start(bf16[16,392,128]{2,1,0:T(8,128)(2,1)} %shard_map.109), calls=%async_computation | async-start | bytes 3211264 | tf_op jit(solution)/shard_map/all_to_all | solution.py:409
  12.3 18.8 %copy-start.6 = (s32[1,10]{1,0:T(1,128)S(1)}, s32[1,10]{1,0:T(1,128)}, u32[]{:S(2)}) copy-start(s32[1,10]{1,0:T(1,128)} %param.18) | copy-start | bytes 124
  12.3 19.6 %copy-start.5 = (s32[1,256]{1,0:T(1,128)S(1)}, s32[1,256]{1,0:T(1,128)}, u32[]{:S(2)}) copy-start(s32[1,256]{1,0:T(1,128)} %refs_7_.1) | copy-start | bytes 3076
  13.3 15.9 %collective-permute-start = (bf16[512,512]{1,0:T(8,128)(2,1)S(1)}, bf16[512,512]{1,0:T(8,128)(2,1)S(1)}, u32[]{:S(2)}, u32[]{:S(2)}) collective-permute-start(bf16[512,512]{1,0:T(8,128)(2,1)S(1)} %get-tuple-element.30), channel_id=1, source_target_pairs={{0,64},{64,0},{1,65},{65,1},{2,66},{66,2},{3,67},{67,3},{4,68},{68... | collective-permute-start | bytes 1572872 | tf_op jit(solution)/shard_map/ppermute | solution.py:418
  15.8 16.9 %collective-permute-start.2 = (bf16[256,512]{1,0:T(8,128)(2,1)S(1)}, bf16[256,512]{1,0:T(8,128)(2,1)S(1)}, u32[]{:S(2)}, u32[]{:S(2)}) collective-permute-start(bf16[256,512]{1,0:T(8,128)(2,1)S(1)} %get-tuple-element.33), channel_id=1, source_target_pairs={{0,4},{4,0},{1,5},{5,1},{2,6},{6,2},{3,7},{7,3},{8,12},{12,8},{9,1... | collective-permute-start | bytes 786440 | tf_op jit(solution)/shard_map/ppermute | solution.py:419
  29.2 9.4 %collective-permute-start.1 = (bf16[256,512]{1,0:T(8,128)(2,1)S(1)}, bf16[256,512]{1,0:T(8,128)(2,1)S(1)}, u32[]{:S(2)}, u32[]{:S(2)}) collective-permute-start(bf16[256,512]{1,0:T(8,128)(2,1)S(1)} %get-tuple-element.56), channel_id=1, source_target_pairs={{0,4},{4,0},{1,5},{5,1},{2,6},{6,2},{3,7},{7,3},{8,12},{12,8},{9,1... | collective-permute-start | bytes 786440 | tf_op jit(solution)/shard_map/ppermute | solution.py:420
  32.7 27.6 %copy-start.2 = (bf16[512,512]{1,0:T(8,128)(2,1)}, bf16[512,512]{1,0:T(8,128)(2,1)S(1)}, u32[]{:S(2)}) copy-start(bf16[512,512]{1,0:T(8,128)(2,1)S(1)} %constant_dynamic-update-slice_fusion.refs_0_) | copy-start | bytes 1572868
  32.7 16.6 %collective-permute-start.4 = (bf16[512,512]{1,0:T(8,128)(2,1)S(1)}, bf16[512,512]{1,0:T(8,128)(2,1)S(1)}, u32[]{:S(2)}, u32[]{:S(2)}) collective-permute-start(bf16[512,512]{1,0:T(8,128)(2,1)S(1)} %constant_dynamic-update-slice_fusion.refs_0_), channel_id=1, source_target_pairs={{0,3},{1,0},{2,1},{3,2},{4,7},{5,4},{6,5},{7,6},{8,11},{9,8},{10,9... | collective-permute-start | bytes 1572872 | tf_op jit(solution)/shard_map/ppermute | solution.py:425
  36.3 17.9 %collective-permute-start.3 = (bf16[512,512]{1,0:T(8,128)(2,1)S(1)}, bf16[512,512]{1,0:T(8,128)(2,1)S(1)}, u32[]{:S(2)}, u32[]{:S(2)}) collective-permute-start(bf16[512,512]{1,0:T(8,128)(2,1)S(1)} %constant_dynamic-update-slice_fusion.refs_0_), channel_id=1, source_target_pairs={{0,1},{1,2},{2,3},{3,0},{4,5},{5,6},{6,7},{7,4},{8,9},{9,10},{10,1... | collective-permute-start | bytes 1572872 | tf_op jit(solution)/shard_map/ppermute | solution.py:425
  38.7 21.7 %copy-start.1 = (bf16[512,512]{1,0:T(8,128)(2,1)}, bf16[512,512]{1,0:T(8,128)(2,1)S(1)}, u32[]{:S(2)}) copy-start(bf16[512,512]{1,0:T(8,128)(2,1)S(1)} %pad_maximum_fusion.refs_0_) | copy-start | bytes 1572868
  38.7 21.6 %collective-permute-start.6 = (bf16[512,512]{1,0:T(8,128)(2,1)S(1)}, bf16[512,512]{1,0:T(8,128)(2,1)}, u32[]{:S(2)}, u32[]{:S(2)}) collective-permute-start(bf16[512,512]{1,0:T(8,128)(2,1)S(1)} %pad_maximum_fusion.refs_0_), channel_id=1, source_target_pairs={{0,3},{1,0},{2,1},{3,2},{4,7},{5,4},{6,5},{7,6},{8,11},{9,8},{10,9... | collective-permute-start | bytes 1572872 | tf_op jit(solution)/shard_map/ppermute | solution.py:425
  43.4 21.4 %collective-permute-start.5 = (bf16[512,512]{1,0:T(8,128)(2,1)S(1)}, bf16[512,512]{1,0:T(8,128)(2,1)}, u32[]{:S(2)}, u32[]{:S(2)}) collective-permute-start(bf16[512,512]{1,0:T(8,128)(2,1)S(1)} %pad_maximum_fusion.refs_0_), channel_id=1, source_target_pairs={{0,1},{1,2},{2,3},{3,0},{4,5},{5,6},{6,7},{7,4},{8,9},{9,10},{10,1... | collective-permute-start | bytes 1572872 | tf_op jit(solution)/shard_map/ppermute | solution.py:425
  49.4 11.0 %copy-start.3 = (bf16[512,512]{1,0:T(8,128)(2,1)}, bf16[512,512]{1,0:T(8,128)(2,1)S(1)}, u32[]{:S(2)}) copy-start(bf16[512,512]{1,0:T(8,128)(2,1)S(1)} %collective-permute-done.4.refs_2_) | copy-start | bytes 1572868
  54.2 6.2 %copy-start.4 = (bf16[512,512]{1,0:T(8,128)(2,1)}, bf16[512,512]{1,0:T(8,128)(2,1)S(1)}, u32[]{:S(2)}) copy-start(bf16[512,512]{1,0:T(8,128)(2,1)S(1)} %collective-permute-done.3.refs_1_) | copy-start | bytes 1572868
  64.8 5.3 %collective-permute-start.7 = (bf16[16,64,128]{2,1,0:T(8,128)(2,1)S(1)}, bf16[16,64,128]{2,1,0:T(8,128)(2,1)S(1)}, u32[]{:S(2)}, u32[]{:S(2)}) collective-permute-start(bf16[16,64,128]{2,1,0:T(8,128)(2,1)S(1)} %get-tuple-element.53), channel_id=1, source_target_pairs={{0,4},{4,0},{1,5},{5,1},{2,6},{6,2},{3,7},{7,3},{8,12},{12,8},{9,1... | collective-permute-start | bytes 786440 | tf_op jit(solution)/shard_map/ppermute | solution.py:443
  72.6 4.4 %collective-permute-start.8 = (bf16[16,64,128]{2,1,0:T(8,128)(2,1)S(1)}, bf16[16,64,128]{2,1,0:T(8,128)(2,1)S(1)}, u32[]{:S(2)}, u32[]{:S(2)}) collective-permute-start(bf16[16,64,128]{2,1,0:T(8,128)(2,1)S(1)} %shard_map.113), channel_id=1, source_target_pairs={{0,4},{4,0},{1,5},{5,1},{2,6},{6,2},{3,7},{7,3},{8,12},{12,8},{9,1... | collective-permute-start | bytes 786440 | tf_op jit(solution)/shard_map/ppermute | solution.py:469
  77.9 26.5 %all-to-all-start.1 = ((bf16[16,2,64,128]{3,2,1,0:T(8,128)(2,1)}), bf16[16,2,64,128]{3,2,1,0:T(8,128)(2,1)S(1)}, u32[]{:S(2)}, u32[]{:S(2)}) async-start(bf16[16,2,64,128]{3,2,1,0:T(8,128)(2,1)} %shard_map.114), calls=%async_computation.1 | async-start | bytes 1048576 | tf_op jit(solution)/shard_map/all_to_all | solution.py:483
  85.2 16.1 %collective-permute-start.10 = (bf16[512,512]{1,0:T(8,128)(2,1)}, bf16[512,512]{1,0:T(8,128)(2,1)S(1)}, u32[]{:S(2)}, u32[]{:S(2)}) collective-permute-start(bf16[512,512]{1,0:T(8,128)(2,1)} %collective-permute-done.6.refs_2_), channel_id=1, source_target_pairs={{0,3},{1,0},{2,1},{3,2},{4,7},{5,4},{6,5},{7,6},{8,11},{9,8},{10,9... | collective-permute-start | bytes 1572872 | tf_op jit(solution)/shard_map/ppermute | solution.py:482
  87.1 17.3 %collective-permute-start.9 = (bf16[512,512]{1,0:T(8,128)(2,1)}, bf16[512,512]{1,0:T(8,128)(2,1)S(1)}, u32[]{:S(2)}, u32[]{:S(2)}) collective-permute-start(bf16[512,512]{1,0:T(8,128)(2,1)} %copy-done.4), channel_id=1, source_target_pairs={{0,1},{1,2},{2,3},{3,0},{4,5},{5,6},{6,7},{7,4},{8,9},{9,10},{10,1... | collective-permute-start | bytes 1572872 | tf_op jit(solution)/shard_map/ppermute | solution.py:481
  105.0 9.6 %collective-permute-start.11 = (bf16[528,256]{1,0:T(8,128)(2,1)S(1)}, bf16[528,256]{1,0:T(8,128)(2,1)S(1)}, u32[]{:S(2)}, u32[]{:S(2)}) collective-permute-start(bf16[528,256]{1,0:T(8,128)(2,1)S(1)} %shard_map.115.refs_4_), channel_id=1, source_target_pairs={{0,64},{64,0},{1,65},{65,1},{2,66},{66,2},{3,67},{67,3},{4,68},{68... | collective-permute-start | bytes 811016 | tf_op jit(solution)/shard_map/ppermute | solution.py:492
  107.9 8.8 %collective-permute-start.13 = (bf16[528,256]{1,0:T(8,128)(2,1)S(1)}, bf16[528,256]{1,0:T(8,128)(2,1)S(1)}, u32[]{:S(2)}, u32[]{:S(2)}) collective-permute-start(bf16[528,256]{1,0:T(8,128)(2,1)S(1)} %shard_map.115.refs_4_), channel_id=1, source_target_pairs={{0,4},{4,0},{1,5},{5,1},{2,6},{6,2},{3,7},{7,3},{8,12},{12,8},{9,1... | collective-permute-start | bytes 811016 | tf_op jit(solution)/shard_map/ppermute | solution.py:493
  114.6 4.4 %collective-permute-start.12 = (bf16[528,256]{1,0:T(8,128)(2,1)S(1)}, bf16[528,256]{1,0:T(8,128)(2,1)S(1)}, u32[]{:S(2)}, u32[]{:S(2)}) collective-permute-start(bf16[528,256]{1,0:T(8,128)(2,1)S(1)} %collective-permute-done.11.refs_4_), channel_id=1, source_target_pairs={{0,4},{4,0},{1,5},{5,1},{2,6},{6,2},{3,7},{7,3},{8,12},{12,8},{9,1... | collective-permute-start | bytes 811016 | tf_op jit(solution)/shard_map/ppermute | solution.py:506

commit v8 on v6

--- a/solution.py
+++ b/solution.py
@@ -107,17 +107,21 @@
         store.wait()
 
 
-def block_grads(key_blk, value_blk, query_refs, cols, lse, dots, live):
+def block_grads(key_blk, value_blk, query_refs, cols, lse, dots, inside, causal=None):
     query_ref, grad_ref, query_turned, grad_turned = query_refs
     scores = jnp.dot(key_blk, query_turned[:, cols], preferred_element_type=jnp.float32)
     dprobs = jnp.dot(value_blk, grad_turned[:, cols], preferred_element_type=jnp.float32)
-    probs = jnp.where(live, jnp.exp2(scores * (HD ** (-0.5) * LOG2E) - lse), 0.0)
+    probs = jnp.exp2(scores * (HD ** (-0.5) * LOG2E) - lse)
+    if causal is not None:
+        before = probs.shape[0] - causal.shape[0]
+        diagonal = jnp.where(causal, probs[before:], 0.0)
+        probs = jnp.concatenate([probs[:before], diagonal], axis=0) if before else diagonal
     dscores = (probs * (dprobs - dots)).astype(jnp.bfloat16)
     value_part = jnp.dot(
         probs.astype(jnp.bfloat16), grad_ref[cols, :], preferred_element_type=jnp.float32
     )
     key_part = jnp.dot(dscores, query_ref[cols, :], preferred_element_type=jnp.float32)
-    return key_part, value_part
+    return jnp.where(inside, key_part, 0.0), jnp.where(inside, value_part, 0.0)
 
 
 def unit_stats(stat_ref, unit):
@@ -163,17 +167,17 @@
     queries = (query_ref, grad_ref, query_turned, grad_turned)
     dkey_scr[...] = jnp.zeros_like(dkey_scr)
     dvalue_scr[...] = jnp.zeros_like(dvalue_scr)
+    key_at = lax.broadcasted_iota(jnp.int32, (PAD, width), 0)
+    column = lax.broadcasted_iota(jnp.int32, (PAD, width), 1)
+    causal = key_at <= (column // QROWS) * BLK + column % BLK
     for unit in range(units):
         rows = slice(0, (unit + 1) * PAD)
         cols = slice(unit * width, (unit + 1) * width)
         lse, dots = unit_stats(stat_ref, unit)
-        key_at = lax.broadcasted_iota(jnp.int32, (rows.stop, width), 0)
-        column = lax.broadcasted_iota(jnp.int32, (rows.stop, width), 1)
-        query_at = unit * PAD + (column // QROWS) * BLK + column % BLK
         first = (start_ref[unit] - (SPAN - 1) * units) * PAD
-        live = (key_at <= query_at) & (key_at >= first)
+        inside = lax.broadcasted_iota(jnp.int32, (rows.stop, HD), 0) >= first
         key_part, value_part = block_grads(
-            key_scr[rows, :], value_scr[rows, :], queries, cols, lse, dots, live
+            key_scr[rows, :], value_scr[rows, :], queries, cols, lse, dots, inside, causal
         )
         dkey_scr[rows, :] += key_part
         dvalue_scr[rows, :] += value_part
@@ -192,7 +196,7 @@
         value_scr[rows, :] = kv_ref[src, BLK : 2 * BLK, :]
     dkey_scr[...] = jnp.zeros_like(dkey_scr)
     dvalue_scr[...] = jnp.zeros_like(dvalue_scr)
-    key_at = lax.broadcasted_iota(jnp.int32, (pair, width), 0)
+    key_at = lax.broadcasted_iota(jnp.int32, (pair, HD), 0)
     for unit in range(units):
         cols = slice(unit * width, (unit + 1) * width)
         lse, dots = unit_stats(stat_ref, unit)

time: 137 us -> 137 us (level)
  no operation moved by 1% of the time
where the time goes in v8:
time: 137 us; the launch traced here: 136 us
  starting transfers between devices  45.6 us (33%)
  blocking collectives  42.6 us (31%)
  waiting for transfers between devices  28.7 us (21%)
  Pallas kernels  15.4 us (11%)
  other arithmetic  2.27 us (2%)
  local copies, waits for them, and re-layouts  1.49 us (1%)
    all_to_all x1, blocking collectives, per_device(): lax.all_to_all(spread, ('dp', 'y'), split_axis=0, concat_axis=0, tiled=True)  42.6 us
    pallas_call x9, Pallas kernels, call(): pl.pallas_call(kernel, out_shape=out_shape, grid_spec=pltpu.PrefetchScala...  15.4 us
    ppermute x4, starting transfers between devices, per_device(): lax.ppermute(array, 'tensor', way)  14.1 us
    ppermute x4, waiting for transfers between devices, per_device(): lax.ppermute(array, 'tensor', way)  13 us
    all_to_all x1, waiting for transfers between devices, per_device(): lax.all_to_all(partial_grads, context, split_axis=0, concat_axis=0, tiled...  9.82 us
    all_to_all x1, starting transfers between devices, per_device(): lax.all_to_all(packed, context, split_axis=0, concat_axis=0, tiled=True)  7.35 us
    all_to_all x1, starting transfers between devices, per_device(): lax.all_to_all(partial_grads, context, split_axis=0, concat_axis=0, tiled...  5.71 us
    all_to_all x1, waiting for transfers between devices, per_device(): lax.all_to_all(packed, context, split_axis=0, concat_axis=0, tiled=True)  5.46 us
  transfers between devices with their start and end apart: 12, of which 7 were waited for; matrix products, arithmetic and copies ran while one was open for 2% of the time, Pallas kernels for 6%

profile of v8, /device:TPU:6, one launch (start us, length us, event | category | flops | bytes accessed | tf_op | source)
XLA Modules:
  0.0 136.4 jit_solution(7657160012155757174)
XLA Ops:
  0.0 2.8 %shard_map.109 = bf16[16,392,128]{2,1,0:T(8,128)(2,1)} custom-call(s32[1]{0:T(128)} %bitcast.2.where_ref, bf16[1,4,512,128]{3,2,1,0:T(8,128)(2,1)} %refs_0_.1, bf16[1,4,512,128]{3,2,1,0:T(8,128)(2,1)} %refs_1_.1, bf16[1,1,512,128]{3,2,1,0:T(8,128)(2,1)} %refs_2_.1, bf16[1,1,512,128]{3,2,1,0:T(8,128)(2,1)} %refs_3_.1, bf16[1,4,512]{2,1,0:T(4,128)(2,1)} %refs_4_.1, ...), custom_call_target="tpu_custom_call" | custom-call | tf_op jit(solution)/shard_map/pallas_call | solution.py:326
  2.8 7.3 %all-to-all-start = ((bf16[16,392,128]{2,1,0:T(8,128)(2,1)}), bf16[16,392,128]{2,1,0:T(8,128)(2,1)S(1)}, u32[]{:S(2)}, u32[]{:S(2)}) async-start(bf16[16,392,128]{2,1,0:T(8,128)(2,1)} %shard_map.109), calls=%async_computation | async-start | bytes 3211264 | tf_op jit(solution)/shard_map/all_to_all | solution.py:388
  10.2 1.1 shard_map.110
  11.3 2.3 %collective-permute-start = (bf16[512,512]{1,0:T(8,128)(2,1)}, bf16[512,512]{1,0:T(8,128)(2,1)S(1)}, u32[]{:S(2)}, u32[]{:S(2)}) collective-permute-start(bf16[512,512]{1,0:T(8,128)(2,1)} %get-tuple-element.26), channel_id=1, source_target_pairs={{0,4},{4,0},{1,5},{5,1},{2,6},{6,2},{3,7},{7,3},{8,12},{12,8},{9,1... | collective-permute-start | bytes 1572872 | tf_op jit(solution)/shard_map/ppermute | solution.py:396
  13.6 2.7 %collective-permute-start.2 = (bf16[512,512]{1,0:T(8,128)(2,1)S(1)}, bf16[512,512]{1,0:T(8,128)(2,1)S(1)}, u32[]{:S(2)}, u32[]{:S(2)}) collective-permute-start(bf16[512,512]{1,0:T(8,128)(2,1)S(1)} %get-tuple-element.28.refs_0_), channel_id=1, source_target_pairs={{0,3},{1,0},{2,1},{3,2},{4,7},{5,4},{6,5},{7,6},{8,11},{9,8},{10,9... | collective-permute-start | bytes 1572872 | tf_op jit(solution)/shard_map/ppermute | solution.py:400
  16.4 4.3 %collective-permute-start.1 = (bf16[512,512]{1,0:T(8,128)(2,1)S(1)}, bf16[512,512]{1,0:T(8,128)(2,1)}, u32[]{:S(2)}, u32[]{:S(2)}) collective-permute-start(bf16[512,512]{1,0:T(8,128)(2,1)S(1)} %get-tuple-element.28.refs_0_), channel_id=1, source_target_pairs={{0,1},{1,2},{2,3},{3,0},{4,5},{5,6},{6,7},{7,4},{8,9},{9,10},{10,1... | collective-permute-start | bytes 1572872 | tf_op jit(solution)/shard_map/ppermute | solution.py:400
  22.2 1.9 %collective-permute-start.4 = (bf16[512,512]{1,0:T(8,128)(2,1)S(1)}, bf16[512,512]{1,0:T(8,128)(2,1)S(1)}, u32[]{:S(2)}, u32[]{:S(2)}) collective-permute-start(bf16[512,512]{1,0:T(8,128)(2,1)S(1)} %collective-permute-done.refs_0_), channel_id=1, source_target_pairs={{0,3},{1,0},{2,1},{3,2},{4,7},{5,4},{6,5},{7,6},{8,11},{9,8},{10,9... | collective-permute-start | bytes 1572872 | tf_op jit(solution)/shard_map/ppermute | solution.py:400
  24.1 5.1 %collective-permute-start.3 = (bf16[512,512]{1,0:T(8,128)(2,1)S(1)}, bf16[512,512]{1,0:T(8,128)(2,1)}, u32[]{:S(2)}, u32[]{:S(2)}) collective-permute-start(bf16[512,512]{1,0:T(8,128)(2,1)S(1)} %collective-permute-done.refs_0_), channel_id=1, source_target_pairs={{0,1},{1,2},{2,3},{3,0},{4,5},{5,6},{6,7},{7,4},{8,9},{9,10},{10,1... | collective-permute-start | bytes 1572872 | tf_op jit(solution)/shard_map/ppermute | solution.py:400
  29.5 2.0 %collective-permute-done.2.refs_2_ = bf16[512,512]{1,0:T(8,128)(2,1)S(1)} collective-permute-done((bf16[512,512]{1,0:T(8,128)(2,1)S(1)}, bf16[512,512]{1,0:T(8,128)(2,1)S(1)}, u32[]{:S(2)}, u32[]{:S(2)}) %collective-permute-start.2) | collective-permute-done | bytes 524320 | tf_op jit(solution)/shard_map/ppermute | solution.py:400
  31.5 1.7 %collective-permute-done.1.refs_1_ = bf16[512,512]{1,0:T(8,128)(2,1)} collective-permute-done((bf16[512,512]{1,0:T(8,128)(2,1)S(1)}, bf16[512,512]{1,0:T(8,128)(2,1)}, u32[]{:S(2)}, u32[]{:S(2)}) %collective-permute-start.1) | collective-permute-done | bytes 524320 | tf_op jit(solution)/shard_map/ppermute | solution.py:400
  33.2 8.7 %collective-permute-done.4.refs_2_ = bf16[512,512]{1,0:T(8,128)(2,1)S(1)} collective-permute-done((bf16[512,512]{1,0:T(8,128)(2,1)S(1)}, bf16[512,512]{1,0:T(8,128)(2,1)S(1)}, u32[]{:S(2)}, u32[]{:S(2)}) %collective-permute-start.4) | collective-permute-done | bytes 524320 | tf_op jit(solution)/shard_map/ppermute | solution.py:400
  43.3 5.5 %all-to-all-done.recv_ref = bf16[16,392,128]{2,1,0:T(8,128)(2,1)S(1)} async-done(((bf16[16,392,128]{2,1,0:T(8,128)(2,1)}), bf16[16,392,128]{2,1,0:T(8,128)(2,1)S(1)}, u32[]{:S(2)}, u32[]{:S(2)}) %all-to-all-start) | async-done | bytes 1605664 | tf_op jit(solution)/shard_map/all_to_all | solution.py:388
  48.8 2.9 %collective-permute-start.5 = (bf16[16,64,128]{2,1,0:T(8,128)(2,1)S(1)}, bf16[16,64,128]{2,1,0:T(8,128)(2,1)S(1)}, u32[]{:S(2)}, u32[]{:S(2)}) collective-permute-start(bf16[16,64,128]{2,1,0:T(8,128)(2,1)S(1)} %get-tuple-element.45), channel_id=1, source_target_pairs={{0,4},{4,0},{1,5},{5,1},{2,6},{6,2},{3,7},{7,3},{8,12},{12,8},{9,1... | collective-permute-start | bytes 786440 | tf_op jit(solution)/shard_map/ppermute | solution.py:418
  51.9 2.7 %shard_map.111 = (bf16[2048,128]{1,0:T(8,128)(2,1)S(1)}, bf16[2048,128]{1,0:T(8,128)(2,1)S(1)}, bf16[128,2048]{1,0:T(8,128)(2,1)S(1)}, bf16[128,2048]{1,0:T(8,12...) custom-call(s32[3,16]{1,0:T(4,128)S(1)} %select_reduce_fusion.slot_ref, ...), custom_call_target="tpu_custom_call" | custom-call | tf_op jit(solution)/shard_map/pallas_call | solution.py:326
  55.4 3.6 %collective-permute-start.6 = (bf16[16,64,128]{2,1,0:T(8,128)(2,1)S(1)}, bf16[16,64,128]{2,1,0:T(8,128)(2,1)S(1)}, u32[]{:S(2)}, u32[]{:S(2)}) collective-permute-start(bf16[16,64,128]{2,1,0:T(8,128)(2,1)S(1)} %shard_map.113), channel_id=1, source_target_pairs={{0,4},{4,0},{1,5},{5,1},{2,6},{6,2},{3,7},{7,3},{8,12},{12,8},{9,1... | collective-permute-start | bytes 786440 | tf_op jit(solution)/shard_map/ppermute | solution.py:444
  60.1 0.9 shard_map.114
  61.0 5.7 %all-to-all-start.1 = ((bf16[16,2,64,128]{3,2,1,0:T(8,128)(2,1)}), bf16[16,2,64,128]{3,2,1,0:T(8,128)(2,1)S(1)}, u32[]{:S(2)}, u32[]{:S(2)}) async-start(bf16[16,2,64,128]{3,2,1,0:T(8,128)(2,1)} %shard_map.114), calls=%async_computation.1 | async-start | bytes 1048576 | tf_op jit(solution)/shard_map/all_to_all | solution.py:458
  66.8 4.2 %collective-permute-start.8 = (bf16[512,512]{1,0:T(8,128)(2,1)}, bf16[512,512]{1,0:T(8,128)(2,1)S(1)}, u32[]{:S(2)}, u32[]{:S(2)}) collective-permute-start(bf16[512,512]{1,0:T(8,128)(2,1)} %collective-permute-done.1.refs_1_), channel_id=1, source_target_pairs={{0,1},{1,2},{2,3},{3,0},{4,5},{5,6},{6,7},{7,4},{8,9},{9,10},{10,1... | collective-permute-start | bytes 1572872 | tf_op jit(solution)/shard_map/ppermute | solution.py:456
  70.9 1.9 %collective-permute-start.7 = (bf16[512,512]{1,0:T(8,128)(2,1)}, bf16[512,512]{1,0:T(8,128)(2,1)S(1)}, u32[]{:S(2)}, u32[]{:S(2)}) collective-permute-start(bf16[512,512]{1,0:T(8,128)(2,1)} %copy-done.4), channel_id=1, source_target_pairs={{0,3},{1,0},{2,1},{3,2},{4,7},{5,4},{6,5},{7,6},{8,11},{9,8},{10,9... | collective-permute-start | bytes 1572872 | tf_op jit(solution)/shard_map/ppermute | solution.py:457
  73.0 9.8 %all-to-all-done.1.recv_ref = bf16[16,2,64,128]{3,2,1,0:T(8,128)(2,1)S(1)} async-done(((bf16[16,2,64,128]{3,2,1,0:T(8,128)(2,1)}), bf16[16,2,64,128]{3,2,1,0:T(8,128)(2,1)S(1)}, u32[]{:S(2)}, u32[]{:S(2)}) %all-to-all-start.1) | async-done | bytes 524320 | tf_op jit(solution)/shard_map/all_to_all | solution.py:458
  83.4 3.6 %collective-permute-start.9 = (bf16[512,256]{1,0:T(8,128)(2,1)S(1)}, bf16[512,256]{1,0:T(8,128)(2,1)S(1)}, u32[]{:S(2)}, u32[]{:S(2)}) collective-permute-start(bf16[512,256]{1,0:T(8,128)(2,1)S(1)} %shard_map.115.refs_4_), channel_id=1, source_target_pairs={{0,4},{4,0},{1,5},{5,1},{2,6},{6,2},{3,7},{7,3},{8,12},{12,8},{9,1... | collective-permute-start | bytes 786440 | tf_op jit(solution)/shard_map/ppermute | solution.py:463
  87.2 2.3 %shard_map.116.refs_4_ = f32[4,512,256]{2,1,0:T(8,128)S(1)} custom-call(bf16[512,512]{1,0:T(8,128)(2,1)} %copy-done.1, bf16[512,512]{1,0:T(8,128)(2,1)} %collective-permute-done.1.refs_1_, bf16[512,512]{1,0:T(8,128)(2,1)} %copy-done.3, bf16[512,512]{1,0:T(8,128)(2,1)S(1)} %collective-permute-done.8.refs_3_, bf16[512,256]{1,0:T(8,128)(2,1)S(1)} %shard_map.115.refs_4_), custom_call_target="tpu_custom_call" | custom-call | tf_op jit(solution)/shard_map/pallas_call | solution.py:326
  89.6 3.4 %shard_map.117 = bf16[8,8,2,16,256]{4,3,2,1,0:T(8,128)(2,1)S(1)} custom-call(s32[2]{0:T(128)S(1)} %pad_add_fusion.where_ref, bf16[512,512]{1,0:T(8,128)(2,1)} %copy-done.2, bf16[512,512]{1,0:T(8,128)(2,1)} %collective-permute-done.3.refs_1_, bf16[512,512]{1,0:T(8,128)(2,1)} %copy-done.4, bf16[512,512]{1,0:T(8,128)(2,1)S(1)} %collective-permute-done.7.refs_3_, ...), custom_call_target="tpu_custom_call" | custom-call | tf_op jit(solution)/shard_map/pallas_call | solution.py:326
  93.0 42.6 %all_to_all.15 = bf16[64,2,16,256]{3,2,1,0:T(8,128)(2,1)S(1)} all-to-all(bf16[64,2,16,256]{3,2,1,0:T(8,128)(2,1)S(1)} %bitcast.15), channel_id=1, replica_groups=mesh['dp'=8,'y'=8,'core'=2,'tensor'=4] {'dp','y'}, dimensions={0} | all-to-all | bytes 2097152 | tf_op jit(solution)/shard_map/all_to_all | solution.py:491
  (40 shorter events, 6.8 us)
Async XLA Ops:
  2.8 7.4 %copy-start = (bf16[1,512,1024]{2,1,0:T(8,128)(2,1)S(1)}, bf16[1,512,1024]{2,1,0:T(8,128)(2,1)}, u32[]{:S(2)}) copy-start(bf16[1,512,1024]{2,1,0:T(8,128)(2,1)} %param.11) | copy-start | bytes 3145732
  2.8 17.9 %copy-start.6 = (s32[1,10]{1,0:T(1,128)S(1)}, s32[1,10]{1,0:T(1,128)}, u32[]{:S(2)}) copy-start(s32[1,10]{1,0:T(1,128)} %param.18) | copy-start | bytes 124
  2.8 18.6 %copy-start.5 = (s32[1,256]{1,0:T(1,128)S(1)}, s32[1,256]{1,0:T(1,128)}, u32[]{:S(2)}) copy-start(s32[1,256]{1,0:T(1,128)} %refs_7_.1) | copy-start | bytes 3076
  2.8 45.9 %all-to-all-start = ((bf16[16,392,128]{2,1,0:T(8,128)(2,1)}), bf16[16,392,128]{2,1,0:T(8,128)(2,1)S(1)}, u32[]{:S(2)}, u32[]{:S(2)}) async-start(bf16[16,392,128]{2,1,0:T(8,128)(2,1)} %shard_map.109), calls=%async_computation | async-start | bytes 3211264 | tf_op jit(solution)/shard_map/all_to_all | solution.py:388
  11.3 44.1 %copy-start.1 = (bf16[512,512]{1,0:T(8,128)(2,1)}, bf16[512,512]{1,0:T(8,128)(2,1)S(1)}, u32[]{:S(2)}) copy-start(bf16[512,512]{1,0:T(8,128)(2,1)S(1)} %get-tuple-element.28.refs_0_) | copy-start | bytes 1572868
  11.3 10.9 %collective-permute-start = (bf16[512,512]{1,0:T(8,128)(2,1)}, bf16[512,512]{1,0:T(8,128)(2,1)S(1)}, u32[]{:S(2)}, u32[]{:S(2)}) collective-permute-start(bf16[512,512]{1,0:T(8,128)(2,1)} %get-tuple-element.26), channel_id=1, source_target_pairs={{0,4},{4,0},{1,5},{5,1},{2,6},{6,2},{3,7},{7,3},{8,12},{12,8},{9,1... | collective-permute-start | bytes 1572872 | tf_op jit(solution)/shard_map/ppermute | solution.py:396
  13.6 17.9 %collective-permute-start.2 = (bf16[512,512]{1,0:T(8,128)(2,1)S(1)}, bf16[512,512]{1,0:T(8,128)(2,1)S(1)}, u32[]{:S(2)}, u32[]{:S(2)}) collective-permute-start(bf16[512,512]{1,0:T(8,128)(2,1)S(1)} %get-tuple-element.28.refs_0_), channel_id=1, source_target_pairs={{0,3},{1,0},{2,1},{3,2},{4,7},{5,4},{6,5},{7,6},{8,11},{9,8},{10,9... | collective-permute-start | bytes 1572872 | tf_op jit(solution)/shard_map/ppermute | solution.py:400
  16.4 16.8 %collective-permute-start.1 = (bf16[512,512]{1,0:T(8,128)(2,1)S(1)}, bf16[512,512]{1,0:T(8,128)(2,1)}, u32[]{:S(2)}, u32[]{:S(2)}) collective-permute-start(bf16[512,512]{1,0:T(8,128)(2,1)S(1)} %get-tuple-element.28.refs_0_), channel_id=1, source_target_pairs={{0,1},{1,2},{2,3},{3,0},{4,5},{5,6},{6,7},{7,4},{8,9},{9,10},{10,1... | collective-permute-start | bytes 1572872 | tf_op jit(solution)/shard_map/ppermute | solution.py:400
  22.2 21.1 %copy-start.2 = (bf16[512,512]{1,0:T(8,128)(2,1)}, bf16[512,512]{1,0:T(8,128)(2,1)S(1)}, u32[]{:S(2)}) copy-start(bf16[512,512]{1,0:T(8,128)(2,1)S(1)} %collective-permute-done.refs_0_) | copy-start | bytes 1572868
  22.2 19.7 %collective-permute-start.4 = (bf16[512,512]{1,0:T(8,128)(2,1)S(1)}, bf16[512,512]{1,0:T(8,128)(2,1)S(1)}, u32[]{:S(2)}, u32[]{:S(2)}) collective-permute-start(bf16[512,512]{1,0:T(8,128)(2,1)S(1)} %collective-permute-done.refs_0_), channel_id=1, source_target_pairs={{0,3},{1,0},{2,1},{3,2},{4,7},{5,4},{6,5},{7,6},{8,11},{9,8},{10,9... | collective-permute-start | bytes 1572872 | tf_op jit(solution)/shard_map/ppermute | solution.py:400
  24.1 19.2 %collective-permute-start.3 = (bf16[512,512]{1,0:T(8,128)(2,1)S(1)}, bf16[512,512]{1,0:T(8,128)(2,1)}, u32[]{:S(2)}, u32[]{:S(2)}) collective-permute-start(bf16[512,512]{1,0:T(8,128)(2,1)S(1)} %collective-permute-done.refs_0_), channel_id=1, source_target_pairs={{0,1},{1,2},{2,3},{3,0},{4,5},{5,6},{6,7},{7,4},{8,9},{9,10},{10,1... | collective-permute-start | bytes 1572872 | tf_op jit(solution)/shard_map/ppermute | solution.py:400
  31.5 20.1 %copy-start.3 = (bf16[512,512]{1,0:T(8,128)(2,1)}, bf16[512,512]{1,0:T(8,128)(2,1)S(1)}, u32[]{:S(2)}) copy-start(bf16[512,512]{1,0:T(8,128)(2,1)S(1)} %collective-permute-done.2.refs_2_) | copy-start | bytes 1572868
  41.9 0.8 copy-start.4
  48.8 5.9 %collective-permute-start.5 = (bf16[16,64,128]{2,1,0:T(8,128)(2,1)S(1)}, bf16[16,64,128]{2,1,0:T(8,128)(2,1)S(1)}, u32[]{:S(2)}, u32[]{:S(2)}) collective-permute-start(bf16[16,64,128]{2,1,0:T(8,128)(2,1)S(1)} %get-tuple-element.45), channel_id=1, source_target_pairs={{0,4},{4,0},{1,5},{5,1},{2,6},{6,2},{3,7},{7,3},{8,12},{12,8},{9,1... | collective-permute-start | bytes 786440 | tf_op jit(solution)/shard_map/ppermute | solution.py:418
  55.4 4.7 %collective-permute-start.6 = (bf16[16,64,128]{2,1,0:T(8,128)(2,1)S(1)}, bf16[16,64,128]{2,1,0:T(8,128)(2,1)S(1)}, u32[]{:S(2)}, u32[]{:S(2)}) collective-permute-start(bf16[16,64,128]{2,1,0:T(8,128)(2,1)S(1)} %shard_map.113), channel_id=1, source_target_pairs={{0,4},{4,0},{1,5},{5,1},{2,6},{6,2},{3,7},{7,3},{8,12},{12,8},{9,1... | collective-permute-start | bytes 786440 | tf_op jit(solution)/shard_map/ppermute | solution.py:444
  61.0 21.7 %all-to-all-start.1 = ((bf16[16,2,64,128]{3,2,1,0:T(8,128)(2,1)}), bf16[16,2,64,128]{3,2,1,0:T(8,128)(2,1)S(1)}, u32[]{:S(2)}, u32[]{:S(2)}) async-start(bf16[16,2,64,128]{3,2,1,0:T(8,128)(2,1)} %shard_map.114), calls=%async_computation.1 | async-start | bytes 1048576 | tf_op jit(solution)/shard_map/all_to_all | solution.py:458
  66.8 20.5 %collective-permute-start.8 = (bf16[512,512]{1,0:T(8,128)(2,1)}, bf16[512,512]{1,0:T(8,128)(2,1)S(1)}, u32[]{:S(2)}, u32[]{:S(2)}) collective-permute-start(bf16[512,512]{1,0:T(8,128)(2,1)} %collective-permute-done.1.refs_1_), channel_id=1, source_target_pairs={{0,1},{1,2},{2,3},{3,0},{4,5},{5,6},{6,7},{7,4},{8,9},{9,10},{10,1... | collective-permute-start | bytes 1572872 | tf_op jit(solution)/shard_map/ppermute | solution.py:456
  70.9 18.6 %collective-permute-start.7 = (bf16[512,512]{1,0:T(8,128)(2,1)}, bf16[512,512]{1,0:T(8,128)(2,1)S(1)}, u32[]{:S(2)}, u32[]{:S(2)}) collective-permute-start(bf16[512,512]{1,0:T(8,128)(2,1)} %copy-done.4), channel_id=1, source_target_pairs={{0,3},{1,0},{2,1},{3,2},{4,7},{5,4},{6,5},{7,6},{8,11},{9,8},{10,9... | collective-permute-start | bytes 1572872 | tf_op jit(solution)/shard_map/ppermute | solution.py:457
  83.4 6.2 %collective-permute-start.9 = (bf16[512,256]{1,0:T(8,128)(2,1)S(1)}, bf16[512,256]{1,0:T(8,128)(2,1)S(1)}, u32[]{:S(2)}, u32[]{:S(2)}) collective-permute-start(bf16[512,256]{1,0:T(8,128)(2,1)S(1)} %shard_map.115.refs_4_), channel_id=1, source_target_pairs={{0,4},{4,0},{1,5},{5,1},{2,6},{6,2},{3,7},{7,3},{8,12},{12,8},{9,1... | collective-permute-start | bytes 786440 | tf_op jit(solution)/shard_map/ppermute | solution.py:463

commit v9 on v8

--- a/solution.py
+++ b/solution.py
@@ -165,12 +165,10 @@
         value_scr[rows, :] = recv_ref[src, KV_AT + BLK : KV_AT + 2 * BLK, :]
 
     queries = (query_ref, grad_ref, query_turned, grad_turned)
-    dkey_scr[...] = jnp.zeros_like(dkey_scr)
-    dvalue_scr[...] = jnp.zeros_like(dvalue_scr)
     key_at = lax.broadcasted_iota(jnp.int32, (PAD, width), 0)
     column = lax.broadcasted_iota(jnp.int32, (PAD, width), 1)
     causal = key_at <= (column // QROWS) * BLK + column % BLK
-    for unit in range(units):
+    for unit in reversed(range(units)):
         rows = slice(0, (unit + 1) * PAD)
         cols = slice(unit * width, (unit + 1) * width)
         lse, dots = unit_stats(stat_ref, unit)
@@ -179,8 +177,12 @@
         key_part, value_part = block_grads(
             key_scr[rows, :], value_scr[rows, :], queries, cols, lse, dots, inside, causal
         )
-        dkey_scr[rows, :] += key_part
-        dvalue_scr[rows, :] += value_part
+        if unit == units - 1:
+            dkey_scr[...] = key_part
+            dvalue_scr[...] = value_part
+        else:
+            dkey_scr[rows, :] += key_part
+            dvalue_scr[rows, :] += value_part
     store_slab(slot_ref, 0, dkey_scr, dvalue_scr, out_ref)
 
 

time: 137 us -> 137 us (level)
  no operation moved by 1% of the time
where the time goes in v9:
time: 137 us; the launch traced here: 136 us
  starting transfers between devices  46.5 us (34%)
  blocking collectives  41.6 us (30%)
  waiting for transfers between devices  28.7 us (21%)
  Pallas kernels  15.4 us (11%)
  other arithmetic  2.27 us (2%)
  local copies, waits for them, and re-layouts  1.49 us (1%)
    all_to_all x1, blocking collectives, per_device(): lax.all_to_all(spread, ('dp', 'y'), split_axis=0, concat_axis=0, tiled=True)  41.6 us
    pallas_call x9, Pallas kernels, call(): pl.pallas_call(kernel, out_shape=out_shape, grid_spec=pltpu.PrefetchScala...  15.4 us
    ppermute x4, starting transfers between devices, per_device(): lax.ppermute(array, 'tensor', way)  14.1 us
    ppermute x4, waiting for transfers between devices, per_device(): lax.ppermute(array, 'tensor', way)  13 us
    all_to_all x1, waiting for transfers between devices, per_device(): lax.all_to_all(partial_grads, context, split_axis=0, concat_axis=0, tiled...  9.82 us
    all_to_all x1, starting transfers between devices, per_device(): lax.all_to_all(packed, context, split_axis=0, concat_axis=0, tiled=True)  7.35 us
    all_to_all x1, starting transfers between devices, per_device(): lax.all_to_all(partial_grads, context, split_axis=0, concat_axis=0, tiled...  5.69 us
    all_to_all x1, waiting for transfers between devices, per_device(): lax.all_to_all(packed, context, split_axis=0, concat_axis=0, tiled=True)  5.46 us
  transfers between devices with their start and end apart: 12, of which 7 were waited for; matrix products, arithmetic and copies ran while one was open for 2% of the time, Pallas kernels for 6%

profile of v9, /device:TPU:6, one launch (start us, length us, event | category | flops | bytes accessed | tf_op | source)
XLA Modules:
  0.0 136.2 jit_solution(2915274771942435220)
XLA Ops:
  0.0 2.8 %shard_map.109 = bf16[16,392,128]{2,1,0:T(8,128)(2,1)} custom-call(s32[1]{0:T(128)} %bitcast.2.where_ref, bf16[1,4,512,128]{3,2,1,0:T(8,128)(2,1)} %refs_0_.1, bf16[1,4,512,128]{3,2,1,0:T(8,128)(2,1)} %refs_1_.1, bf16[1,1,512,128]{3,2,1,0:T(8,128)(2,1)} %refs_2_.1, bf16[1,1,512,128]{3,2,1,0:T(8,128)(2,1)} %refs_3_.1, bf16[1,4,512]{2,1,0:T(4,128)(2,1)} %refs_4_.1, ...), custom_call_target="tpu_custom_call" | custom-call | tf_op jit(solution)/shard_map/pallas_call | solution.py:328
  2.8 7.3 %all-to-all-start = ((bf16[16,392,128]{2,1,0:T(8,128)(2,1)}), bf16[16,392,128]{2,1,0:T(8,128)(2,1)S(1)}, u32[]{:S(2)}, u32[]{:S(2)}) async-start(bf16[16,392,128]{2,1,0:T(8,128)(2,1)} %shard_map.109), calls=%async_computation | async-start | bytes 3211264 | tf_op jit(solution)/shard_map/all_to_all | solution.py:390
  10.2 1.1 shard_map.110
  11.3 2.3 %collective-permute-start = (bf16[512,512]{1,0:T(8,128)(2,1)}, bf16[512,512]{1,0:T(8,128)(2,1)S(1)}, u32[]{:S(2)}, u32[]{:S(2)}) collective-permute-start(bf16[512,512]{1,0:T(8,128)(2,1)} %get-tuple-element.26), channel_id=1, source_target_pairs={{0,4},{4,0},{1,5},{5,1},{2,6},{6,2},{3,7},{7,3},{8,12},{12,8},{9,1... | collective-permute-start | bytes 1572872 | tf_op jit(solution)/shard_map/ppermute | solution.py:398
  13.6 2.7 %collective-permute-start.2 = (bf16[512,512]{1,0:T(8,128)(2,1)S(1)}, bf16[512,512]{1,0:T(8,128)(2,1)S(1)}, u32[]{:S(2)}, u32[]{:S(2)}) collective-permute-start(bf16[512,512]{1,0:T(8,128)(2,1)S(1)} %get-tuple-element.28.refs_0_), channel_id=1, source_target_pairs={{0,3},{1,0},{2,1},{3,2},{4,7},{5,4},{6,5},{7,6},{8,11},{9,8},{10,9... | collective-permute-start | bytes 1572872 | tf_op jit(solution)/shard_map/ppermute | solution.py:402
  16.4 4.3 %collective-permute-start.1 = (bf16[512,512]{1,0:T(8,128)(2,1)S(1)}, bf16[512,512]{1,0:T(8,128)(2,1)}, u32[]{:S(2)}, u32[]{:S(2)}) collective-permute-start(bf16[512,512]{1,0:T(8,128)(2,1)S(1)} %get-tuple-element.28.refs_0_), channel_id=1, source_target_pairs={{0,1},{1,2},{2,3},{3,0},{4,5},{5,6},{6,7},{7,4},{8,9},{9,10},{10,1... | collective-permute-start | bytes 1572872 | tf_op jit(solution)/shard_map/ppermute | solution.py:402
  22.2 1.9 %collective-permute-start.4 = (bf16[512,512]{1,0:T(8,128)(2,1)S(1)}, bf16[512,512]{1,0:T(8,128)(2,1)S(1)}, u32[]{:S(2)}, u32[]{:S(2)}) collective-permute-start(bf16[512,512]{1,0:T(8,128)(2,1)S(1)} %collective-permute-done.refs_0_), channel_id=1, source_target_pairs={{0,3},{1,0},{2,1},{3,2},{4,7},{5,4},{6,5},{7,6},{8,11},{9,8},{10,9... | collective-permute-start | bytes 1572872 | tf_op jit(solution)/shard_map/ppermute | solution.py:402
  24.1 5.1 %collective-permute-start.3 = (bf16[512,512]{1,0:T(8,128)(2,1)S(1)}, bf16[512,512]{1,0:T(8,128)(2,1)}, u32[]{:S(2)}, u32[]{:S(2)}) collective-permute-start(bf16[512,512]{1,0:T(8,128)(2,1)S(1)} %collective-permute-done.refs_0_), channel_id=1, source_target_pairs={{0,1},{1,2},{2,3},{3,0},{4,5},{5,6},{6,7},{7,4},{8,9},{9,10},{10,1... | collective-permute-start | bytes 1572872 | tf_op jit(solution)/shard_map/ppermute | solution.py:402
  29.5 2.0 %collective-permute-done.2.refs_2_ = bf16[512,512]{1,0:T(8,128)(2,1)S(1)} collective-permute-done((bf16[512,512]{1,0:T(8,128)(2,1)S(1)}, bf16[512,512]{1,0:T(8,128)(2,1)S(1)}, u32[]{:S(2)}, u32[]{:S(2)}) %collective-permute-start.2) | collective-permute-done | bytes 524320 | tf_op jit(solution)/shard_map/ppermute | solution.py:402
  31.5 1.7 %collective-permute-done.1.refs_1_ = bf16[512,512]{1,0:T(8,128)(2,1)} collective-permute-done((bf16[512,512]{1,0:T(8,128)(2,1)S(1)}, bf16[512,512]{1,0:T(8,128)(2,1)}, u32[]{:S(2)}, u32[]{:S(2)}) %collective-permute-start.1) | collective-permute-done | bytes 524320 | tf_op jit(solution)/shard_map/ppermute | solution.py:402
  33.2 8.7 %collective-permute-done.4.refs_2_ = bf16[512,512]{1,0:T(8,128)(2,1)S(1)} collective-permute-done((bf16[512,512]{1,0:T(8,128)(2,1)S(1)}, bf16[512,512]{1,0:T(8,128)(2,1)S(1)}, u32[]{:S(2)}, u32[]{:S(2)}) %collective-permute-start.4) | collective-permute-done | bytes 524320 | tf_op jit(solution)/shard_map/ppermute | solution.py:402
  43.3 5.5 %all-to-all-done.recv_ref = bf16[16,392,128]{2,1,0:T(8,128)(2,1)S(1)} async-done(((bf16[16,392,128]{2,1,0:T(8,128)(2,1)}), bf16[16,392,128]{2,1,0:T(8,128)(2,1)S(1)}, u32[]{:S(2)}, u32[]{:S(2)}) %all-to-all-start) | async-done | bytes 1605664 | tf_op jit(solution)/shard_map/all_to_all | solution.py:390
  48.8 2.9 %collective-permute-start.5 = (bf16[16,64,128]{2,1,0:T(8,128)(2,1)S(1)}, bf16[16,64,128]{2,1,0:T(8,128)(2,1)S(1)}, u32[]{:S(2)}, u32[]{:S(2)}) collective-permute-start(bf16[16,64,128]{2,1,0:T(8,128)(2,1)S(1)} %get-tuple-element.45), channel_id=1, source_target_pairs={{0,4},{4,0},{1,5},{5,1},{2,6},{6,2},{3,7},{7,3},{8,12},{12,8},{9,1... | collective-permute-start | bytes 786440 | tf_op jit(solution)/shard_map/ppermute | solution.py:420
  51.9 2.7 %shard_map.111 = (bf16[2048,128]{1,0:T(8,128)(2,1)S(1)}, bf16[2048,128]{1,0:T(8,128)(2,1)S(1)}, bf16[128,2048]{1,0:T(8,128)(2,1)S(1)}, bf16[128,2048]{1,0:T(8,12...) custom-call(s32[3,16]{1,0:T(4,128)S(1)} %select_reduce_fusion.slot_ref, ...), custom_call_target="tpu_custom_call" | custom-call | tf_op jit(solution)/shard_map/pallas_call | solution.py:328
  55.3 4.4 %collective-permute-start.6 = (bf16[16,64,128]{2,1,0:T(8,128)(2,1)S(1)}, bf16[16,64,128]{2,1,0:T(8,128)(2,1)S(1)}, u32[]{:S(2)}, u32[]{:S(2)}) collective-permute-start(bf16[16,64,128]{2,1,0:T(8,128)(2,1)S(1)} %shard_map.113), channel_id=1, source_target_pairs={{0,4},{4,0},{1,5},{5,1},{2,6},{6,2},{3,7},{7,3},{8,12},{12,8},{9,1... | collective-permute-start | bytes 786440 | tf_op jit(solution)/shard_map/ppermute | solution.py:446
  60.9 0.9 shard_map.114
  61.8 5.7 %all-to-all-start.1 = ((bf16[16,2,64,128]{3,2,1,0:T(8,128)(2,1)}), bf16[16,2,64,128]{3,2,1,0:T(8,128)(2,1)S(1)}, u32[]{:S(2)}, u32[]{:S(2)}) async-start(bf16[16,2,64,128]{3,2,1,0:T(8,128)(2,1)} %shard_map.114), calls=%async_computation.1 | async-start | bytes 1048576 | tf_op jit(solution)/shard_map/all_to_all | solution.py:460
  67.5 4.2 %collective-permute-start.8 = (bf16[512,512]{1,0:T(8,128)(2,1)}, bf16[512,512]{1,0:T(8,128)(2,1)S(1)}, u32[]{:S(2)}, u32[]{:S(2)}) collective-permute-start(bf16[512,512]{1,0:T(8,128)(2,1)} %collective-permute-done.1.refs_1_), channel_id=1, source_target_pairs={{0,1},{1,2},{2,3},{3,0},{4,5},{5,6},{6,7},{7,4},{8,9},{9,10},{10,1... | collective-permute-start | bytes 1572872 | tf_op jit(solution)/shard_map/ppermute | solution.py:458
  71.7 1.9 %collective-permute-start.7 = (bf16[512,512]{1,0:T(8,128)(2,1)}, bf16[512,512]{1,0:T(8,128)(2,1)S(1)}, u32[]{:S(2)}, u32[]{:S(2)}) collective-permute-start(bf16[512,512]{1,0:T(8,128)(2,1)} %copy-done.4), channel_id=1, source_target_pairs={{0,3},{1,0},{2,1},{3,2},{4,7},{5,4},{6,5},{7,6},{8,11},{9,8},{10,9... | collective-permute-start | bytes 1572872 | tf_op jit(solution)/shard_map/ppermute | solution.py:459
  73.7 9.8 %all-to-all-done.1.recv_ref = bf16[16,2,64,128]{3,2,1,0:T(8,128)(2,1)S(1)} async-done(((bf16[16,2,64,128]{3,2,1,0:T(8,128)(2,1)}), bf16[16,2,64,128]{3,2,1,0:T(8,128)(2,1)S(1)}, u32[]{:S(2)}, u32[]{:S(2)}) %all-to-all-start.1) | async-done | bytes 524320 | tf_op jit(solution)/shard_map/all_to_all | solution.py:460
  84.2 3.6 %collective-permute-start.9 = (bf16[512,256]{1,0:T(8,128)(2,1)S(1)}, bf16[512,256]{1,0:T(8,128)(2,1)S(1)}, u32[]{:S(2)}, u32[]{:S(2)}) collective-permute-start(bf16[512,256]{1,0:T(8,128)(2,1)S(1)} %shard_map.115.refs_4_), channel_id=1, source_target_pairs={{0,4},{4,0},{1,5},{5,1},{2,6},{6,2},{3,7},{7,3},{8,12},{12,8},{9,1... | collective-permute-start | bytes 786440 | tf_op jit(solution)/shard_map/ppermute | solution.py:465
  88.0 2.3 %shard_map.116.refs_4_ = f32[4,512,256]{2,1,0:T(8,128)S(1)} custom-call(bf16[512,512]{1,0:T(8,128)(2,1)} %copy-done.1, bf16[512,512]{1,0:T(8,128)(2,1)} %collective-permute-done.1.refs_1_, bf16[512,512]{1,0:T(8,128)(2,1)} %copy-done.3, bf16[512,512]{1,0:T(8,128)(2,1)S(1)} %collective-permute-done.8.refs_3_, bf16[512,256]{1,0:T(8,128)(2,1)S(1)} %shard_map.115.refs_4_), custom_call_target="tpu_custom_call" | custom-call | tf_op jit(solution)/shard_map/pallas_call | solution.py:328
  90.4 3.4 %shard_map.117 = bf16[8,8,2,16,256]{4,3,2,1,0:T(8,128)(2,1)S(1)} custom-call(s32[2]{0:T(128)S(1)} %pad_add_fusion.where_ref, bf16[512,512]{1,0:T(8,128)(2,1)} %copy-done.2, bf16[512,512]{1,0:T(8,128)(2,1)} %collective-permute-done.3.refs_1_, bf16[512,512]{1,0:T(8,128)(2,1)} %copy-done.4, bf16[512,512]{1,0:T(8,128)(2,1)S(1)} %collective-permute-done.7.refs_3_, ...), custom_call_target="tpu_custom_call" | custom-call | tf_op jit(solution)/shard_map/pallas_call | solution.py:328
  93.8 41.6 %all_to_all.15 = bf16[64,2,16,256]{3,2,1,0:T(8,128)(2,1)S(1)} all-to-all(bf16[64,2,16,256]{3,2,1,0:T(8,128)(2,1)S(1)} %bitcast.15), channel_id=1, replica_groups=mesh['dp'=8,'y'=8,'core'=2,'tensor'=4] {'dp','y'}, dimensions={0} | all-to-all | bytes 2097152 | tf_op jit(solution)/shard_map/all_to_all | solution.py:493
  (40 shorter events, 6.8 us)
Async XLA Ops:
  2.8 7.4 %copy-start = (bf16[1,512,1024]{2,1,0:T(8,128)(2,1)S(1)}, bf16[1,512,1024]{2,1,0:T(8,128)(2,1)}, u32[]{:S(2)}) copy-start(bf16[1,512,1024]{2,1,0:T(8,128)(2,1)} %param.11) | copy-start | bytes 3145732
  2.8 17.9 %copy-start.6 = (s32[1,10]{1,0:T(1,128)S(1)}, s32[1,10]{1,0:T(1,128)}, u32[]{:S(2)}) copy-start(s32[1,10]{1,0:T(1,128)} %param.18) | copy-start | bytes 124
  2.8 18.6 %copy-start.5 = (s32[1,256]{1,0:T(1,128)S(1)}, s32[1,256]{1,0:T(1,128)}, u32[]{:S(2)}) copy-start(s32[1,256]{1,0:T(1,128)} %refs_7_.1) | copy-start | bytes 3076
  2.8 45.9 %all-to-all-start = ((bf16[16,392,128]{2,1,0:T(8,128)(2,1)}), bf16[16,392,128]{2,1,0:T(8,128)(2,1)S(1)}, u32[]{:S(2)}, u32[]{:S(2)}) async-start(bf16[16,392,128]{2,1,0:T(8,128)(2,1)} %shard_map.109), calls=%async_computation | async-start | bytes 3211264 | tf_op jit(solution)/shard_map/all_to_all | solution.py:390
  11.3 44.0 %copy-start.1 = (bf16[512,512]{1,0:T(8,128)(2,1)}, bf16[512,512]{1,0:T(8,128)(2,1)S(1)}, u32[]{:S(2)}) copy-start(bf16[512,512]{1,0:T(8,128)(2,1)S(1)} %get-tuple-element.28.refs_0_) | copy-start | bytes 1572868
  11.3 10.9 %collective-permute-start = (bf16[512,512]{1,0:T(8,128)(2,1)}, bf16[512,512]{1,0:T(8,128)(2,1)S(1)}, u32[]{:S(2)}, u32[]{:S(2)}) collective-permute-start(bf16[512,512]{1,0:T(8,128)(2,1)} %get-tuple-element.26), channel_id=1, source_target_pairs={{0,4},{4,0},{1,5},{5,1},{2,6},{6,2},{3,7},{7,3},{8,12},{12,8},{9,1... | collective-permute-start | bytes 1572872 | tf_op jit(solution)/shard_map/ppermute | solution.py:398
  13.6 17.9 %collective-permute-start.2 = (bf16[512,512]{1,0:T(8,128)(2,1)S(1)}, bf16[512,512]{1,0:T(8,128)(2,1)S(1)}, u32[]{:S(2)}, u32[]{:S(2)}) collective-permute-start(bf16[512,512]{1,0:T(8,128)(2,1)S(1)} %get-tuple-element.28.refs_0_), channel_id=1, source_target_pairs={{0,3},{1,0},{2,1},{3,2},{4,7},{5,4},{6,5},{7,6},{8,11},{9,8},{10,9... | collective-permute-start | bytes 1572872 | tf_op jit(solution)/shard_map/ppermute | solution.py:402
  16.4 16.8 %collective-permute-start.1 = (bf16[512,512]{1,0:T(8,128)(2,1)S(1)}, bf16[512,512]{1,0:T(8,128)(2,1)}, u32[]{:S(2)}, u32[]{:S(2)}) collective-permute-start(bf16[512,512]{1,0:T(8,128)(2,1)S(1)} %get-tuple-element.28.refs_0_), channel_id=1, source_target_pairs={{0,1},{1,2},{2,3},{3,0},{4,5},{5,6},{6,7},{7,4},{8,9},{9,10},{10,1... | collective-permute-start | bytes 1572872 | tf_op jit(solution)/shard_map/ppermute | solution.py:402
  22.2 21.1 %copy-start.2 = (bf16[512,512]{1,0:T(8,128)(2,1)}, bf16[512,512]{1,0:T(8,128)(2,1)S(1)}, u32[]{:S(2)}) copy-start(bf16[512,512]{1,0:T(8,128)(2,1)S(1)} %collective-permute-done.refs_0_) | copy-start | bytes 1572868
  22.2 19.7 %collective-permute-start.4 = (bf16[512,512]{1,0:T(8,128)(2,1)S(1)}, bf16[512,512]{1,0:T(8,128)(2,1)S(1)}, u32[]{:S(2)}, u32[]{:S(2)}) collective-permute-start(bf16[512,512]{1,0:T(8,128)(2,1)S(1)} %collective-permute-done.refs_0_), channel_id=1, source_target_pairs={{0,3},{1,0},{2,1},{3,2},{4,7},{5,4},{6,5},{7,6},{8,11},{9,8},{10,9... | collective-permute-start | bytes 1572872 | tf_op jit(solution)/shard_map/ppermute | solution.py:402
  24.1 19.2 %collective-permute-start.3 = (bf16[512,512]{1,0:T(8,128)(2,1)S(1)}, bf16[512,512]{1,0:T(8,128)(2,1)}, u32[]{:S(2)}, u32[]{:S(2)}) collective-permute-start(bf16[512,512]{1,0:T(8,128)(2,1)S(1)} %collective-permute-done.refs_0_), channel_id=1, source_target_pairs={{0,1},{1,2},{2,3},{3,0},{4,5},{5,6},{6,7},{7,4},{8,9},{9,10},{10,1... | collective-permute-start | bytes 1572872 | tf_op jit(solution)/shard_map/ppermute | solution.py:402
  31.5 20.1 %copy-start.3 = (bf16[512,512]{1,0:T(8,128)(2,1)}, bf16[512,512]{1,0:T(8,128)(2,1)S(1)}, u32[]{:S(2)}) copy-start(bf16[512,512]{1,0:T(8,128)(2,1)S(1)} %collective-permute-done.2.refs_2_) | copy-start | bytes 1572868
  41.9 0.8 copy-start.4
  48.8 5.8 %collective-permute-start.5 = (bf16[16,64,128]{2,1,0:T(8,128)(2,1)S(1)}, bf16[16,64,128]{2,1,0:T(8,128)(2,1)S(1)}, u32[]{:S(2)}, u32[]{:S(2)}) collective-permute-start(bf16[16,64,128]{2,1,0:T(8,128)(2,1)S(1)} %get-tuple-element.45), channel_id=1, source_target_pairs={{0,4},{4,0},{1,5},{5,1},{2,6},{6,2},{3,7},{7,3},{8,12},{12,8},{9,1... | collective-permute-start | bytes 786440 | tf_op jit(solution)/shard_map/ppermute | solution.py:420
  55.3 5.6 %collective-permute-start.6 = (bf16[16,64,128]{2,1,0:T(8,128)(2,1)S(1)}, bf16[16,64,128]{2,1,0:T(8,128)(2,1)S(1)}, u32[]{:S(2)}, u32[]{:S(2)}) collective-permute-start(bf16[16,64,128]{2,1,0:T(8,128)(2,1)S(1)} %shard_map.113), channel_id=1, source_target_pairs={{0,4},{4,0},{1,5},{5,1},{2,6},{6,2},{3,7},{7,3},{8,12},{12,8},{9,1... | collective-permute-start | bytes 786440 | tf_op jit(solution)/shard_map/ppermute | solution.py:446
  61.8 21.7 %all-to-all-start.1 = ((bf16[16,2,64,128]{3,2,1,0:T(8,128)(2,1)}), bf16[16,2,64,128]{3,2,1,0:T(8,128)(2,1)S(1)}, u32[]{:S(2)}, u32[]{:S(2)}) async-start(bf16[16,2,64,128]{3,2,1,0:T(8,128)(2,1)} %shard_map.114), calls=%async_computation.1 | async-start | bytes 1048576 | tf_op jit(solution)/shard_map/all_to_all | solution.py:460
  67.5 20.5 %collective-permute-start.8 = (bf16[512,512]{1,0:T(8,128)(2,1)}, bf16[512,512]{1,0:T(8,128)(2,1)S(1)}, u32[]{:S(2)}, u32[]{:S(2)}) collective-permute-start(bf16[512,512]{1,0:T(8,128)(2,1)} %collective-permute-done.1.refs_1_), channel_id=1, source_target_pairs={{0,1},{1,2},{2,3},{3,0},{4,5},{5,6},{6,7},{7,4},{8,9},{9,10},{10,1... | collective-permute-start | bytes 1572872 | tf_op jit(solution)/shard_map/ppermute | solution.py:458
  71.7 18.6 %collective-permute-start.7 = (bf16[512,512]{1,0:T(8,128)(2,1)}, bf16[512,512]{1,0:T(8,128)(2,1)S(1)}, u32[]{:S(2)}, u32[]{:S(2)}) collective-permute-start(bf16[512,512]{1,0:T(8,128)(2,1)} %copy-done.4), channel_id=1, source_target_pairs={{0,3},{1,0},{2,1},{3,2},{4,7},{5,4},{6,5},{7,6},{8,11},{9,8},{10,9... | collective-permute-start | bytes 1572872 | tf_op jit(solution)/shard_map/ppermute | solution.py:459
  84.2 6.2 %collective-permute-start.9 = (bf16[512,256]{1,0:T(8,128)(2,1)S(1)}, bf16[512,256]{1,0:T(8,128)(2,1)S(1)}, u32[]{:S(2)}, u32[]{:S(2)}) collective-permute-start(bf16[512,256]{1,0:T(8,128)(2,1)S(1)} %shard_map.115.refs_4_), channel_id=1, source_target_pairs={{0,4},{4,0},{1,5},{5,1},{2,6},{6,2},{3,7},{7,3},{8,12},{12,8},{9,1... | collective-permute-start | bytes 786440 | tf_op jit(solution)/shard_map/ppermute | solution.py:465
